TPU v7x, 32 devices: a whole 2x2x4 slice. The times are simulated.
32 devices in a mesh: dp: 4 (over z), seq: 8 (over y, x, core).
Axes of the slice: x: 2, y: 2, z: 4, core: 2. Of those that a mesh axis runs over, the one named last changes fastest.
Arguments:
- layer_input: bfloat16 [4, 2048, 1024], P('dp', 'seq'), may hold values from -6 to 6
- w_qkv: bfloat16 [1024, 3072], replicated, may hold values from -8.75 to 8.75
- w_out: bfloat16 [1024, 1024], replicated, may hold values from -0.1875 to 0.1875
- w_proj: bfloat16 [16, 64, 256], replicated, may hold values from -35 to 35
- w_up: bfloat16 [1024, 4096], P('dp', 'seq'), may hold values from -0.1875 to 0.1875
- w_down: bfloat16 [1024, 4096], P('dp', 'seq'), may hold values from -0.09375 to 0.09375
Outputs:
- layer_output: bfloat16 [4, 2048, 1024], P('dp', 'seq')
All inputs are finite; a program needn't handle non-finite values.
Results may differ from a plain program's by a relative error of at most 0.025.
The roundings to bfloat16 on the way count: a program that leaves them out, or rounds other values in their place, can miss the bound.
Values may be sent and summed in bfloat16 or wider, within the bound.
No kernel may reach another device: no remote copies, remote signals or barrier semaphores. Data moves between devices by JAX's collectives and lax.ppermute only.
A program may use at most 128 MiB of HBM per device.

v0:
```python
import functools

import jax
import jax.numpy as jnp
from jax import lax
from jax.experimental import pallas as pl
from jax.experimental.pallas import tpu as pltpu
from jax.sharding import PartitionSpec as P


HS = 64
WBLK = 256
EPS = 1e-05
F32 = jnp.float32
BF = jnp.bfloat16
NT = (((1,), (1,)), ((), ()))
TT = (((0,), (1,)), ((), ()))
VMEM_LIMIT = 24 * 1024 * 1024
SMALL = 60.0


def dot(a, b):
    return jnp.dot(a, b, preferred_element_type=F32)


def layer_norm(x):
    center = x - jnp.mean(x, axis=-1, keepdims=True)
    spread = jnp.mean(center * center, axis=-1, keepdims=True)
    return center * lax.rsqrt(spread + EPS)


def head_average(width):
    a = lax.broadcasted_iota(jnp.int32, (width, width), 0) // HS
    b = lax.broadcasted_iota(jnp.int32, (width, width), 1) // HS
    return jnp.where(a == b, 1.0 / HS, 0.0).astype(F32)


def split(x):
    high = x.astype(BF)
    return high, (x - high.astype(F32)).astype(BF)


def head_norm(x):
    avg = head_average(x.shape[1]).astype(BF)
    center = x.astype(F32) - dot(x, avg)
    spread = dot((center * center).astype(BF), avg)
    return (center * lax.rsqrt(spread + EPS)).astype(BF)


def head_sum(x):
    square = x.astype(F32) * x.astype(F32)
    return dot(square.astype(BF), head_average(x.shape[1]).astype(BF)) * HS


def head_norm_wide(x):
    avg = head_average(x.shape[1]).astype(BF)

    def mean(y):
        one = y.astype(BF)
        rest = y - one.astype(F32)
        two, three = split(rest)
        return dot(one, avg) + dot(two, avg) + dot(three, avg)

    center = x - mean(x)
    spread = mean(center * center)
    return (center * lax.rsqrt(spread + EPS)).astype(BF)


def lanes(shape):
    return lax.broadcasted_iota(jnp.int32, shape, len(shape) - 1)


def diagonal(size):
    return lax.broadcasted_iota(jnp.int32, (size, size), 0) == lax.broadcasted_iota(
        jnp.int32, (size, size), 1
    )


def to_row(column):
    size = column.shape[0]
    return jnp.sum(jnp.where(diagonal(size), column, 0.0), axis=0, keepdims=True)


def to_column(row):
    size = row.shape[1]
    return jnp.sum(jnp.where(diagonal(size), row, 0.0), axis=1, keepdims=True)


def qkv_kernel(sizes, s_ref, tok_ref, par_ref, wq_ref, wk_ref, wv_ref, wp_ref, q_ref, nk_ref, nv_ref, top_ref, *rest):
    chips, owned, extra, steps, rank = sizes
    pays, (xn_ref, pay_ref, sem) = rest[:chips], rest[chips:]
    rows = tok_ref.shape[0]
    step = pl.program_id(0)

    @pl.when(step == 0)
    def _():
        xn_ref[:rows] = layer_norm(tok_ref[...].astype(F32)).astype(BF)
        xn_ref[rows:] = layer_norm(par_ref[...].astype(F32)).astype(BF)
        top_ref[...] = jnp.zeros_like(top_ref)

    x = xn_ref[...]
    kk = dot(x, wk_ref[...]).astype(BF)
    vv = dot(x, wv_ref[...]).astype(BF)
    width = kk.shape[1]
    heads = width // HS
    owners = heads * rank // owned
    stat_rows = owned // 128
    place = lax.broadcasted_iota(jnp.int32, (extra, 128), 0)

    def partial_sums(shifted):
        stats = [jnp.zeros((extra, 128), F32) for _ in range(owners)]
        for pair in range(heads // 2):
            kp = kk[:, pair * 128 : (pair + 1) * 128]
            vp = vv[:, pair * 128 : (pair + 1) * 128]
            turned = pltpu.roll(vp.astype(F32), 64, 1).astype(BF)
            low_half = lanes(kp.shape) < HS
            for side in range(2):
                head = pair * 2 + side
                mixed = jnp.where(low_half, kp, turned) if side == 0 else jnp.where(low_half, turned, kp)
                wp = wp_ref[head]
                none = jnp.zeros_like(wp)
                wide = jnp.concatenate([wp, none] if side == 0 else [none, wp], axis=0)
                logits = lax.dot_general(wide, kp, TT, preferred_element_type=F32)
                if shifted:
                    peak = jnp.max(logits, axis=1, keepdims=True)
                    logits = logits - peak
                weight = jnp.exp(logits).astype(BF)
                total = jnp.sum(weight.astype(F32), axis=1, keepdims=True)
                sums = dot(weight, mixed).astype(BF)
                for part in range(rank // 128):
                    column = head * rank + part * 128
                    owner, offset = column // owned, column % owned
                    cut = slice(part * 128, (part + 1) * 128)
                    pay_ref[step * owners + owner, offset : offset + 128, :] = sums[cut]
                    entries = [(3, to_row(total[cut]))]
                    if shifted:
                        one = to_row(peak[cut])
                        first = one.astype(BF).astype(F32)
                        second = (one - first).astype(BF).astype(F32)
                        entries += [(0, first), (1, second), (2, one - first - second)]
                    for i, row in entries:
                        stats[owner] = jnp.where(place == i * stat_rows + offset // 128, row, stats[owner])
        for owner in range(owners):
            pay_ref[step * owners + owner, owned : owned + extra, :] = stats[owner].astype(BF)

    key_norm = jnp.max(head_sum(kk))
    column_norm = jnp.max(jnp.sum(jnp.square(wp_ref[...].astype(F32)), axis=1))
    near_zero = key_norm * column_norm < SMALL * SMALL
    pl.when(near_zero)(lambda: partial_sums(False))
    pl.when(jnp.logical_not(near_zero))(lambda: partial_sums(True))
    nk_ref[...] = head_norm(kk)
    nv_ref[...] = head_norm(vv)
    query = (dot(x, wq_ref[...]).astype(BF).astype(F32) * HS ** (-0.5)).astype(BF)
    q_ref[...] = query
    top_ref[...] = jnp.maximum(top_ref[...], jnp.max(head_sum(query)))

    @pl.when(step == steps - 1)
    def _():
        chip = s_ref[1]
        copies = [
            pltpu.make_async_copy(pay_ref.at[lax.bitwise_xor(chip, k)], pays[k], sem.at[k]) for k in range(chips)
        ]
        for copy in copies:
            copy.start()
        for copy in copies:
            copy.wait()


def combine_kernel(sizes, *refs):
    chips, owned, extra = sizes
    pays, far_ref = refs[:chips], refs[chips]
    stat_rows = owned // 128
    tails = [p[owned : owned + extra, :].astype(F32) for p in pays]
    peaks = [
        t[:stat_rows] + t[stat_rows : 2 * stat_rows] + t[2 * stat_rows : 3 * stat_rows] for t in tails
    ]
    peak = functools.reduce(jnp.maximum, peaks)
    scales = [jnp.exp(p - peak) for p in peaks]
    total = sum(s * t[3 * stat_rows : 4 * stat_rows] for s, t in zip(scales, tails))
    scales = [s / total for s in scales]
    for i in range(stat_rows):
        cut = slice(i * 128, (i + 1) * 128)
        summary = sum(to_column(s[i : i + 1]) * p[cut, :].astype(F32) for s, p in zip(scales, pays))
        far_ref[cut, :] = head_norm_wide(summary)


def one_head(qp, side):
    low_half = lanes(qp.shape) < HS
    none = jnp.zeros_like(qp)
    return jnp.where(low_half, qp, none) if side == 0 else jnp.where(low_half, none, qp)


def with_ones(v, side):
    low_half = lanes(v.shape) < HS
    ones = jnp.ones_like(v)
    return jnp.where(low_half, v, ones) if side == 0 else jnp.where(low_half, ones, v)


def small_scores(top_ref):
    return jnp.max(top_ref[...]) * (HS * 1.02) < SMALL * SMALL


def near_kernel(s_ref, top_ref, q_ref, nk_ref, nv_ref, halo_ref, halop_ref, wk_ref, wv_ref, o_ref, m_ref, xh_ref):
    rows = halo_ref.shape[0]
    step = pl.program_id(0)

    @pl.when(step == 0)
    def _():
        xh_ref[:rows] = layer_norm(halo_ref[...].astype(F32)).astype(BF)
        xh_ref[rows:] = layer_norm(halop_ref[...].astype(F32)).astype(BF)
        m_ref[...] = jnp.zeros_like(m_ref)

    x = xh_ref[...]
    halo_k = head_norm(dot(x, wk_ref[...]).astype(BF))
    halo_v = head_norm(dot(x, wv_ref[...]).astype(BF))
    inside = [s_ref[i] > 0 for i in (2, 3)]
    heads = halo_k.shape[1] // HS
    place = lanes((rows, 128))

    def attend(shifted):
        for pair in range(heads // 2):
            cut = slice(pair * 128, (pair + 1) * 128)
            kp = nk_ref[:, cut]
            for side in range(2):
                vp = with_ones(nv_ref[:, cut], side)
                for part in range(2):
                    these = slice(part * rows, (part + 1) * rows)
                    qm = one_head(q_ref[these, cut], side)
                    main = lax.dot_general(qm, kp, NT, preferred_element_type=F32)
                    halo = lax.dot_general(qm, halo_k[these, cut], NT, preferred_element_type=F32)
                    halo = halo + jnp.where(inside[part], 0.0, -jnp.inf).astype(F32)
                    if shifted:
                        peak = jnp.maximum(
                            jnp.max(main, axis=1, keepdims=True), jnp.max(halo, axis=1, keepdims=True)
                        )
                        main, halo = main - peak, halo - peak
                        here = place == step * heads + pair * 2 + side
                        m_ref[these] = jnp.where(here, peak, m_ref[these])
                    out = dot(jnp.exp(main).astype(BF), vp)
                    out = out + dot(jnp.exp(halo).astype(BF), with_ones(halo_v[these, cut], side))
                    o_ref[these, (pair * 2 + side) * 128 : (pair * 2 + side + 1) * 128] = out

    small = small_scores(top_ref)
    pl.when(small)(lambda: attend(False))
    pl.when(jnp.logical_not(small))(lambda: attend(True))


def far_kernel(sizes, s_ref, top_ref, q_ref, o_ref, m_ref, *rest):
    chips, owned, rank = sizes
    fars, (mine_ref, theirs_ref, all_ref) = rest[:chips], rest[chips:]
    rows = mine_ref.shape[0]
    step = pl.program_id(0)

    @pl.when(step == 0)
    def _():
        for k in range(chips):
            source = lax.bitwise_xor(s_ref[1], k)
            all_ref[pl.ds(pl.multiple_of(source * owned, owned), owned), :] = fars[k][...]

    heads = q_ref.shape[1] // HS
    place = lanes((rows, 128))

    def attend(shifted):
        for pair in range(heads // 2):
            cut = slice(pair * 128, (pair + 1) * 128)
            for part in range(2):
                these = slice(part * rows, (part + 1) * rows)
                low_half = lanes((rows, 128)) < HS
                sums = []
                for side in range(2):
                    qm = one_head(q_ref[these, cut], side)
                    head = step * heads + pair * 2 + side
                    kv = all_ref[pl.ds(pl.multiple_of(head * rank, rank), rank), :]
                    scores = lax.dot_general(qm, kv, NT, preferred_element_type=F32)
                    before = o_ref[these, (pair * 2 + side) * 128 : (pair * 2 + side + 1) * 128]
                    if shifted:
                        peak = jnp.sum(jnp.where(place == head, m_ref[these], 0.0), axis=1, keepdims=True)
                        new = jnp.maximum(peak, jnp.max(scores, axis=1, keepdims=True))
                        scores = scores - new
                        before = before * jnp.exp(peak - new)
                    out = dot(jnp.exp(scores).astype(BF), with_ones(kv, 1 - side))
                    sums.append(before + pltpu.roll(out, 64, 1))
                total = pltpu.roll(jnp.where(low_half, sums[1], sums[0]), 64, 1)
                result = (jnp.where(low_half, sums[0], sums[1]) / total).astype(BF)
                (mine_ref, theirs_ref)[part][:, cut] = result

    small = small_scores(top_ref)
    pl.when(small)(lambda: attend(False))
    pl.when(jnp.logical_not(small))(lambda: attend(True))


def mix_kernel(s_ref, tok_ref, a_ref, b_ref, w_ref, mixed_ref, yn_ref):
    wide = a_ref.shape[1]
    first = pl.ds(pl.multiple_of(s_ref[0] * wide, wide), wide)
    second = pl.ds(pl.multiple_of(s_ref[5] * wide, wide), wide)
    total = dot(a_ref[...], w_ref[first, :]) + dot(b_ref[...], w_ref[second, :])
    mixed = (tok_ref[...].astype(F32) + total).astype(BF)
    mixed_ref[...] = mixed
    yn_ref[...] = layer_norm(mixed.astype(F32)).astype(BF)


def gelu(v):
    return 0.5 * v * (1.0 + jnp.tanh((2.0 / jnp.pi) ** 0.5 * (v + 0.044715 * (v * v * v))))


def feed_kernel(parts, s_ref, yn_ref, *rest):
    sides = len(rest[:-1]) // parts
    out_ref = rest[-1]
    depth = rest[0].shape[1]
    starts = [
        pl.multiple_of(lax.rem(s_ref[4] + parts - i, parts) * depth, depth) for i in range(parts)
    ]
    hidden = []
    for side in range(sides):
        bufs = rest[side * parts : (side + 1) * parts]
        total = sum(dot(yn_ref[:, pl.ds(starts[i], depth)], bufs[i][0]) for i in range(parts))
        hidden.append(gelu(total).astype(BF))
    for i in range(parts):
        total = sum(
            lax.dot_general(hidden[side], rest[side * parts + i][1], NT, preferred_element_type=F32)
            for side in range(sides)
        )
        out_ref[:, pl.ds(starts[i], depth)] = total.astype(out_ref.dtype)


def call(kernel, grid, in_specs, out_specs, out_shape, scratch=(), cost=(0, 0, 0)):
    return pl.pallas_call(
        kernel,
        grid_spec=pltpu.PrefetchScalarGridSpec(
            num_scalar_prefetch=1, grid=grid, in_specs=in_specs, out_specs=out_specs, scratch_shapes=scratch
        ),
        out_shape=out_shape,
        compiler_params=pltpu.CompilerParams(vmem_limit_bytes=VMEM_LIMIT),
        cost_estimate=pl.CostEstimate(flops=cost[0], bytes_accessed=cost[1], transcendentals=cost[2]),
    )


def shape(dims, dtype=BF):
    return jax.ShapeDtypeStruct(dims, dtype)


def whole(dims):
    return pl.BlockSpec(dims, lambda *_: (0,) * len(dims))


def after(x, *earlier):
    return lax.optimization_barrier((x,) + earlier)[0]


def on_device(layer_input, w_qkv, w_out, w_proj, w_up, w_down):
    tokens = layer_input[0]
    rows, width = tokens.shape
    heads, _, rank = w_proj.shape
    n, parts = lax.axis_size("seq"), lax.axis_size("dp")
    chips = n // 2
    me = lax.axis_index("seq")
    core = me % 2
    other = me + 1 - 2 * core
    inner = lambda i: ((i > 0) & (i < n - 1)).astype(jnp.int32)
    scalars = jnp.stack([core, me // 2, inner(me), inner(other), lax.axis_index("dp"), 1 - core]).astype(jnp.int32)
    vmem = pl.BlockSpec(memory_space=pltpu.VMEM)

    swap = lambda x: lax.ppermute(x, "seq", [(i, i ^ 1) for i in range(n)])
    jump = lambda x, k: lax.ppermute(x, "seq", [(i, i ^ (2 * k)) for i in range(n)])
    edges = [(i, i + 1) for i in range(1, n - 1, 2)]

    partner = swap(tokens)
    halo = lax.ppermute(tokens, "seq", edges + [(j, i) for i, j in edges])

    own = jnp.stack([w_up, w_down])
    gathered = [own]
    for s in range(1, parts):
        gathered.append(lax.ppermute(own, "dp", [(i, (i + s) % parts) for i in range(parts)]))
    share = chips // 2
    shared = []

    def share_part(s, *earlier):
        if share and s < parts:
            shared.append(jump(after(gathered[s], *earlier) if earlier else gathered[s], share))

    share_part(0)
    w_qkv = pltpu.with_memory_space_constraint(w_qkv, pltpu.HBM)

    half = heads // 2
    wide = half * HS
    block = 4 * HS
    steps = wide // block
    owned = half * rank // chips
    extra = max(16, 4 * owned // 128)
    blocks = width // block
    tok_spec = whole((rows, width))
    column = lambda which: pl.BlockSpec(
        (width, block), lambda g, s, which=which: (0, which * blocks + s[0] * steps + g)
    )
    proj_spec = pl.BlockSpec((4, HS, rank), lambda g, s: (s[0] * steps + g, 0, 0))
    slab = pl.BlockSpec((2 * rows, block), lambda g, s: (0, g))
    out = call(
        functools.partial(qkv_kernel, (chips, owned, extra, steps, rank)),
        (steps,),
        [tok_spec, tok_spec, column(0), column(1), column(2), proj_spec],
        [slab, slab, slab, whole((8, 128))] + [pl.BlockSpec(memory_space=pl.ANY)] * chips,
        [shape((2 * rows, wide))] * 3 + [shape((8, 128), F32)] + [shape((owned + extra, 128))] * chips,
        [
            pltpu.VMEM((2 * rows, width), BF),
            pltpu.VMEM((chips, owned + extra, 128), BF),
            pltpu.SemaphoreType.DMA((chips,)),
        ],
        (4 * rows * width * 3 * wide, 6 * width * wide, half * rank * 2 * rows),
    )(scalars, tokens, partner, w_qkv, w_qkv, w_qkv, w_proj)
    query, near_keys, near_values, top = out[:4]
    pays = [out[4]] + [jump(out[4 + k], k) for k in range(1, chips)]

    halo = after(halo, out[4])
    halo_partner = swap(halo)
    share_part(1, out[4])
    per_head = pl.BlockSpec((2 * rows, 2 * block), lambda g, s: (0, g))
    near, peaks = call(
        near_kernel,
        (steps,),
        [whole((8, 128)), slab, slab, slab, tok_spec, tok_spec, column(1), column(2)],
        [per_head, whole((2 * rows, 128))],
        [shape((2 * rows, 2 * wide), F32), shape((2 * rows, 128), F32)],
        [pltpu.VMEM((2 * rows, width), BF)],
        (4 * rows * width * 2 * wide, 6 * width * wide, half * 3 * WBLK * 2 * rows),
    )(scalars, top, query, near_keys, near_values, halo, halo_partner, w_qkv, w_qkv)

    pays = [after(p, near) for p in pays]
    far = pl.pallas_call(
        functools.partial(combine_kernel, (chips, owned, extra)),
        out_shape=shape((owned, 128)),
        compiler_params=pltpu.CompilerParams(vmem_limit_bytes=VMEM_LIMIT),
        cost_estimate=pl.CostEstimate(flops=1000000, bytes_accessed=1000000, transcendentals=0),
    )(*pays)
    own_sides = gathered + [swap(after(w, far)) for w in gathered]
    share_part(2, far)
    fars = [far] + [jump(far, k) for k in range(1, chips)]
    mine, theirs = call(
        functools.partial(far_kernel, (chips, owned, rank)),
        (steps,),
        [whole((8, 128)), slab, per_head, whole((2 * rows, 128))] + [whole((owned, 128))] * chips,
        [pl.BlockSpec((rows, block), lambda g, s: (0, g))] * 2,
        [shape((rows, wide))] * 2,
        [pltpu.VMEM((half * rank, 128), BF)],
        (4 * rows * wide * rank * 2, 6 * rows * wide, half * rank * 2 * rows),
    )(scalars, top, query, near, peaks, *fars)
    arrived = swap(theirs)
    for s in range(3, parts):
        share_part(s, theirs)
    mixed, yn = call(
        mix_kernel,
        (1,),
        [vmem] * 4,
        [vmem] * 2,
        [shape((rows, width))] * 2,
        (),
        (4 * rows * width * wide, 2 * width * width, 0),
    )(scalars, tokens, mine, arrived, w_out)


    def feed(x, dtype, weights):
        return call(
            functools.partial(feed_kernel, parts),
            (1,),
            [vmem] * (1 + len(weights)),
            vmem,
            shape((rows, width), dtype),
            (),
            (2 * rows * width * len(weights) * w_up.shape[1], len(weights) * own.size, rows * w_up.shape[1]),
        )(scalars, x, *weights)

    visits = range(1, max(share, 1))
    visitors = []
    for k in visits:
        visitors.append(jump(yn, k))
    terms = [feed(yn, F32, own_sides)]
    all_sides = own_sides
    if share:
        shared = [after(w, terms[0]) for w in shared]
        far_sides = shared + [swap(w) for w in shared]
        all_sides = own_sides + far_sides
    returned = []
    for k, x in zip(visits, visitors):
        x = feed(after(x, terms[0]), BF, all_sides)
        returned.append(jump(x, k))
    if share:
        terms.append(feed(after(yn, x) if returned else yn, F32, far_sides))
    result = mixed.astype(F32) + sum(terms)
    for x in returned:
        result = result + x.astype(F32)
    return result.astype(BF)[None]


def solution(mesh):
    in_specs = (P("dp", "seq", None), P(), P(), P(), P("dp", "seq"), P("dp", "seq"))
    out_specs = P("dp", "seq", None)
    return jax.shard_map(on_device, mesh=mesh, in_specs=in_specs, out_specs=out_specs, check_vma=False)
```

profile of v0, /device:TPU:28, one launch (start us, length us, event | category | flops | bytes accessed | tf_op | source)
XLA Modules:
  0.0 148.1 jit_solution(2109897513218802142)
XLA Ops:
  0.0 3.4 %collective-permute-start.1 = (bf16[256,1024]{1,0:T(8,128)(2,1)}, bf16[256,1024]{1,0:T(8,128)(2,1)S(1)}, u32[]{:S(2)}, u32[]{:S(2)}) collective-permute-start(bf16[256,1024]{1,0:T(8,128)(2,1)} %bitcast.12), channel_id=1, source_target_pairs={{1,2},{3,4},{5,6},{2,1},{4,3},{6,5},{9,10},{11,12},{13,14},{10,9},... | collective-permute-start | bytes 1572872 | tf_op jit(solution)/shard_map/ppermute | solution.py:368
  3.6 1.0 copy-done.1
  4.6 1.0 copy-done.3
  5.7 10.5 %shard_map.64 = (bf16[512,512]{1,0:T(8,128)(2,1)S(1)}, bf16[512,512]{1,0:T(8,128)(2,1)S(1)}, bf16[512,512]{1,0:T(8,128)(2,1)S(1)}, f32[8,128]{1,0:T(8,128)S(1)},...) custom-call(s32[6]{0:T(128)S(1)} %stack.44.s_ref, ...), custom_call_target="tpu_custom_call" | custom-call | flops 1610612736 | bytes 3145728 | tf_op jit(solution)/shard_map/pallas_call | solution.py:397
  16.2 0.7 collective-permute-done.1.halo_ref
  17.1 1.9 %collective-permute-start.11 = (bf16[2,256,512]{2,1,0:T(8,128)(2,1)S(1)}, bf16[2,256,512]{2,1,0:T(8,128)(2,1)S(1)}, u32[]{:S(2)}, u32[]{:S(2)}) collective-permute-start(bf16[2,256,512]{2,1,0:T(8,128)(2,1)S(1)} %pad_maximum_fusion.rest_0_), channel_id=1, source_target_pairs={{0,16},{8,24},{16,0},{24,8},{1,17},{9,25},{17,1},{25,9},{2,18},{10... | collective-permute-start | bytes 1572872 | tf_op jit(solution)/shard_map/ppermute | solution.py:373
  19.0 1.6 %collective-permute-start.5 = (bf16[528,128]{1,0:T(8,128)(2,1)S(1)}, bf16[528,128]{1,0:T(8,128)(2,1)S(1)}, u32[]{:S(2)}, u32[]{:S(2)}) collective-permute-start(bf16[528,128]{1,0:T(8,128)(2,1)S(1)} %get-tuple-element.49), channel_id=1, source_target_pairs={{0,6},{1,7},{2,4},{3,5},{4,2},{5,3},{6,0},{7,1},{8,14},{9,15},{10,... | collective-permute-start | bytes 405512 | tf_op jit(solution)/shard_map/ppermute | solution.py:364
  20.7 4.7 %collective-permute-done.5.refs_3_ = bf16[528,128]{1,0:T(8,128)(2,1)S(1)} collective-permute-done((bf16[528,128]{1,0:T(8,128)(2,1)S(1)}, bf16[528,128]{1,0:T(8,128)(2,1)S(1)}, u32[]{:S(2)}, u32[]{:S(2)}) %collective-permute-start.5) | collective-permute-done | bytes 135200 | tf_op jit(solution)/shard_map/ppermute | solution.py:364
  26.1 12.8 %shard_map.65 = (f32[512,1024]{1,0:T(8,128)S(1)}, f32[512,128]{1,0:T(8,128)S(1)}) custom-call(s32[6]{0:T(128)S(1)} %stack.44.s_ref, f32[8,128]{1,0:T(8,128)S(1)} %get-tuple-element.36.top_ref, bf16[512,512]{1,0:T(8,128)(2,1)S(1)} %get-tuple-element.37.q_ref, bf16[512,512]{1,0:T(8,128)(2,1)S(1)} %get-tuple-element.38.nk_ref, ...), custom_call_target="tpu_custom_call" | custom-call | flops 1073741824 | bytes 3145728 | tf_op jit(solution)/shard_map/pallas_call | solution.py:417
  39.0 0.7 shard_map.66.rest_0_
  39.7 0.9 collective-permute-start.8
  40.6 2.4 %collective-permute-start.7 = (bf16[512,128]{1,0:T(8,128)(2,1)S(1)}, bf16[512,128]{1,0:T(8,128)(2,1)S(1)}, u32[]{:S(2)}, u32[]{:S(2)}) collective-permute-start(bf16[512,128]{1,0:T(8,128)(2,1)S(1)} %shard_map.66.rest_0_), channel_id=1, source_target_pairs={{0,4},{1,5},{2,6},{3,7},{4,0},{5,1},{6,2},{7,3},{8,12},{9,13},{10,... | collective-permute-start | bytes 393224 | tf_op jit(solution)/shard_map/ppermute | solution.py:364
  43.0 22.0 %collective-permute-done.11.rest_2_ = bf16[2,256,512]{2,1,0:T(8,128)(2,1)S(1)} collective-permute-done((bf16[2,256,512]{2,1,0:T(8,128)(2,1)S(1)}, bf16[2,256,512]{2,1,0:T(8,128)(2,1)S(1)}, u32[]{:S(2)}, u32[]{:S(2)}) %collective-permute-start.11) | collective-permute-done | bytes 524320 | tf_op jit(solution)/shard_map/ppermute | solution.py:373
  65.0 0.5 collective-permute-start.15
  65.7 5.2 %collective-permute-done.6.rest_1_ = bf16[512,128]{1,0:T(8,128)(2,1)S(1)} collective-permute-done((bf16[512,128]{1,0:T(8,128)(2,1)S(1)}, bf16[512,128]{1,0:T(8,128)(2,1)S(1)}, u32[]{:S(2)}, u32[]{:S(2)}) %collective-permute-start.6) | collective-permute-done | bytes 131104 | tf_op jit(solution)/shard_map/ppermute | solution.py:364
  71.0 7.7 %shard_map.67 = (bf16[256,512]{1,0:T(8,128)(2,1)S(1)}, bf16[256,512]{1,0:T(8,128)(2,1)S(1)}) custom-call(s32[6]{0:T(128)S(1)} %stack.44.s_ref, f32[8,128]{1,0:T(8,128)S(1)} %get-tuple-element.36.top_ref, bf16[512,512]{1,0:T(8,128)(2,1)S(1)} %get-tuple-element.37.q_ref, f32[512,1024]{1,0:T(8,128)S(1)} %get-tuple-element.42.o_ref, ...), custom_call_target="tpu_custom_call" | custom-call | flops 268435456 | bytes 786432 | tf_op jit(solution)/shard_map/pallas_call | solution.py:437
  78.8 0.5 collective-permute-start.16
  79.3 1.0 collective-permute-done.9.b_ref
  80.3 2.0 %collective-permute-start.19 = (bf16[2,256,512]{2,1,0:T(8,128)(2,1)S(1)}, bf16[2,256,512]{2,1,0:T(8,128)(2,1)S(1)}, u32[]{:S(2)}, u32[]{:S(2)}) collective-permute-start(bf16[2,256,512]{2,1,0:T(8,128)(2,1)S(1)} %collective-permute-done.10.rest_1_), channel_id=1, source_target_pairs={{0,4},{1,5},{2,6},{3,7},{4,0},{5,1},{6,2},{7,3},{8,12},{9,13},{10,... | collective-permute-start | bytes 1572872 | tf_op jit(solution)/shard_map/ppermute | solution.py:364
  82.4 2.0 %collective-permute-start.21 = (bf16[2,256,512]{2,1,0:T(8,128)(2,1)S(1)}, bf16[2,256,512]{2,1,0:T(8,128)(2,1)S(1)}, u32[]{:S(2)}, u32[]{:S(2)}) collective-permute-start(bf16[2,256,512]{2,1,0:T(8,128)(2,1)S(1)} %collective-permute-done.12.rest_3_), channel_id=1, source_target_pairs={{0,4},{1,5},{2,6},{3,7},{4,0},{5,1},{6,2},{7,3},{8,12},{9,13},{10,... | collective-permute-start | bytes 1572872 | tf_op jit(solution)/shard_map/ppermute | solution.py:364
  84.4 1.5 %shard_map.68 = (bf16[256,1024]{1,0:T(8,128)(2,1)S(1)}, bf16[256,1024]{1,0:T(8,128)(2,1)S(1)}) custom-call(s32[6]{0:T(128)S(1)} %stack.44.s_ref, bf16[256,1024]{1,0:T(8,128)(2,1)S(1)} %bitcast.14, bf16[256,512]{1,0:T(8,128)(2,1)S(1)} %get-tuple-element.51.a_ref, bf16[256,512]{1,0:T(8,128)(2,1)S(1)} %collective-permute-done.9.b_ref, ...), custom_call_target="tpu_custom_call" | custom-call | flops 536870912 | bytes 2097152 | tf_op jit(solution)/shard_map/pallas_call | solution.py:449
  86.3 2.0 %shard_map.69 = f32[256,1024]{1,0:T(8,128)S(1)} custom-call(s32[6]{0:T(128)S(1)} %stack.44.s_ref, bf16[256,1024]{1,0:T(8,128)(2,1)S(1)} %get-tuple-element.66.yn_ref, bf16[2,256,512]{2,1,0:T(8,128)(2,1)S(1)} %pad_maximum_fusion.rest_0_, bf16[2,256,512]{2,1,0:T(8,128)(2,1)S(1)} %collective-permute-done.10.rest_1_, ...), custom_call_target="tpu_custom_call" | custom-call | flops 2147483648 | bytes 2097152 | tf_op jit(solution)/shard_map/pallas_call | solution.py:461
  88.3 6.8 %collective-permute-done.20.rest_10_.rest_2_ = bf16[2,256,512]{2,1,0:T(8,128)(2,1)S(1)} collective-permute-done((bf16[2,256,512]{2,1,0:T(8,128)(2,1)S(1)}, bf16[2,256,512]{2,1,0:T(8,128)(2,1)S(1)}, u32[]{:S(2)}, u32[]{:S(2)}) %collective-permute-start.20) | collective-permute-done | bytes 524320 | tf_op jit(solution)/shard_map/ppermute | solution.py:364
  95.1 11.2 %collective-permute-done.19.rest_9_.rest_1_ = bf16[2,256,512]{2,1,0:T(8,128)(2,1)S(1)} collective-permute-done((bf16[2,256,512]{2,1,0:T(8,128)(2,1)S(1)}, bf16[2,256,512]{2,1,0:T(8,128)(2,1)S(1)}, u32[]{:S(2)}, u32[]{:S(2)}) %collective-permute-start.19) | collective-permute-done | bytes 524320 | tf_op jit(solution)/shard_map/ppermute | solution.py:364
  106.3 11.2 %collective-permute-done.18.rest_8_.rest_0_ = bf16[2,256,512]{2,1,0:T(8,128)(2,1)S(1)} collective-permute-done((bf16[2,256,512]{2,1,0:T(8,128)(2,1)S(1)}, bf16[2,256,512]{2,1,0:T(8,128)(2,1)S(1)}, u32[]{:S(2)}, u32[]{:S(2)}) %collective-permute-start.18) | collective-permute-done | bytes 524320 | tf_op jit(solution)/shard_map/ppermute | solution.py:364
  117.6 0.5 collective-permute-start.23
  118.1 9.9 %collective-permute-done.21.rest_11_.rest_3_ = bf16[2,256,512]{2,1,0:T(8,128)(2,1)S(1)} collective-permute-done((bf16[2,256,512]{2,1,0:T(8,128)(2,1)S(1)}, bf16[2,256,512]{2,1,0:T(8,128)(2,1)S(1)}, u32[]{:S(2)}, u32[]{:S(2)}) %collective-permute-start.21) | collective-permute-done | bytes 524320 | tf_op jit(solution)/shard_map/ppermute | solution.py:364
  128.0 1.9 %collective-permute-done.25.rest_15_.rest_7_ = bf16[2,256,512]{2,1,0:T(8,128)(2,1)S(1)} collective-permute-done((bf16[2,256,512]{2,1,0:T(8,128)(2,1)S(1)}, bf16[2,256,512]{2,1,0:T(8,128)(2,1)S(1)}, u32[]{:S(2)}, u32[]{:S(2)}) %collective-permute-start.25) | collective-permute-done | bytes 524320 | tf_op jit(solution)/shard_map/ppermute | solution.py:363
  129.9 3.0 %shard_map.70 = bf16[256,1024]{1,0:T(8,128)(2,1)S(1)} custom-call(s32[6]{0:T(128)S(1)} %stack.44.s_ref, bf16[256,1024]{1,0:T(8,128)(2,1)S(1)} %collective-permute-done.17.yn_ref, bf16[2,256,512]{2,1,0:T(8,128)(2,1)S(1)} %pad_maximum_fusion.rest_0_, bf16[2,256,512]{2,1,0:T(8,128)(2,1)S(1)} %collective-permute-done.10.rest_1_, ...), custom_call_target="tpu_custom_call" | custom-call | flops 4294967296 | bytes 4194304 | tf_op jit(solution)/shard_map/pallas_call | solution.py:461
  133.3 2.0 %shard_map.71 = f32[256,1024]{1,0:T(8,128)S(1)} custom-call(s32[6]{0:T(128)S(1)} %stack.44.s_ref, bf16[256,1024]{1,0:T(8,128)(2,1)S(1)} %get-tuple-element.66.yn_ref, bf16[2,256,512]{2,1,0:T(8,128)(2,1)S(1)} %collective-permute-done.18.rest_8_.rest_0_, bf16[2,256,512]{2,1,0:T(8,128)(2,1)S(1)} %collective-permute-done.19.rest_9_.rest_1_, ...), custom_call_target="tpu_custom_call" | custom-call | flops 2147483648 | bytes 2097152 | tf_op jit(solution)/shard_map/pallas_call | solution.py:461
  135.3 11.7 %collective-permute-done.26 = bf16[256,1024]{1,0:T(8,128)(2,1)S(1)} collective-permute-done((bf16[256,1024]{1,0:T(8,128)(2,1)S(1)}, bf16[256,1024]{1,0:T(8,128)(2,1)S(1)}, u32[]{:S(2)}, u32[]{:S(2)}) %collective-permute-start.26) | collective-permute-done | bytes 524320 | tf_op jit(solution)/shard_map/ppermute | solution.py:364
  147.0 1.1 fusion
  (45 shorter events, 2.2 us)
Async XLA Ops:
  0.0 3.6 %collective-permute-start = (bf16[256,1024]{1,0:T(8,128)(2,1)}, bf16[256,1024]{1,0:T(8,128)(2,1)S(1)}, u32[]{:S(2)}, u32[]{:S(2)}) collective-permute-start(bf16[256,1024]{1,0:T(8,128)(2,1)} %bitcast.11), channel_id=1, source_target_pairs={{0,1},{1,0},{2,3},{3,2},{4,5},{5,4},{6,7},{7,6},{8,9},{9,8},{10,11... | collective-permute-start | bytes 1572872 | tf_op jit(solution)/shard_map/ppermute | solution.py:363
  0.0 16.9 %collective-permute-start.1 = (bf16[256,1024]{1,0:T(8,128)(2,1)}, bf16[256,1024]{1,0:T(8,128)(2,1)S(1)}, u32[]{:S(2)}, u32[]{:S(2)}) collective-permute-start(bf16[256,1024]{1,0:T(8,128)(2,1)} %bitcast.12), channel_id=1, source_target_pairs={{1,2},{3,4},{5,6},{2,1},{4,3},{6,5},{9,10},{11,12},{13,14},{10,9},... | collective-permute-start | bytes 1572872 | tf_op jit(solution)/shard_map/ppermute | solution.py:368
  3.6 1.0 copy-start.1
  5.7 11.3 %copy-start.4 = (bf16[256,512]{1,0:T(8,128)(2,1)S(1)}, bf16[256,512]{1,0:T(8,128)(2,1)}, u32[]{:S(2)}) copy-start(bf16[256,512]{1,0:T(8,128)(2,1)} %param.11) | copy-start | bytes 786436
  5.7 11.3 %copy-start.5 = (bf16[256,512]{1,0:T(8,128)(2,1)S(1)}, bf16[256,512]{1,0:T(8,128)(2,1)}, u32[]{:S(2)}) copy-start(bf16[256,512]{1,0:T(8,128)(2,1)} %param.10) | copy-start | bytes 786436
  17.0 8.7 %collective-permute-start.2 = (bf16[256,1024]{1,0:T(8,128)(2,1)S(1)}, bf16[256,1024]{1,0:T(8,128)(2,1)S(1)}, u32[]{:S(2)}, u32[]{:S(2)}) collective-permute-start(bf16[256,1024]{1,0:T(8,128)(2,1)S(1)} %collective-permute-done.1.halo_ref), channel_id=1, source_target_pairs={{0,1},{1,0},{2,3},{3,2},{4,5},{5,4},{6,7},{7,6},{8,9},{9,8},{10,11... | collective-permute-start | bytes 1572872 | tf_op jit(solution)/shard_map/ppermute | solution.py:363
  17.0 26.0 %collective-permute-start.10 = (bf16[2,256,512]{2,1,0:T(8,128)(2,1)S(1)}, bf16[2,256,512]{2,1,0:T(8,128)(2,1)S(1)}, u32[]{:S(2)}, u32[]{:S(2)}) collective-permute-start(bf16[2,256,512]{2,1,0:T(8,128)(2,1)S(1)} %pad_maximum_fusion.rest_0_), channel_id=1, source_target_pairs={{0,8},{8,16},{16,24},{24,0},{1,9},{9,17},{17,25},{25,1},{2,10},{10... | collective-permute-start | bytes 1572872 | tf_op jit(solution)/shard_map/ppermute | solution.py:373
  17.1 47.9 %collective-permute-start.11 = (bf16[2,256,512]{2,1,0:T(8,128)(2,1)S(1)}, bf16[2,256,512]{2,1,0:T(8,128)(2,1)S(1)}, u32[]{:S(2)}, u32[]{:S(2)}) collective-permute-start(bf16[2,256,512]{2,1,0:T(8,128)(2,1)S(1)} %pad_maximum_fusion.rest_0_), channel_id=1, source_target_pairs={{0,16},{8,24},{16,0},{24,8},{1,17},{9,25},{17,1},{25,9},{2,18},{10... | collective-permute-start | bytes 1572872 | tf_op jit(solution)/shard_map/ppermute | solution.py:373
  19.0 6.4 %collective-permute-start.5 = (bf16[528,128]{1,0:T(8,128)(2,1)S(1)}, bf16[528,128]{1,0:T(8,128)(2,1)S(1)}, u32[]{:S(2)}, u32[]{:S(2)}) collective-permute-start(bf16[528,128]{1,0:T(8,128)(2,1)S(1)} %get-tuple-element.49), channel_id=1, source_target_pairs={{0,6},{1,7},{2,4},{3,5},{4,2},{5,3},{6,0},{7,1},{8,14},{9,15},{10,... | collective-permute-start | bytes 405512 | tf_op jit(solution)/shard_map/ppermute | solution.py:364
  20.6 18.4 %collective-permute-start.4 = (bf16[528,128]{1,0:T(8,128)(2,1)S(1)}, bf16[528,128]{1,0:T(8,128)(2,1)S(1)}, u32[]{:S(2)}, u32[]{:S(2)}) collective-permute-start(bf16[528,128]{1,0:T(8,128)(2,1)S(1)} %get-tuple-element.47), channel_id=1, source_target_pairs={{0,4},{1,5},{2,6},{3,7},{4,0},{5,1},{6,2},{7,3},{8,12},{9,13},{10,... | collective-permute-start | bytes 405512 | tf_op jit(solution)/shard_map/ppermute | solution.py:364
  25.4 13.5 %collective-permute-start.3 = (bf16[528,128]{1,0:T(8,128)(2,1)S(1)}, bf16[528,128]{1,0:T(8,128)(2,1)S(1)}, u32[]{:S(2)}, u32[]{:S(2)}) collective-permute-start(bf16[528,128]{1,0:T(8,128)(2,1)S(1)} %get-tuple-element.45), channel_id=1, source_target_pairs={{0,2},{1,3},{2,0},{3,1},{4,6},{5,7},{6,4},{7,5},{8,10},{9,11},{10,... | collective-permute-start | bytes 405512 | tf_op jit(solution)/shard_map/ppermute | solution.py:364
  25.7 53.1 %collective-permute-start.12 = (bf16[2,256,512]{2,1,0:T(8,128)(2,1)S(1)}, bf16[2,256,512]{2,1,0:T(8,128)(2,1)S(1)}, u32[]{:S(2)}, u32[]{:S(2)}) collective-permute-start(bf16[2,256,512]{2,1,0:T(8,128)(2,1)S(1)} %pad_maximum_fusion.rest_0_), channel_id=1, source_target_pairs={{0,24},{8,0},{16,8},{24,16},{1,25},{9,1},{17,9},{25,17},{2,26},{10... | collective-permute-start | bytes 1572872 | tf_op jit(solution)/shard_map/ppermute | solution.py:373
  38.9 45.5 %copy-start = (bf16[1024,1024]{1,0:T(8,128)(2,1)S(1)}, bf16[1024,1024]{1,0:T(8,128)(2,1)}, u32[]{:S(2)}) copy-start(bf16[1024,1024]{1,0:T(8,128)(2,1)} %w_ref.1) | copy-start | bytes 6291460
  38.9 45.4 %copy-start.2 = (bf16[1,256,1024]{2,1,0:T(8,128)(2,1)S(1)}, bf16[1,256,1024]{2,1,0:T(8,128)(2,1)}, u32[]{:S(2)}) copy-start(bf16[1,256,1024]{2,1,0:T(8,128)(2,1)} %param.6) | copy-start | bytes 1572868
  39.7 25.3 %collective-permute-start.8 = (bf16[512,128]{1,0:T(8,128)(2,1)S(1)}, bf16[512,128]{1,0:T(8,128)(2,1)S(1)}, u32[]{:S(2)}, u32[]{:S(2)}) collective-permute-start(bf16[512,128]{1,0:T(8,128)(2,1)S(1)} %shard_map.66.rest_0_), channel_id=1, source_target_pairs={{0,6},{1,7},{2,4},{3,5},{4,2},{5,3},{6,0},{7,1},{8,14},{9,15},{10,... | collective-permute-start | bytes 393224 | tf_op jit(solution)/shard_map/ppermute | solution.py:364
  40.6 24.9 %collective-permute-start.7 = (bf16[512,128]{1,0:T(8,128)(2,1)S(1)}, bf16[512,128]{1,0:T(8,128)(2,1)S(1)}, u32[]{:S(2)}, u32[]{:S(2)}) collective-permute-start(bf16[512,128]{1,0:T(8,128)(2,1)S(1)} %shard_map.66.rest_0_), channel_id=1, source_target_pairs={{0,4},{1,5},{2,6},{3,7},{4,0},{5,1},{6,2},{7,3},{8,12},{9,13},{10,... | collective-permute-start | bytes 393224 | tf_op jit(solution)/shard_map/ppermute | solution.py:364
  43.0 37.3 %collective-permute-start.13 = (bf16[2,256,512]{2,1,0:T(8,128)(2,1)S(1)}, bf16[2,256,512]{2,1,0:T(8,128)(2,1)S(1)}, u32[]{:S(2)}, u32[]{:S(2)}) collective-permute-start(bf16[2,256,512]{2,1,0:T(8,128)(2,1)S(1)} %pad_maximum_fusion.rest_0_), channel_id=1, source_target_pairs={{0,1},{1,0},{2,3},{3,2},{4,5},{5,4},{6,7},{7,6},{8,9},{9,8},{10,11... | collective-permute-start | bytes 1572872 | tf_op jit(solution)/shard_map/ppermute | solution.py:363
  65.0 17.3 %collective-permute-start.14 = (bf16[2,256,512]{2,1,0:T(8,128)(2,1)S(1)}, bf16[2,256,512]{2,1,0:T(8,128)(2,1)S(1)}, u32[]{:S(2)}, u32[]{:S(2)}) collective-permute-start(bf16[2,256,512]{2,1,0:T(8,128)(2,1)S(1)} %collective-permute-done.10.rest_1_), channel_id=1, source_target_pairs={{0,1},{1,0},{2,3},{3,2},{4,5},{5,4},{6,7},{7,6},{8,9},{9,8},{10,11... | collective-permute-start | bytes 1572872 | tf_op jit(solution)/shard_map/ppermute | solution.py:363
  65.0 17.4 %collective-permute-start.15 = (bf16[2,256,512]{2,1,0:T(8,128)(2,1)S(1)}, bf16[2,256,512]{2,1,0:T(8,128)(2,1)S(1)}, u32[]{:S(2)}, u32[]{:S(2)}) collective-permute-start(bf16[2,256,512]{2,1,0:T(8,128)(2,1)S(1)} %collective-permute-done.11.rest_2_), channel_id=1, source_target_pairs={{0,1},{1,0},{2,3},{3,2},{4,5},{5,4},{6,7},{7,6},{8,9},{9,8},{10,11... | collective-permute-start | bytes 1572872 | tf_op jit(solution)/shard_map/ppermute | solution.py:363
  65.5 5.5 %collective-permute-start.6 = (bf16[512,128]{1,0:T(8,128)(2,1)S(1)}, bf16[512,128]{1,0:T(8,128)(2,1)S(1)}, u32[]{:S(2)}, u32[]{:S(2)}) collective-permute-start(bf16[512,128]{1,0:T(8,128)(2,1)S(1)} %shard_map.66.rest_0_), channel_id=1, source_target_pairs={{0,2},{1,3},{2,0},{3,1},{4,6},{5,7},{6,4},{7,5},{8,10},{9,11},{10,... | collective-permute-start | bytes 393224 | tf_op jit(solution)/shard_map/ppermute | solution.py:364
  78.7 1.6 %collective-permute-start.9 = (bf16[256,512]{1,0:T(8,128)(2,1)S(1)}, bf16[256,512]{1,0:T(8,128)(2,1)S(1)}, u32[]{:S(2)}, u32[]{:S(2)}) collective-permute-start(bf16[256,512]{1,0:T(8,128)(2,1)S(1)} %get-tuple-element.52), channel_id=1, source_target_pairs={{0,1},{1,0},{2,3},{3,2},{4,5},{5,4},{6,7},{7,6},{8,9},{9,8},{10,11... | collective-permute-start | bytes 786440 | tf_op jit(solution)/shard_map/ppermute | solution.py:363
  78.8 7.1 %collective-permute-start.16 = (bf16[2,256,512]{2,1,0:T(8,128)(2,1)S(1)}, bf16[2,256,512]{2,1,0:T(8,128)(2,1)S(1)}, u32[]{:S(2)}, u32[]{:S(2)}) collective-permute-start(bf16[2,256,512]{2,1,0:T(8,128)(2,1)S(1)} %collective-permute-done.12.rest_3_), channel_id=1, source_target_pairs={{0,1},{1,0},{2,3},{3,2},{4,5},{5,4},{6,7},{7,6},{8,9},{9,8},{10,11... | collective-permute-start | bytes 1572872 | tf_op jit(solution)/shard_map/ppermute | solution.py:363
  80.3 14.8 %collective-permute-start.20 = (bf16[2,256,512]{2,1,0:T(8,128)(2,1)S(1)}, bf16[2,256,512]{2,1,0:T(8,128)(2,1)S(1)}, u32[]{:S(2)}, u32[]{:S(2)}) collective-permute-start(bf16[2,256,512]{2,1,0:T(8,128)(2,1)S(1)} %collective-permute-done.11.rest_2_), channel_id=1, source_target_pairs={{0,4},{1,5},{2,6},{3,7},{4,0},{5,1},{6,2},{7,3},{8,12},{9,13},{10,... | collective-permute-start | bytes 1572872 | tf_op jit(solution)/shard_map/ppermute | solution.py:364
  80.3 26.0 %collective-permute-start.19 = (bf16[2,256,512]{2,1,0:T(8,128)(2,1)S(1)}, bf16[2,256,512]{2,1,0:T(8,128)(2,1)S(1)}, u32[]{:S(2)}, u32[]{:S(2)}) collective-permute-start(bf16[2,256,512]{2,1,0:T(8,128)(2,1)S(1)} %collective-permute-done.10.rest_1_), channel_id=1, source_target_pairs={{0,4},{1,5},{2,6},{3,7},{4,0},{5,1},{6,2},{7,3},{8,12},{9,13},{10,... | collective-permute-start | bytes 1572872 | tf_op jit(solution)/shard_map/ppermute | solution.py:364
  82.3 35.2 %collective-permute-start.18 = (bf16[2,256,512]{2,1,0:T(8,128)(2,1)S(1)}, bf16[2,256,512]{2,1,0:T(8,128)(2,1)S(1)}, u32[]{:S(2)}, u32[]{:S(2)}) collective-permute-start(bf16[2,256,512]{2,1,0:T(8,128)(2,1)S(1)} %pad_maximum_fusion.rest_0_), channel_id=1, source_target_pairs={{0,4},{1,5},{2,6},{3,7},{4,0},{5,1},{6,2},{7,3},{8,12},{9,13},{10,... | collective-permute-start | bytes 1572872 | tf_op jit(solution)/shard_map/ppermute | solution.py:364
  82.4 45.6 %collective-permute-start.21 = (bf16[2,256,512]{2,1,0:T(8,128)(2,1)S(1)}, bf16[2,256,512]{2,1,0:T(8,128)(2,1)S(1)}, u32[]{:S(2)}, u32[]{:S(2)}) collective-permute-start(bf16[2,256,512]{2,1,0:T(8,128)(2,1)S(1)} %collective-permute-done.12.rest_3_), channel_id=1, source_target_pairs={{0,4},{1,5},{2,6},{3,7},{4,0},{5,1},{6,2},{7,3},{8,12},{9,13},{10,... | collective-permute-start | bytes 1572872 | tf_op jit(solution)/shard_map/ppermute | solution.py:364
  85.9 42.1 %collective-permute-start.17 = (bf16[256,1024]{1,0:T(8,128)(2,1)S(1)}, bf16[256,1024]{1,0:T(8,128)(2,1)S(1)}, u32[]{:S(2)}, u32[]{:S(2)}) collective-permute-start(bf16[256,1024]{1,0:T(8,128)(2,1)S(1)} %get-tuple-element.66.yn_ref), channel_id=1, source_target_pairs={{0,2},{1,3},{2,0},{3,1},{4,6},{5,7},{6,4},{7,5},{8,10},{9,11},{10,... | collective-permute-start | bytes 1572872 | tf_op jit(solution)/shard_map/ppermute | solution.py:364
  117.6 10.4 %collective-permute-start.22 = (bf16[2,256,512]{2,1,0:T(8,128)(2,1)S(1)}, bf16[2,256,512]{2,1,0:T(8,128)(2,1)S(1)}, u32[]{:S(2)}, u32[]{:S(2)}) collective-permute-start(bf16[2,256,512]{2,1,0:T(8,128)(2,1)S(1)} %collective-permute-done.18.rest_8_.rest_0_), channel_id=1, source_target_pairs={{0,1},{1,0},{2,3},{3,2},{4,5},{5,4},{6,7},{7,6},{8,9},{9,8},{10,11... | collective-permute-start | bytes 1572872 | tf_op jit(solution)/shard_map/ppermute | solution.py:363
  117.6 10.4 %collective-permute-start.23 = (bf16[2,256,512]{2,1,0:T(8,128)(2,1)S(1)}, bf16[2,256,512]{2,1,0:T(8,128)(2,1)S(1)}, u32[]{:S(2)}, u32[]{:S(2)}) collective-permute-start(bf16[2,256,512]{2,1,0:T(8,128)(2,1)S(1)} %collective-permute-done.19.rest_9_.rest_1_), channel_id=1, source_target_pairs={{0,1},{1,0},{2,3},{3,2},{4,5},{5,4},{6,7},{7,6},{8,9},{9,8},{10,11... | collective-permute-start | bytes 1572872 | tf_op jit(solution)/shard_map/ppermute | solution.py:363
  118.1 9.9 %collective-permute-start.24 = (bf16[2,256,512]{2,1,0:T(8,128)(2,1)S(1)}, bf16[2,256,512]{2,1,0:T(8,128)(2,1)S(1)}, u32[]{:S(2)}, u32[]{:S(2)}) collective-permute-start(bf16[2,256,512]{2,1,0:T(8,128)(2,1)S(1)} %collective-permute-done.20.rest_10_.rest_2_), channel_id=1, source_target_pairs={{0,1},{1,0},{2,3},{3,2},{4,5},{5,4},{6,7},{7,6},{8,9},{9,8},{10,11... | collective-permute-start | bytes 1572872 | tf_op jit(solution)/shard_map/ppermute | solution.py:363
  128.0 1.9 %collective-permute-start.25 = (bf16[2,256,512]{2,1,0:T(8,128)(2,1)S(1)}, bf16[2,256,512]{2,1,0:T(8,128)(2,1)S(1)}, u32[]{:S(2)}, u32[]{:S(2)}) collective-permute-start(bf16[2,256,512]{2,1,0:T(8,128)(2,1)S(1)} %collective-permute-done.21.rest_11_.rest_3_), channel_id=1, source_target_pairs={{0,1},{1,0},{2,3},{3,2},{4,5},{5,4},{6,7},{7,6},{8,9},{9,8},{10,11... | collective-permute-start | bytes 1572872 | tf_op jit(solution)/shard_map/ppermute | solution.py:363
  132.9 14.0 %collective-permute-start.26 = (bf16[256,1024]{1,0:T(8,128)(2,1)S(1)}, bf16[256,1024]{1,0:T(8,128)(2,1)S(1)}, u32[]{:S(2)}, u32[]{:S(2)}) collective-permute-start(bf16[256,1024]{1,0:T(8,128)(2,1)S(1)} %shard_map.70), channel_id=1, source_target_pairs={{0,2},{1,3},{2,0},{3,1},{4,6},{5,7},{6,4},{7,5},{8,10},{9,11},{10,... | collective-permute-start | bytes 1572872 | tf_op jit(solution)/shard_map/ppermute | solution.py:364
  (1 other events, 1.0 us)
where the time goes:
time: 148 us
  waiting for transfers between devices  86.5 us (58%)
  Pallas kernels  40.3 us (27%)
  starting transfers between devices  17.7 us (12%)
  local copies, waits for them, and re-layouts  2.19 us (1%)
    ppermute x12, waiting for transfers between devices, on_device(): lax.ppermute(x, 'seq', [(i, i ^ 2 * k) for i in range(n)])  60.8 us
    ppermute x3, waiting for transfers between devices, on_device(): lax.ppermute(own, 'dp', [(i, (i + s) % parts) for i in range(parts)])  22 us
    pallas_call x1, Pallas kernels, on_device(): call(near_kernel, (steps,), [whole((8, 128)), slab, slab, slab, tok_spec,...  12.8 us
    pallas_call x1, Pallas kernels, on_device(): call(functools.partial(qkv_kernel, (chips, owned, extra, steps, rank)), (...  10.5 us
    ppermute x12, starting transfers between devices, on_device(): lax.ppermute(x, 'seq', [(i, i ^ 2 * k) for i in range(n)])  10.2 us
    pallas_call x1, Pallas kernels, on_device(): call(functools.partial(far_kernel, (chips, owned, rank)), (steps,), [whol...  7.71 us
    pallas_call x3, Pallas kernels, feed(): call(functools.partial(feed_kernel, parts), (1,), [vmem] * (1 + len(weigh...  7.04 us
    ppermute x1, starting transfers between devices, on_device(): halo = lax.ppermute(tokens, 'seq', edges + [(j, i) for i, j in edges])  3.44 us
  transfers between devices with their start and end apart: 27, of which 11 were waited for; matrix products, arithmetic and copies ran while one was open for 0% of the time, Pallas kernels for 25%

commit v1 on v0

--- a/solution.py
+++ b/solution.py
@@ -292,7 +292,7 @@
 def mix_kernel(s_ref, tok_ref, a_ref, b_ref, w_ref, mixed_ref, yn_ref):
     wide = a_ref.shape[1]
     first = pl.ds(pl.multiple_of(s_ref[0] * wide, wide), wide)
-    second = pl.ds(pl.multiple_of(s_ref[5] * wide, wide), wide)
+    second = pl.ds(pl.multiple_of(s_ref[4] * wide, wide), wide)
     total = dot(a_ref[...], w_ref[first, :]) + dot(b_ref[...], w_ref[second, :])
     mixed = (tok_ref[...].astype(F32) + total).astype(BF)
     mixed_ref[...] = mixed
@@ -307,9 +307,7 @@
     sides = len(rest[:-1]) // parts
     out_ref = rest[-1]
     depth = rest[0].shape[1]
-    starts = [
-        pl.multiple_of(lax.rem(s_ref[4] + parts - i, parts) * depth, depth) for i in range(parts)
-    ]
+    starts = [pl.multiple_of(s_ref[5 + i] * depth, depth) for i in range(parts)]
     hidden = []
     for side in range(sides):
         bufs = rest[side * parts : (side + 1) * parts]
@@ -357,7 +355,13 @@
     core = me % 2
     other = me + 1 - 2 * core
     inner = lambda i: ((i > 0) & (i < n - 1)).astype(jnp.int32)
-    scalars = jnp.stack([core, me // 2, inner(me), inner(other), lax.axis_index("dp"), 1 - core]).astype(jnp.int32)
+    ring = [0] + list(range(1, parts, 2)) + list(range(2, parts, 2))[::-1]
+    follow = [(ring[i], ring[(i + 1) % parts]) for i in range(parts)]
+    dp = lax.axis_index("dp")
+    held = [
+        sum(jnp.where(dp == ring[i], ring[(i - s) % parts], 0) for i in range(parts)) for s in range(parts)
+    ]
+    scalars = jnp.stack([core, me // 2, inner(me), inner(other), 1 - core] + held).astype(jnp.int32)
     vmem = pl.BlockSpec(memory_space=pltpu.VMEM)
 
     swap = lambda x: lax.ppermute(x, "seq", [(i, i ^ 1) for i in range(n)])
@@ -369,8 +373,12 @@
 
     own = jnp.stack([w_up, w_down])
     gathered = [own]
-    for s in range(1, parts):
-        gathered.append(lax.ppermute(own, "dp", [(i, (i + s) % parts) for i in range(parts)]))
+
+    def gather_part(s, *earlier):
+        if s < parts:
+            gathered.append(lax.ppermute(after(gathered[-1], *earlier), "dp", follow))
+
+    gather_part(1)
     share = chips // 2
     shared = []
 
@@ -379,7 +387,8 @@
             shared.append(jump(after(gathered[s], *earlier) if earlier else gathered[s], share))
 
     share_part(0)
-    w_qkv = pltpu.with_memory_space_constraint(w_qkv, pltpu.HBM)
+    hbm = lambda x: pltpu.with_memory_space_constraint(x, pltpu.HBM)
+    w_qkv = hbm(w_qkv)
 
     half = heads // 2
     wide = half * HS
@@ -406,13 +415,16 @@
             pltpu.SemaphoreType.DMA((chips,)),
         ],
         (4 * rows * width * 3 * wide, 6 * width * wide, half * rank * 2 * rows),
-    )(scalars, tokens, partner, w_qkv, w_qkv, w_qkv, w_proj)
+    )(scalars, hbm(tokens), partner, w_qkv, w_qkv, w_qkv, hbm(w_proj))
     query, near_keys, near_values, top = out[:4]
-    pays = [out[4]] + [jump(out[4 + k], k) for k in range(1, chips)]
+    pays = [out[4]]
+    for k in range(1, chips):
+        pays.append(jump(out[4 + k], k))
 
     halo = after(halo, out[4])
     halo_partner = swap(halo)
     share_part(1, out[4])
+    gather_part(2, out[4])
     per_head = pl.BlockSpec((2 * rows, 2 * block), lambda g, s: (0, g))
     near, peaks = call(
         near_kernel,
@@ -431,9 +443,12 @@
         compiler_params=pltpu.CompilerParams(vmem_limit_bytes=VMEM_LIMIT),
         cost_estimate=pl.CostEstimate(flops=1000000, bytes_accessed=1000000, transcendentals=0),
     )(*pays)
-    own_sides = gathered + [swap(after(w, far)) for w in gathered]
+    for s in range(3, parts):
+        gather_part(s, far)
     share_part(2, far)
-    fars = [far] + [jump(far, k) for k in range(1, chips)]
+    fars = [far]
+    for k in range(1, chips):
+        fars.append(jump(far, k))
     mine, theirs = call(
         functools.partial(far_kernel, (chips, owned, rank)),
         (steps,),
@@ -446,6 +461,7 @@
     arrived = swap(theirs)
     for s in range(3, parts):
         share_part(s, theirs)
+    own_sides = gathered + [swap(after(w, theirs)) for w in gathered]
     mixed, yn = call(
         mix_kernel,
         (1,),

time: 148 us -> 132 us (0.89)
  the two profiles are of different devices: /device:TPU:28 before, /device:TPU:0 now
where the time goes in v1:
time: 132 us
  waiting for transfers between devices  60.4 us (46%)
  Pallas kernels  40.6 us (31%)
  starting transfers between devices  28.2 us (21%)
  other arithmetic  2.2 us (2%)
    ppermute x12, waiting for transfers between devices, on_device(): lax.ppermute(x, 'seq', [(i, i ^ 2 * k) for i in range(n)])  54.5 us
    ppermute x12, starting transfers between devices, on_device(): lax.ppermute(x, 'seq', [(i, i ^ 2 * k) for i in range(n)])  13.8 us
    pallas_call x1, Pallas kernels, on_device(): call(near_kernel, (steps,), [whole((8, 128)), slab, slab, slab, tok_spec,...  12.8 us
    pallas_call x1, Pallas kernels, on_device(): call(functools.partial(qkv_kernel, (chips, owned, extra, steps, rank)), (...  11 us
    ppermute x3, starting transfers between devices, gather_part(): gathered.append(lax.ppermute(after(gathered[-1], *earlier), 'dp', follow))  8.86 us
    pallas_call x1, Pallas kernels, on_device(): call(functools.partial(far_kernel, (chips, owned, rank)), (steps,), [whol...  7.48 us
    pallas_call x3, Pallas kernels, feed(): call(functools.partial(feed_kernel, parts), (1,), [vmem] * (1 + len(weigh...  7.13 us
    ppermute x11, waiting for transfers between devices, on_device(): swap = lambda x: lax.ppermute(x, 'seq', [(i, i ^ 1) for i in range(n)])  5.83 us
  transfers between devices with their start and end apart: 27, of which 13 were waited for; matrix products, arithmetic and copies ran while one was open for 1% of the time, Pallas kernels for 29%

profile of v1, /device:TPU:0, one launch (start us, length us, event | category | flops | bytes accessed | tf_op | source)
XLA Modules:
  0.0 131.7 jit_solution(18135216703360637748)
XLA Ops:
  1.2 1.1 pad_maximum_fusion.rest_0_
  2.3 2.6 %collective-permute-start.10 = (bf16[2,256,512]{2,1,0:T(8,128)(2,1)S(1)}, bf16[2,256,512]{2,1,0:T(8,128)(2,1)S(1)}, u32[]{:S(2)}, u32[]{:S(2)}) collective-permute-start(bf16[2,256,512]{2,1,0:T(8,128)(2,1)S(1)} %pad_maximum_fusion.rest_0_), channel_id=1, source_target_pairs={{0,8},{8,24},{24,16},{16,0},{1,9},{9,25},{25,17},{17,1},{2,10},{10... | collective-permute-start | bytes 1572872 | tf_op jit(solution)/shard_map/ppermute | solution.py:379
  5.0 11.0 %shard_map.64 = (bf16[512,512]{1,0:T(8,128)(2,1)S(1)}, bf16[512,512]{1,0:T(8,128)(2,1)S(1)}, bf16[512,512]{1,0:T(8,128)(2,1)S(1)}, f32[8,128]{1,0:T(8,128)S(1)},...) custom-call(s32[9]{0:T(128)S(1)} %stack.56.s_ref, ...), custom_call_target="tpu_custom_call" | custom-call | flops 1610612736 | bytes 3145728 | tf_op jit(solution)/shard_map/pallas_call | solution.py:406
  16.0 2.2 %collective-permute-start.2 = (bf16[256,1024]{1,0:T(8,128)(2,1)S(1)}, bf16[256,1024]{1,0:T(8,128)(2,1)S(1)}, u32[]{:S(2)}, u32[]{:S(2)}) collective-permute-start(bf16[256,1024]{1,0:T(8,128)(2,1)S(1)} %collective-permute-done.1.halo_ref), channel_id=1, source_target_pairs={{0,1},{1,0},{2,3},{3,2},{4,5},{5,4},{6,7},{7,6},{8,9},{9,8},{10,11... | collective-permute-start | bytes 1572872 | tf_op jit(solution)/shard_map/ppermute | solution.py:367
  18.2 2.6 %collective-permute-start.11 = (bf16[2,256,512]{2,1,0:T(8,128)(2,1)S(1)}, bf16[2,256,512]{2,1,0:T(8,128)(2,1)S(1)}, u32[]{:S(2)}, u32[]{:S(2)}) collective-permute-start(bf16[2,256,512]{2,1,0:T(8,128)(2,1)S(1)} %collective-permute-done.10.rest_1_), channel_id=1, source_target_pairs={{0,8},{8,24},{24,16},{16,0},{1,9},{9,25},{25,17},{17,1},{2,10},{10... | collective-permute-start | bytes 1572872 | tf_op jit(solution)/shard_map/ppermute | solution.py:379
  20.8 2.4 %collective-permute-start.5 = (bf16[528,128]{1,0:T(8,128)(2,1)S(1)}, bf16[528,128]{1,0:T(8,128)(2,1)S(1)}, u32[]{:S(2)}, u32[]{:S(2)}) collective-permute-start(bf16[528,128]{1,0:T(8,128)(2,1)S(1)} %get-tuple-element.49), channel_id=1, source_target_pairs={{0,6},{1,7},{2,4},{3,5},{4,2},{5,3},{6,0},{7,1},{8,14},{9,15},{10,... | collective-permute-start | bytes 405512 | tf_op jit(solution)/shard_map/ppermute | solution.py:368
  23.2 1.4 %collective-permute-start.4 = (bf16[528,128]{1,0:T(8,128)(2,1)S(1)}, bf16[528,128]{1,0:T(8,128)(2,1)S(1)}, u32[]{:S(2)}, u32[]{:S(2)}) collective-permute-start(bf16[528,128]{1,0:T(8,128)(2,1)S(1)} %get-tuple-element.47), channel_id=1, source_target_pairs={{0,4},{1,5},{2,6},{3,7},{4,0},{5,1},{6,2},{7,3},{8,12},{9,13},{10,... | collective-permute-start | bytes 405512 | tf_op jit(solution)/shard_map/ppermute | solution.py:368
  24.6 12.8 %shard_map.65 = (f32[512,1024]{1,0:T(8,128)S(1)}, f32[512,128]{1,0:T(8,128)S(1)}) custom-call(s32[9]{0:T(128)S(1)} %stack.56.s_ref, f32[8,128]{1,0:T(8,128)S(1)} %get-tuple-element.36.top_ref, bf16[512,512]{1,0:T(8,128)(2,1)S(1)} %get-tuple-element.37.q_ref, bf16[512,512]{1,0:T(8,128)(2,1)S(1)} %get-tuple-element.38.nk_ref, ...), custom_call_target="tpu_custom_call" | custom-call | flops 1073741824 | bytes 3145728 | tf_op jit(solution)/shard_map/pallas_call | solution.py:429
  38.2 3.7 %collective-permute-start.12 = (bf16[2,256,512]{2,1,0:T(8,128)(2,1)S(1)}, bf16[2,256,512]{2,1,0:T(8,128)(2,1)S(1)}, u32[]{:S(2)}, u32[]{:S(2)}) collective-permute-start(bf16[2,256,512]{2,1,0:T(8,128)(2,1)S(1)} %collective-permute-done.11.rest_2_), channel_id=1, source_target_pairs={{0,8},{8,24},{24,16},{16,0},{1,9},{9,25},{25,17},{17,1},{2,10},{10... | collective-permute-start | bytes 1572872 | tf_op jit(solution)/shard_map/ppermute | solution.py:379
  41.9 1.5 %collective-permute-start.8 = (bf16[512,128]{1,0:T(8,128)(2,1)S(1)}, bf16[512,128]{1,0:T(8,128)(2,1)S(1)}, u32[]{:S(2)}, u32[]{:S(2)}) collective-permute-start(bf16[512,128]{1,0:T(8,128)(2,1)S(1)} %shard_map.66.rest_0_), channel_id=1, source_target_pairs={{0,6},{1,7},{2,4},{3,5},{4,2},{5,3},{6,0},{7,1},{8,14},{9,15},{10,... | collective-permute-start | bytes 393224 | tf_op jit(solution)/shard_map/ppermute | solution.py:368
  43.3 2.0 %collective-permute-start.7 = (bf16[512,128]{1,0:T(8,128)(2,1)S(1)}, bf16[512,128]{1,0:T(8,128)(2,1)S(1)}, u32[]{:S(2)}, u32[]{:S(2)}) collective-permute-start(bf16[512,128]{1,0:T(8,128)(2,1)S(1)} %shard_map.66.rest_0_), channel_id=1, source_target_pairs={{0,4},{1,5},{2,6},{3,7},{4,0},{5,1},{6,2},{7,3},{8,12},{9,13},{10,... | collective-permute-start | bytes 393224 | tf_op jit(solution)/shard_map/ppermute | solution.py:368
  45.4 3.3 %collective-permute-done.8.rest_3_ = bf16[512,128]{1,0:T(8,128)(2,1)S(1)} collective-permute-done((bf16[512,128]{1,0:T(8,128)(2,1)S(1)}, bf16[512,128]{1,0:T(8,128)(2,1)S(1)}, u32[]{:S(2)}, u32[]{:S(2)}) %collective-permute-start.8) | collective-permute-done | bytes 131104 | tf_op jit(solution)/shard_map/ppermute | solution.py:368
  48.7 1.2 collective-permute-done.7.rest_2_
  50.3 7.5 %shard_map.67 = (bf16[256,512]{1,0:T(8,128)(2,1)S(1)}, bf16[256,512]{1,0:T(8,128)(2,1)S(1)}) custom-call(s32[9]{0:T(128)S(1)} %stack.56.s_ref, f32[8,128]{1,0:T(8,128)S(1)} %get-tuple-element.36.top_ref, bf16[512,512]{1,0:T(8,128)(2,1)S(1)} %get-tuple-element.37.q_ref, f32[512,1024]{1,0:T(8,128)S(1)} %get-tuple-element.42.o_ref, ...), custom_call_target="tpu_custom_call" | custom-call | flops 268435456 | bytes 786432 | tf_op jit(solution)/shard_map/pallas_call | solution.py:452
  58.9 2.7 %collective-permute-done.9.b_ref = bf16[256,512]{1,0:T(8,128)(2,1)S(1)} collective-permute-done((bf16[256,512]{1,0:T(8,128)(2,1)S(1)}, bf16[256,512]{1,0:T(8,128)(2,1)S(1)}, u32[]{:S(2)}, u32[]{:S(2)}) %collective-permute-start.9) | collective-permute-done | bytes 262176 | tf_op jit(solution)/shard_map/ppermute | solution.py:367
  61.6 1.1 collective-permute-start.21
  62.8 0.9 collective-permute-start.20
  63.7 1.1 collective-permute-start.19
  64.8 0.9 collective-permute-start.18
  65.7 1.5 %shard_map.68 = (bf16[256,1024]{1,0:T(8,128)(2,1)S(1)}, bf16[256,1024]{1,0:T(8,128)(2,1)S(1)}) custom-call(s32[9]{0:T(128)S(1)} %stack.56.s_ref, bf16[256,1024]{1,0:T(8,128)(2,1)S(1)} %bitcast.17, bf16[256,512]{1,0:T(8,128)(2,1)S(1)} %get-tuple-element.51.a_ref, bf16[256,512]{1,0:T(8,128)(2,1)S(1)} %collective-permute-done.9.b_ref, ...), custom_call_target="tpu_custom_call" | custom-call | flops 536870912 | bytes 2097152 | tf_op jit(solution)/shard_map/pallas_call | solution.py:465
  67.2 1.2 collective-permute-start.17
  68.5 2.0 %shard_map.69 = f32[256,1024]{1,0:T(8,128)S(1)} custom-call(s32[9]{0:T(128)S(1)} %stack.56.s_ref, bf16[256,1024]{1,0:T(8,128)(2,1)S(1)} %get-tuple-element.66.yn_ref, bf16[2,256,512]{2,1,0:T(8,128)(2,1)S(1)} %pad_maximum_fusion.rest_0_, bf16[2,256,512]{2,1,0:T(8,128)(2,1)S(1)} %collective-permute-done.10.rest_1_, ...), custom_call_target="tpu_custom_call" | custom-call | flops 2147483648 | bytes 2097152 | tf_op jit(solution)/shard_map/pallas_call | solution.py:477
  70.5 5.9 %collective-permute-done.21.rest_11_.rest_3_ = bf16[2,256,512]{2,1,0:T(8,128)(2,1)S(1)} collective-permute-done((bf16[2,256,512]{2,1,0:T(8,128)(2,1)S(1)}, bf16[2,256,512]{2,1,0:T(8,128)(2,1)S(1)}, u32[]{:S(2)}, u32[]{:S(2)}) %collective-permute-start.21) | collective-permute-done | bytes 524320 | tf_op jit(solution)/shard_map/ppermute | solution.py:368
  76.4 11.2 %collective-permute-done.20.rest_10_.rest_2_ = bf16[2,256,512]{2,1,0:T(8,128)(2,1)S(1)} collective-permute-done((bf16[2,256,512]{2,1,0:T(8,128)(2,1)S(1)}, bf16[2,256,512]{2,1,0:T(8,128)(2,1)S(1)}, u32[]{:S(2)}, u32[]{:S(2)}) %collective-permute-start.20) | collective-permute-done | bytes 524320 | tf_op jit(solution)/shard_map/ppermute | solution.py:368
  87.7 11.2 %collective-permute-done.19.rest_9_.rest_1_ = bf16[2,256,512]{2,1,0:T(8,128)(2,1)S(1)} collective-permute-done((bf16[2,256,512]{2,1,0:T(8,128)(2,1)S(1)}, bf16[2,256,512]{2,1,0:T(8,128)(2,1)S(1)}, u32[]{:S(2)}, u32[]{:S(2)}) %collective-permute-start.19) | collective-permute-done | bytes 524320 | tf_op jit(solution)/shard_map/ppermute | solution.py:368
  98.9 10.4 %collective-permute-done.18.rest_8_.rest_0_ = bf16[2,256,512]{2,1,0:T(8,128)(2,1)S(1)} collective-permute-done((bf16[2,256,512]{2,1,0:T(8,128)(2,1)S(1)}, bf16[2,256,512]{2,1,0:T(8,128)(2,1)S(1)}, u32[]{:S(2)}, u32[]{:S(2)}) %collective-permute-start.18) | collective-permute-done | bytes 524320 | tf_op jit(solution)/shard_map/ppermute | solution.py:368
  110.3 0.9 collective-permute-done.22.rest_12_.rest_4_
  113.5 3.0 %shard_map.70 = bf16[256,1024]{1,0:T(8,128)(2,1)S(1)} custom-call(s32[9]{0:T(128)S(1)} %stack.56.s_ref, bf16[256,1024]{1,0:T(8,128)(2,1)S(1)} %collective-permute-done.17.yn_ref, bf16[2,256,512]{2,1,0:T(8,128)(2,1)S(1)} %pad_maximum_fusion.rest_0_, bf16[2,256,512]{2,1,0:T(8,128)(2,1)S(1)} %collective-permute-done.10.rest_1_, ...), custom_call_target="tpu_custom_call" | custom-call | flops 4294967296 | bytes 4194304 | tf_op jit(solution)/shard_map/pallas_call | solution.py:477
  116.5 1.2 collective-permute-start.26
  117.7 2.0 %shard_map.71 = f32[256,1024]{1,0:T(8,128)S(1)} custom-call(s32[9]{0:T(128)S(1)} %stack.56.s_ref, bf16[256,1024]{1,0:T(8,128)(2,1)S(1)} %get-tuple-element.66.yn_ref, bf16[2,256,512]{2,1,0:T(8,128)(2,1)S(1)} %collective-permute-done.18.rest_8_.rest_0_, bf16[2,256,512]{2,1,0:T(8,128)(2,1)S(1)} %collective-permute-done.19.rest_9_.rest_1_, ...), custom_call_target="tpu_custom_call" | custom-call | flops 2147483648 | bytes 2097152 | tf_op jit(solution)/shard_map/pallas_call | solution.py:477
  119.8 10.8 %collective-permute-done.26 = bf16[256,1024]{1,0:T(8,128)(2,1)S(1)} collective-permute-done((bf16[256,1024]{1,0:T(8,128)(2,1)S(1)}, bf16[256,1024]{1,0:T(8,128)(2,1)S(1)}, u32[]{:S(2)}, u32[]{:S(2)}) %collective-permute-start.26) | collective-permute-done | bytes 524320 | tf_op jit(solution)/shard_map/ppermute | solution.py:368
  130.6 1.1 fusion
  (37 shorter events, 6.9 us)
Async XLA Ops:
  0.0 5.0 %collective-permute-start = (bf16[256,1024]{1,0:T(8,128)(2,1)}, bf16[256,1024]{1,0:T(8,128)(2,1)S(1)}, u32[]{:S(2)}, u32[]{:S(2)}) collective-permute-start(bf16[256,1024]{1,0:T(8,128)(2,1)} %bitcast.14), channel_id=1, source_target_pairs={{0,1},{1,0},{2,3},{3,2},{4,5},{5,4},{6,7},{7,6},{8,9},{9,8},{10,11... | collective-permute-start | bytes 1572872 | tf_op jit(solution)/shard_map/ppermute | solution.py:367
  0.5 15.5 %collective-permute-start.1 = (bf16[256,1024]{1,0:T(8,128)(2,1)}, bf16[256,1024]{1,0:T(8,128)(2,1)S(1)}, u32[]{:S(2)}, u32[]{:S(2)}) collective-permute-start(bf16[256,1024]{1,0:T(8,128)(2,1)} %bitcast.15), channel_id=1, source_target_pairs={{1,2},{3,4},{5,6},{2,1},{4,3},{6,5},{9,10},{11,12},{13,14},{10,9},... | collective-permute-start | bytes 1572872 | tf_op jit(solution)/shard_map/ppermute | solution.py:372
  2.3 15.9 %collective-permute-start.10 = (bf16[2,256,512]{2,1,0:T(8,128)(2,1)S(1)}, bf16[2,256,512]{2,1,0:T(8,128)(2,1)S(1)}, u32[]{:S(2)}, u32[]{:S(2)}) collective-permute-start(bf16[2,256,512]{2,1,0:T(8,128)(2,1)S(1)} %pad_maximum_fusion.rest_0_), channel_id=1, source_target_pairs={{0,8},{8,24},{24,16},{16,0},{1,9},{9,25},{25,17},{17,1},{2,10},{10... | collective-permute-start | bytes 1572872 | tf_op jit(solution)/shard_map/ppermute | solution.py:379
  16.0 8.7 %collective-permute-start.2 = (bf16[256,1024]{1,0:T(8,128)(2,1)S(1)}, bf16[256,1024]{1,0:T(8,128)(2,1)S(1)}, u32[]{:S(2)}, u32[]{:S(2)}) collective-permute-start(bf16[256,1024]{1,0:T(8,128)(2,1)S(1)} %collective-permute-done.1.halo_ref), channel_id=1, source_target_pairs={{0,1},{1,0},{2,3},{3,2},{4,5},{5,4},{6,7},{7,6},{8,9},{9,8},{10,11... | collective-permute-start | bytes 1572872 | tf_op jit(solution)/shard_map/ppermute | solution.py:367
  18.2 20.0 %collective-permute-start.11 = (bf16[2,256,512]{2,1,0:T(8,128)(2,1)S(1)}, bf16[2,256,512]{2,1,0:T(8,128)(2,1)S(1)}, u32[]{:S(2)}, u32[]{:S(2)}) collective-permute-start(bf16[2,256,512]{2,1,0:T(8,128)(2,1)S(1)} %collective-permute-done.10.rest_1_), channel_id=1, source_target_pairs={{0,8},{8,24},{24,16},{16,0},{1,9},{9,25},{25,17},{17,1},{2,10},{10... | collective-permute-start | bytes 1572872 | tf_op jit(solution)/shard_map/ppermute | solution.py:379
  20.8 16.7 %collective-permute-start.5 = (bf16[528,128]{1,0:T(8,128)(2,1)S(1)}, bf16[528,128]{1,0:T(8,128)(2,1)S(1)}, u32[]{:S(2)}, u32[]{:S(2)}) collective-permute-start(bf16[528,128]{1,0:T(8,128)(2,1)S(1)} %get-tuple-element.49), channel_id=1, source_target_pairs={{0,6},{1,7},{2,4},{3,5},{4,2},{5,3},{6,0},{7,1},{8,14},{9,15},{10,... | collective-permute-start | bytes 405512 | tf_op jit(solution)/shard_map/ppermute | solution.py:368
  23.2 14.3 %collective-permute-start.4 = (bf16[528,128]{1,0:T(8,128)(2,1)S(1)}, bf16[528,128]{1,0:T(8,128)(2,1)S(1)}, u32[]{:S(2)}, u32[]{:S(2)}) collective-permute-start(bf16[528,128]{1,0:T(8,128)(2,1)S(1)} %get-tuple-element.47), channel_id=1, source_target_pairs={{0,4},{1,5},{2,6},{3,7},{4,0},{5,1},{6,2},{7,3},{8,12},{9,13},{10,... | collective-permute-start | bytes 405512 | tf_op jit(solution)/shard_map/ppermute | solution.py:368
  24.6 12.9 %collective-permute-start.3 = (bf16[528,128]{1,0:T(8,128)(2,1)S(1)}, bf16[528,128]{1,0:T(8,128)(2,1)S(1)}, u32[]{:S(2)}, u32[]{:S(2)}) collective-permute-start(bf16[528,128]{1,0:T(8,128)(2,1)S(1)} %get-tuple-element.45), channel_id=1, source_target_pairs={{0,2},{1,3},{2,0},{3,1},{4,6},{5,7},{6,4},{7,5},{8,10},{9,11},{10,... | collective-permute-start | bytes 405512 | tf_op jit(solution)/shard_map/ppermute | solution.py:368
  37.4 28.3 %copy-start = (bf16[1024,1024]{1,0:T(8,128)(2,1)S(1)}, bf16[1024,1024]{1,0:T(8,128)(2,1)}, u32[]{:S(2)}) copy-start(bf16[1024,1024]{1,0:T(8,128)(2,1)} %w_ref.1) | copy-start | bytes 6291460
  37.4 28.3 %copy-start.1 = (bf16[1,256,1024]{2,1,0:T(8,128)(2,1)S(1)}, bf16[1,256,1024]{2,1,0:T(8,128)(2,1)}, u32[]{:S(2)}) copy-start(bf16[1,256,1024]{2,1,0:T(8,128)(2,1)} %param.6) | copy-start | bytes 1572868
  38.2 20.7 %collective-permute-start.12 = (bf16[2,256,512]{2,1,0:T(8,128)(2,1)S(1)}, bf16[2,256,512]{2,1,0:T(8,128)(2,1)S(1)}, u32[]{:S(2)}, u32[]{:S(2)}) collective-permute-start(bf16[2,256,512]{2,1,0:T(8,128)(2,1)S(1)} %collective-permute-done.11.rest_2_), channel_id=1, source_target_pairs={{0,8},{8,24},{24,16},{16,0},{1,9},{9,25},{25,17},{17,1},{2,10},{10... | collective-permute-start | bytes 1572872 | tf_op jit(solution)/shard_map/ppermute | solution.py:379
  41.9 6.8 %collective-permute-start.8 = (bf16[512,128]{1,0:T(8,128)(2,1)S(1)}, bf16[512,128]{1,0:T(8,128)(2,1)S(1)}, u32[]{:S(2)}, u32[]{:S(2)}) collective-permute-start(bf16[512,128]{1,0:T(8,128)(2,1)S(1)} %shard_map.66.rest_0_), channel_id=1, source_target_pairs={{0,6},{1,7},{2,4},{3,5},{4,2},{5,3},{6,0},{7,1},{8,14},{9,15},{10,... | collective-permute-start | bytes 393224 | tf_op jit(solution)/shard_map/ppermute | solution.py:368
  43.3 6.6 %collective-permute-start.7 = (bf16[512,128]{1,0:T(8,128)(2,1)S(1)}, bf16[512,128]{1,0:T(8,128)(2,1)S(1)}, u32[]{:S(2)}, u32[]{:S(2)}) collective-permute-start(bf16[512,128]{1,0:T(8,128)(2,1)S(1)} %shard_map.66.rest_0_), channel_id=1, source_target_pairs={{0,4},{1,5},{2,6},{3,7},{4,0},{5,1},{6,2},{7,3},{8,12},{9,13},{10,... | collective-permute-start | bytes 393224 | tf_op jit(solution)/shard_map/ppermute | solution.py:368
  45.3 5.0 %collective-permute-start.6 = (bf16[512,128]{1,0:T(8,128)(2,1)S(1)}, bf16[512,128]{1,0:T(8,128)(2,1)S(1)}, u32[]{:S(2)}, u32[]{:S(2)}) collective-permute-start(bf16[512,128]{1,0:T(8,128)(2,1)S(1)} %shard_map.66.rest_0_), channel_id=1, source_target_pairs={{0,2},{1,3},{2,0},{3,1},{4,6},{5,7},{6,4},{7,5},{8,10},{9,11},{10,... | collective-permute-start | bytes 393224 | tf_op jit(solution)/shard_map/ppermute | solution.py:368
  57.8 5.0 %collective-permute-start.13 = (bf16[2,256,512]{2,1,0:T(8,128)(2,1)S(1)}, bf16[2,256,512]{2,1,0:T(8,128)(2,1)S(1)}, u32[]{:S(2)}, u32[]{:S(2)}) collective-permute-start(bf16[2,256,512]{2,1,0:T(8,128)(2,1)S(1)} %pad_maximum_fusion.rest_0_), channel_id=1, source_target_pairs={{0,1},{1,0},{2,3},{3,2},{4,5},{5,4},{6,7},{7,6},{8,9},{9,8},{10,11... | collective-permute-start | bytes 1572872 | tf_op jit(solution)/shard_map/ppermute | solution.py:367
  57.9 5.8 %collective-permute-start.14 = (bf16[2,256,512]{2,1,0:T(8,128)(2,1)S(1)}, bf16[2,256,512]{2,1,0:T(8,128)(2,1)S(1)}, u32[]{:S(2)}, u32[]{:S(2)}) collective-permute-start(bf16[2,256,512]{2,1,0:T(8,128)(2,1)S(1)} %collective-permute-done.10.rest_1_), channel_id=1, source_target_pairs={{0,1},{1,0},{2,3},{3,2},{4,5},{5,4},{6,7},{7,6},{8,9},{9,8},{10,11... | collective-permute-start | bytes 1572872 | tf_op jit(solution)/shard_map/ppermute | solution.py:367
  58.4 6.5 %collective-permute-start.15 = (bf16[2,256,512]{2,1,0:T(8,128)(2,1)S(1)}, bf16[2,256,512]{2,1,0:T(8,128)(2,1)S(1)}, u32[]{:S(2)}, u32[]{:S(2)}) collective-permute-start(bf16[2,256,512]{2,1,0:T(8,128)(2,1)S(1)} %collective-permute-done.11.rest_2_), channel_id=1, source_target_pairs={{0,1},{1,0},{2,3},{3,2},{4,5},{5,4},{6,7},{7,6},{8,9},{9,8},{10,11... | collective-permute-start | bytes 1572872 | tf_op jit(solution)/shard_map/ppermute | solution.py:367
  58.4 3.2 %collective-permute-start.9 = (bf16[256,512]{1,0:T(8,128)(2,1)S(1)}, bf16[256,512]{1,0:T(8,128)(2,1)S(1)}, u32[]{:S(2)}, u32[]{:S(2)}) collective-permute-start(bf16[256,512]{1,0:T(8,128)(2,1)S(1)} %get-tuple-element.52), channel_id=1, source_target_pairs={{0,1},{1,0},{2,3},{3,2},{4,5},{5,4},{6,7},{7,6},{8,9},{9,8},{10,11... | collective-permute-start | bytes 786440 | tf_op jit(solution)/shard_map/ppermute | solution.py:367
  58.9 8.4 %collective-permute-start.16 = (bf16[2,256,512]{2,1,0:T(8,128)(2,1)S(1)}, bf16[2,256,512]{2,1,0:T(8,128)(2,1)S(1)}, u32[]{:S(2)}, u32[]{:S(2)}) collective-permute-start(bf16[2,256,512]{2,1,0:T(8,128)(2,1)S(1)} %collective-permute-done.12.rest_3_), channel_id=1, source_target_pairs={{0,1},{1,0},{2,3},{3,2},{4,5},{5,4},{6,7},{7,6},{8,9},{9,8},{10,11... | collective-permute-start | bytes 1572872 | tf_op jit(solution)/shard_map/ppermute | solution.py:367
  61.6 14.8 %collective-permute-start.21 = (bf16[2,256,512]{2,1,0:T(8,128)(2,1)S(1)}, bf16[2,256,512]{2,1,0:T(8,128)(2,1)S(1)}, u32[]{:S(2)}, u32[]{:S(2)}) collective-permute-start(bf16[2,256,512]{2,1,0:T(8,128)(2,1)S(1)} %collective-permute-done.12.rest_3_), channel_id=1, source_target_pairs={{0,4},{1,5},{2,6},{3,7},{4,0},{5,1},{6,2},{7,3},{8,12},{9,13},{10,... | collective-permute-start | bytes 1572872 | tf_op jit(solution)/shard_map/ppermute | solution.py:368
  62.8 24.9 %collective-permute-start.20 = (bf16[2,256,512]{2,1,0:T(8,128)(2,1)S(1)}, bf16[2,256,512]{2,1,0:T(8,128)(2,1)S(1)}, u32[]{:S(2)}, u32[]{:S(2)}) collective-permute-start(bf16[2,256,512]{2,1,0:T(8,128)(2,1)S(1)} %collective-permute-done.11.rest_2_), channel_id=1, source_target_pairs={{0,4},{1,5},{2,6},{3,7},{4,0},{5,1},{6,2},{7,3},{8,12},{9,13},{10,... | collective-permute-start | bytes 1572872 | tf_op jit(solution)/shard_map/ppermute | solution.py:368
  63.7 35.2 %collective-permute-start.19 = (bf16[2,256,512]{2,1,0:T(8,128)(2,1)S(1)}, bf16[2,256,512]{2,1,0:T(8,128)(2,1)S(1)}, u32[]{:S(2)}, u32[]{:S(2)}) collective-permute-start(bf16[2,256,512]{2,1,0:T(8,128)(2,1)S(1)} %collective-permute-done.10.rest_1_), channel_id=1, source_target_pairs={{0,4},{1,5},{2,6},{3,7},{4,0},{5,1},{6,2},{7,3},{8,12},{9,13},{10,... | collective-permute-start | bytes 1572872 | tf_op jit(solution)/shard_map/ppermute | solution.py:368
  64.8 44.5 %collective-permute-start.18 = (bf16[2,256,512]{2,1,0:T(8,128)(2,1)S(1)}, bf16[2,256,512]{2,1,0:T(8,128)(2,1)S(1)}, u32[]{:S(2)}, u32[]{:S(2)}) collective-permute-start(bf16[2,256,512]{2,1,0:T(8,128)(2,1)S(1)} %pad_maximum_fusion.rest_0_), channel_id=1, source_target_pairs={{0,4},{1,5},{2,6},{3,7},{4,0},{5,1},{6,2},{7,3},{8,12},{9,13},{10,... | collective-permute-start | bytes 1572872 | tf_op jit(solution)/shard_map/ppermute | solution.py:368
  67.2 43.1 %collective-permute-start.17 = (bf16[256,1024]{1,0:T(8,128)(2,1)S(1)}, bf16[256,1024]{1,0:T(8,128)(2,1)S(1)}, u32[]{:S(2)}, u32[]{:S(2)}) collective-permute-start(bf16[256,1024]{1,0:T(8,128)(2,1)S(1)} %get-tuple-element.66.yn_ref), channel_id=1, source_target_pairs={{0,2},{1,3},{2,0},{3,1},{4,6},{5,7},{6,4},{7,5},{8,10},{9,11},{10,... | collective-permute-start | bytes 1572872 | tf_op jit(solution)/shard_map/ppermute | solution.py:368
  109.3 1.9 %collective-permute-start.22 = (bf16[2,256,512]{2,1,0:T(8,128)(2,1)S(1)}, bf16[2,256,512]{2,1,0:T(8,128)(2,1)S(1)}, u32[]{:S(2)}, u32[]{:S(2)}) collective-permute-start(bf16[2,256,512]{2,1,0:T(8,128)(2,1)S(1)} %collective-permute-done.18.rest_8_.rest_0_), channel_id=1, source_target_pairs={{0,1},{1,0},{2,3},{3,2},{4,5},{5,4},{6,7},{7,6},{8,9},{9,8},{10,11... | collective-permute-start | bytes 1572872 | tf_op jit(solution)/shard_map/ppermute | solution.py:367
  109.3 2.7 %collective-permute-start.23 = (bf16[2,256,512]{2,1,0:T(8,128)(2,1)S(1)}, bf16[2,256,512]{2,1,0:T(8,128)(2,1)S(1)}, u32[]{:S(2)}, u32[]{:S(2)}) collective-permute-start(bf16[2,256,512]{2,1,0:T(8,128)(2,1)S(1)} %collective-permute-done.19.rest_9_.rest_1_), channel_id=1, source_target_pairs={{0,1},{1,0},{2,3},{3,2},{4,5},{5,4},{6,7},{7,6},{8,9},{9,8},{10,11... | collective-permute-start | bytes 1572872 | tf_op jit(solution)/shard_map/ppermute | solution.py:367
  109.8 2.9 %collective-permute-start.24 = (bf16[2,256,512]{2,1,0:T(8,128)(2,1)S(1)}, bf16[2,256,512]{2,1,0:T(8,128)(2,1)S(1)}, u32[]{:S(2)}, u32[]{:S(2)}) collective-permute-start(bf16[2,256,512]{2,1,0:T(8,128)(2,1)S(1)} %collective-permute-done.20.rest_10_.rest_2_), channel_id=1, source_target_pairs={{0,1},{1,0},{2,3},{3,2},{4,5},{5,4},{6,7},{7,6},{8,9},{9,8},{10,11... | collective-permute-start | bytes 1572872 | tf_op jit(solution)/shard_map/ppermute | solution.py:367
  109.8 3.6 %collective-permute-start.25 = (bf16[2,256,512]{2,1,0:T(8,128)(2,1)S(1)}, bf16[2,256,512]{2,1,0:T(8,128)(2,1)S(1)}, u32[]{:S(2)}, u32[]{:S(2)}) collective-permute-start(bf16[2,256,512]{2,1,0:T(8,128)(2,1)S(1)} %collective-permute-done.21.rest_11_.rest_3_), channel_id=1, source_target_pairs={{0,1},{1,0},{2,3},{3,2},{4,5},{5,4},{6,7},{7,6},{8,9},{9,8},{10,11... | collective-permute-start | bytes 1572872 | tf_op jit(solution)/shard_map/ppermute | solution.py:367
  116.5 14.0 %collective-permute-start.26 = (bf16[256,1024]{1,0:T(8,128)(2,1)S(1)}, bf16[256,1024]{1,0:T(8,128)(2,1)S(1)}, u32[]{:S(2)}, u32[]{:S(2)}) collective-permute-start(bf16[256,1024]{1,0:T(8,128)(2,1)S(1)} %shard_map.70), channel_id=1, source_target_pairs={{0,2},{1,3},{2,0},{3,1},{4,6},{5,7},{6,4},{7,5},{8,10},{9,11},{10,... | collective-permute-start | bytes 1572872 | tf_op jit(solution)/shard_map/ppermute | solution.py:368

commit v2 on v1

v2 whole, which is shorter than its diff:
```python
import functools

import jax
import jax.numpy as jnp
from jax import lax
from jax.experimental import pallas as pl
from jax.experimental.pallas import tpu as pltpu
from jax.sharding import PartitionSpec as P


HS = 64
WBLK = 256
EPS = 1e-05
F32 = jnp.float32
BF = jnp.bfloat16
NT = (((1,), (1,)), ((), ()))
TT = (((0,), (1,)), ((), ()))
VMEM_LIMIT = 24 * 1024 * 1024
SMALL = 60.0


def dot(a, b):
    return jnp.dot(a, b, preferred_element_type=F32)


def layer_norm(x):
    center = x - jnp.mean(x, axis=-1, keepdims=True)
    spread = jnp.mean(center * center, axis=-1, keepdims=True)
    return center * lax.rsqrt(spread + EPS)


def head_average(width):
    a = lax.broadcasted_iota(jnp.int32, (width, width), 0) // HS
    b = lax.broadcasted_iota(jnp.int32, (width, width), 1) // HS
    return jnp.where(a == b, 1.0 / HS, 0.0).astype(F32)


def split(x):
    high = x.astype(BF)
    return high, (x - high.astype(F32)).astype(BF)


def blocks_of(x, size=256):
    return [x[:, i : i + size] for i in range(0, x.shape[1], size)]


def join(parts):
    return parts[0] if len(parts) == 1 else jnp.concatenate(parts, axis=1)


def head_norm(x):
    out, top = [], []
    for y in blocks_of(x):
        avg = head_average(y.shape[1]).astype(BF)
        mean = dot(y, avg)
        center = y.astype(F32) - mean
        spread = dot((center * center).astype(BF), avg)
        out.append((center * lax.rsqrt(spread + EPS)).astype(BF))
        top.append(spread + mean * mean)
    return join(out), functools.reduce(jnp.maximum, top)


def head_sum(x):
    out = []
    for y in blocks_of(x):
        square = y.astype(F32) * y.astype(F32)
        out.append(dot(square.astype(BF), head_average(y.shape[1]).astype(BF)) * HS)
    return functools.reduce(jnp.maximum, out)


def head_norm_wide(x):
    avg = head_average(x.shape[1]).astype(BF)

    def mean(y):
        one = y.astype(BF)
        rest = y - one.astype(F32)
        two, three = split(rest)
        return dot(one, avg) + dot(two, avg) + dot(three, avg)

    center = x - mean(x)
    spread = mean(center * center)
    return (center * lax.rsqrt(spread + EPS)).astype(BF)


def lanes(shape):
    return lax.broadcasted_iota(jnp.int32, shape, len(shape) - 1)


def diagonal(size):
    return lax.broadcasted_iota(jnp.int32, (size, size), 0) == lax.broadcasted_iota(
        jnp.int32, (size, size), 1
    )


def to_row(column):
    size = column.shape[0]
    return jnp.sum(jnp.where(diagonal(size), column, 0.0), axis=0, keepdims=True)


def to_column(row):
    size = row.shape[1]
    return jnp.sum(jnp.where(diagonal(size), row, 0.0), axis=1, keepdims=True)


def place_in_seq():
    me = lax.axis_index("seq")
    return lax.rem(me, 2), lax.div(me, 2)


def project_kernel(sizes, tok_hbm, par_ref, w_hbm, wp_hbm, q_ref, nk_ref, nv_ref, wk_ref, wv_ref, top_ref, *rest):
    chips, owned, _, rank = sizes
    pays, (tok_ref, wq_ref, wp_ref, xn_ref, kk_ref, vv_ref, pay_ref, stat_ref, sem, out_sem) = rest[:chips], rest[chips:]
    rows, width = tok_ref.shape
    wide = q_ref.shape[1]
    heads = wide // HS
    core, chip = place_in_seq()
    mine = lambda which: w_hbm.at[:, pl.ds(pl.multiple_of(which * width + core * wide, wide), wide)]
    loads = [
        pltpu.make_async_copy(tok_hbm, tok_ref, sem.at[0]),
        pltpu.make_async_copy(mine(1), wk_ref, sem.at[1]),
        pltpu.make_async_copy(mine(2), wv_ref, sem.at[2]),
        pltpu.make_async_copy(wp_hbm.at[pl.ds(core * heads, heads)], wp_ref, sem.at[3]),
        pltpu.make_async_copy(mine(0), wq_ref, sem.at[4]),
    ]
    for load in loads:
        load.start()
    xn_ref[rows:] = layer_norm(par_ref[...].astype(F32)).astype(BF)
    stat_ref[...] = jnp.zeros_like(stat_ref)
    loads[0].wait()
    xn_ref[:rows] = layer_norm(tok_ref[...].astype(F32)).astype(BF)
    x = xn_ref[...]
    loads[1].wait()
    kk = dot(x, wk_ref[...]).astype(BF)
    kk_ref[...] = kk
    loads[2].wait()
    vv = dot(x, wv_ref[...]).astype(BF)
    vv_ref[...] = vv
    loads[3].wait()
    nk_ref[...], key_top = head_norm(kk)
    nv_ref[...], _ = head_norm(vv)
    loads[4].wait()
    query = (dot(x, wq_ref[...]).astype(BF).astype(F32) * HS ** (-0.5)).astype(BF)
    q_ref[...] = query
    top_ref[...] = jnp.broadcast_to(jnp.max(head_sum(query)), top_ref.shape)
    stat_rows = owned // 128

    def pair_sums(pair, shifted):
        cut = pl.ds(pl.multiple_of(pair * 128, 128), 128)
        kp, vp = kk_ref[:, cut], vv_ref[:, cut]
        turned = pltpu.roll(vp.astype(F32), 64, 1).astype(BF)
        low_half = lanes(kp.shape) < HS
        for side in range(2):
            mixed = jnp.where(low_half, kp, turned) if side == 0 else jnp.where(low_half, turned, kp)
            wp = wp_ref[pair * 2 + side]
            none = jnp.zeros_like(wp)
            wide_wp = jnp.concatenate([wp, none] if side == 0 else [none, wp], axis=0)
            logits = lax.dot_general(wide_wp, kp, TT, preferred_element_type=F32)
            if shifted:
                peak = jnp.max(logits, axis=1, keepdims=True)
                logits = logits - peak
            weight = jnp.exp(logits).astype(BF)
            total = jnp.sum(weight.astype(F32), axis=1, keepdims=True)
            sums = dot(weight, mixed).astype(BF)
            for part in range(rank // 128):
                column = (pair * 2 + side) * rank + part * 128
                owner, offset = column // owned, column % owned
                here = slice(part * 128, (part + 1) * 128)
                pay_ref[owner, pl.ds(pl.multiple_of(offset, 128), 128), :] = sums[here]
                entries = [(3, to_row(total[here]))]
                if shifted:
                    one = to_row(peak[here])
                    first = one.astype(BF).astype(F32)
                    second = (one - first).astype(BF).astype(F32)
                    entries += [(0, first), (1, second), (2, one - first - second)]
                for i, row in entries:
                    stat_ref[owner, pl.ds(i * stat_rows + offset // 128, 1), :] = row

    column_norm = jnp.max(jnp.sum(jnp.square(wp_ref[...].astype(F32)), axis=1))
    near_zero = jnp.max(key_top) * HS * column_norm < SMALL * SMALL

    @pl.when(near_zero)
    def _():
        for pair in range(heads // 2):
            pair_sums(pair, False)

    @pl.when(jnp.logical_not(near_zero))
    def _():
        def one(pair, carry):
            pair_sums(pair, True)
            return carry

        lax.fori_loop(0, heads // 2, one, 0)

    pay_ref[:, owned:, :] = stat_ref[...].astype(BF)
    copies = [
        pltpu.make_async_copy(pay_ref.at[lax.bitwise_xor(chip, k)], pays[k], out_sem.at[k]) for k in range(chips)
    ]
    for copy in copies:
        copy.start()
    for copy in copies:
        copy.wait()


def combine_kernel(sizes, *refs):
    chips, owned, extra = sizes
    pays, far_ref = refs[:chips], refs[chips]
    stat_rows = owned // 128
    tails = [p[owned : owned + extra, :].astype(F32) for p in pays]
    peaks = [
        t[:stat_rows] + t[stat_rows : 2 * stat_rows] + t[2 * stat_rows : 3 * stat_rows] for t in tails
    ]
    peak = functools.reduce(jnp.maximum, peaks)
    scales = [jnp.exp(p - peak) for p in peaks]
    total = sum(s * t[3 * stat_rows : 4 * stat_rows] for s, t in zip(scales, tails))
    scales = [s / total for s in scales]
    for i in range(stat_rows):
        cut = slice(i * 128, (i + 1) * 128)
        summary = sum(to_column(s[i : i + 1]) * p[cut, :].astype(F32) for s, p in zip(scales, pays))
        far_ref[cut, :] = head_norm_wide(summary)


def one_head(qp, side):
    low_half = lanes(qp.shape) < HS
    none = jnp.zeros_like(qp)
    return jnp.where(low_half, qp, none) if side == 0 else jnp.where(low_half, none, qp)


def with_ones(v, side):
    low_half = lanes(v.shape) < HS
    ones = jnp.ones_like(v)
    return jnp.where(low_half, v, ones) if side == 0 else jnp.where(low_half, ones, v)


def small_scores(top_ref):
    return jnp.max(top_ref[...]) * (HS * 1.02) < SMALL * SMALL


def near_kernel(group, top_ref, q_ref, nk_ref, nv_ref, *rest):
    if group == 0:
        halo_ref, halop_ref, wk_ref, wv_ref, o_ref, m_ref, hk_ref, hv_ref, xh_ref = rest
        half = halo_ref.shape[0]
        xh_ref[:half] = layer_norm(halo_ref[...].astype(F32)).astype(BF)
        xh_ref[half:] = layer_norm(halop_ref[...].astype(F32)).astype(BF)
        x = xh_ref[...]
        hk_ref[...], _ = head_norm(dot(x, wk_ref[...]).astype(BF))
        hv_ref[...], _ = head_norm(dot(x, wv_ref[...]).astype(BF))
    else:
        hk_ref, hv_ref, o_ref, m_ref = rest
    rows = hk_ref.shape[0] // 2
    heads = o_ref.shape[1] // 128
    me, n = lax.axis_index("seq"), lax.axis_size("seq")
    other = lax.bitwise_xor(me, 1)
    inside = [(i > 0) & (i < n - 1) for i in (me, other)]
    place = lanes((rows, 128))

    def attend(pair, shifted):
        cut = pl.ds(pl.multiple_of(group * heads * HS + pair * 128, 128), 128)
        kp = nk_ref[:, cut]
        for side in range(2):
            head = pair * 2 + side
            vp = with_ones(nv_ref[:, cut], side)
            for part in range(2):
                these = slice(part * rows, (part + 1) * rows)
                qm = one_head(q_ref[these, cut], side)
                main = lax.dot_general(qm, kp, NT, preferred_element_type=F32)
                halo = lax.dot_general(qm, hk_ref[these, cut], NT, preferred_element_type=F32)
                halo = halo + jnp.where(inside[part], 0.0, -jnp.inf).astype(F32)
                if shifted:
                    peak = jnp.maximum(
                        jnp.max(main, axis=1, keepdims=True), jnp.max(halo, axis=1, keepdims=True)
                    )
                    main, halo = main - peak, halo - peak
                    m_ref[these] = jnp.where(place == head, peak, m_ref[these])
                out = dot(jnp.exp(main).astype(BF), vp)
                out = out + dot(jnp.exp(halo).astype(BF), with_ones(hv_ref[these, cut], side))
                o_ref[these, pl.ds(pl.multiple_of(head * 128, 128), 128)] = out

    small = small_scores(top_ref)
    m_ref[...] = jnp.zeros_like(m_ref)

    @pl.when(small)
    def _():
        for pair in range(heads // 2):
            attend(pair, False)

    @pl.when(jnp.logical_not(small))
    def _():
        def one(pair, carry):
            attend(pair, True)
            return carry

        lax.fori_loop(0, heads // 2, one, 0)


def far_kernel(sizes, top_ref, q_ref, o_ref, m_ref, *rest):
    chips, owned, rank, group = sizes
    fars, (mine_ref, theirs_ref, all_ref) = rest[:chips], rest[chips:]
    rows = mine_ref.shape[0]
    heads = o_ref.shape[1] // 128
    _, chip = place_in_seq()
    for k in range(chips):
        source = lax.bitwise_xor(chip, k)
        all_ref[pl.ds(pl.multiple_of(source * owned, owned), owned), :] = fars[k][...]
    place = lanes((rows, 128))

    def attend(pair, shifted):
        cut = pl.ds(pl.multiple_of(group * heads * HS + pair * 128, 128), 128)
        low_half = lanes((rows, 128)) < HS
        for part in range(2):
            these = slice(part * rows, (part + 1) * rows)
            sums = []
            for side in range(2):
                qm = one_head(q_ref[these, cut], side)
                head = pair * 2 + side
                kv = all_ref[pl.ds(pl.multiple_of((group * heads + head) * rank, rank), rank), :]
                scores = lax.dot_general(qm, kv, NT, preferred_element_type=F32)
                before = o_ref[these, pl.ds(pl.multiple_of(head * 128, 128), 128)]
                if shifted:
                    peak = jnp.sum(jnp.where(place == head, m_ref[these], 0.0), axis=1, keepdims=True)
                    new = jnp.maximum(peak, jnp.max(scores, axis=1, keepdims=True))
                    scores = scores - new
                    before = before * jnp.exp(peak - new)
                out = dot(jnp.exp(scores).astype(BF), with_ones(kv, 1 - side))
                sums.append(before + pltpu.roll(out, 64, 1))
            total = pltpu.roll(jnp.where(low_half, sums[1], sums[0]), 64, 1)
            result = (jnp.where(low_half, sums[0], sums[1]) / total).astype(BF)
            (mine_ref, theirs_ref)[part][:, pl.ds(pl.multiple_of(pair * 128, 128), 128)] = result

    small = small_scores(top_ref)

    @pl.when(small)
    def _():
        for pair in range(heads // 2):
            attend(pair, False)

    @pl.when(jnp.logical_not(small))
    def _():
        def one(pair, carry):
            attend(pair, True)
            return carry

        lax.fori_loop(0, heads // 2, one, 0)


def mix_kernel(tok_ref, *rest):
    pieces, (w_ref, mixed_ref, yn_ref) = rest[:-3], rest[-3:]
    wide = pieces[0].shape[1]
    half = len(pieces) // 2
    total = 0.0
    core, _ = place_in_seq()
    for i, piece in enumerate(pieces):
        owner = core if i < half else 1 - core
        start = pl.multiple_of((owner * half + i % half) * wide, wide)
        total = total + dot(piece[...], w_ref[pl.ds(start, wide), :])
    mixed = (tok_ref[...].astype(F32) + total).astype(BF)
    mixed_ref[...] = mixed
    yn_ref[...] = layer_norm(mixed.astype(F32)).astype(BF)


def gelu(v):
    return 0.5 * v * (1.0 + jnp.tanh((2.0 / jnp.pi) ** 0.5 * (v + 0.044715 * (v * v * v))))


def folded(size):
    return [0] + list(range(1, size, 2)) + list(range(2, size, 2))[::-1]


def feed_kernel(parts, yn_ref, *rest):
    sides = len(rest[:-1]) // parts
    out_ref = rest[-1]
    depth = rest[0].shape[1]
    dp = lax.axis_index("dp")
    ring = folded(parts)
    starts = []
    for s in range(parts):
        block = sum(jnp.where(dp == ring[i], ring[(i - s) % parts], 0) for i in range(parts))
        starts.append(pl.multiple_of(block * depth, depth))
    hidden = []
    for side in range(sides):
        bufs = rest[side * parts : (side + 1) * parts]
        total = sum(dot(yn_ref[:, pl.ds(starts[i], depth)], bufs[i][0]) for i in range(parts))
        hidden.append(gelu(total).astype(BF))
    for i in range(parts):
        total = sum(
            lax.dot_general(hidden[side], rest[side * parts + i][1], NT, preferred_element_type=F32)
            for side in range(sides)
        )
        out_ref[:, pl.ds(starts[i], depth)] = total.astype(out_ref.dtype)


def call(kernel, in_specs, out_specs, out_shape, scratch=(), cost=(0, 0, 0)):
    return pl.pallas_call(
        kernel,
        in_specs=in_specs,
        out_specs=out_specs,
        scratch_shapes=scratch,
        out_shape=out_shape,
        compiler_params=pltpu.CompilerParams(vmem_limit_bytes=VMEM_LIMIT),
        cost_estimate=pl.CostEstimate(flops=cost[0], bytes_accessed=cost[1], transcendentals=cost[2]),
    )


def shape(dims, dtype=BF):
    return jax.ShapeDtypeStruct(dims, dtype)


def after(x, *earlier):
    return lax.optimization_barrier((x,) + earlier)[0]


def on_device(layer_input, w_qkv, w_out, w_proj, w_up, w_down):
    tokens = layer_input[0]
    rows, width = tokens.shape
    heads, _, rank = w_proj.shape
    n, parts = lax.axis_size("seq"), lax.axis_size("dp")
    chips = n // 2
    ring = folded(parts)
    follow = [(ring[i], ring[(i + 1) % parts]) for i in range(parts)]
    anywhere = pl.BlockSpec(memory_space=pl.ANY)
    hbm = lambda x: pltpu.with_memory_space_constraint(x, pltpu.HBM)
    vmem = pl.BlockSpec(memory_space=pltpu.VMEM)

    swap = lambda x: lax.ppermute(x, "seq", [(i, i ^ 1) for i in range(n)])
    jump = lambda x, k: lax.ppermute(x, "seq", [(i, i ^ (2 * k)) for i in range(n)])
    cross = lambda x, ks: lax.ppermute(x, "seq", [(i, i ^ (2 * ks[i % 2])) for i in range(n)])
    edges = [(i, i + 1) for i in range(1, n - 1, 2)]

    partner = swap(tokens)
    halo = lax.ppermute(tokens, "seq", edges + [(j, i) for i, j in edges])

    own = jnp.stack([w_up, w_down])
    gathered = [own]

    def gather_part(s, *earlier):
        if s < parts:
            gathered.append(lax.ppermute(after(gathered[-1], *earlier), "dp", follow))

    gather_part(1)
    share = (chips // 2, 1) if chips > 1 else ()
    shared = []

    def share_part(s, *earlier):
        if share and s < parts:
            shared.append(cross(after(gathered[s], *earlier) if earlier else gathered[s], share))

    share_part(0)

    half = heads // 2
    wide = half * HS
    block = 4 * HS
    steps = wide // block
    owned = half * rank // chips
    extra = max(16, 4 * owned // 128)
    hbm_space = pl.BlockSpec(memory_space=pltpu.HBM)
    out = call(
        functools.partial(project_kernel, (chips, owned, extra, rank)),
        [hbm_space, vmem, hbm_space, hbm_space],
        [vmem] * 6 + [anywhere] * chips,
        [shape((2 * rows, wide))] * 3
        + [shape((width, wide))] * 2
        + [shape((8, 128), F32)]
        + [shape((owned + extra, 128))] * chips,
        [
            pltpu.VMEM((rows, width), BF),
            pltpu.VMEM((width, wide), BF),
            pltpu.VMEM((half, HS, rank), BF),
            pltpu.VMEM((2 * rows, width), BF),
            pltpu.VMEM((2 * rows, wide), BF),
            pltpu.VMEM((2 * rows, wide), BF),
            pltpu.VMEM((chips, owned + extra, 128), BF),
            pltpu.VMEM((chips, extra, 128), F32),
            pltpu.SemaphoreType.DMA((5,)),
            pltpu.SemaphoreType.DMA((chips,)),
        ],
        (4 * rows * width * 3 * wide, 6 * width * wide, half * rank * 2 * rows),
    )(hbm(tokens), partner, hbm(w_qkv), hbm(w_proj))
    query, near_keys, near_values, w_key, w_value, top = out[:6]
    out = out[6:]
    pays = [out[0]]
    for k in range(1, chips):
        pays.append(jump(out[k], k))

    halo = after(halo, top)
    halo_partner = swap(halo)
    share_part(1, top)
    gather_part(2, top)
    halos, near = [halo, halo_partner, w_key, w_value], []

    def near_part(g, *earlier):
        kept = [shape((2 * rows, wide))] * 2 if g == 0 else []
        res = call(
            functools.partial(near_kernel, g),
            [vmem] * (4 + len(halos)),
            [vmem] * (2 + len(kept)),
            [shape((2 * rows, 2 * block), F32), shape((2 * rows, 128), F32)] + kept,
            [pltpu.VMEM((2 * rows, width), BF)] if g == 0 else [],
            (4 * rows * width * 2 * block, 4 * width * block, 4 * 3 * WBLK * 2 * rows),
        )(after(top, *earlier) if earlier else top, query, near_keys, near_values, *halos)
        near.append(res[:2])
        return res[2:]

    halos = near_part(0)
    pays = [after(p, near[0][0]) for p in pays]
    far = pl.pallas_call(
        functools.partial(combine_kernel, (chips, owned, extra)),
        out_shape=shape((owned, 128)),
        compiler_params=pltpu.CompilerParams(vmem_limit_bytes=VMEM_LIMIT),
        cost_estimate=pl.CostEstimate(flops=1000000, bytes_accessed=1000000, transcendentals=0),
    )(*pays)
    share_part(2, far)
    for s in range(3, parts):
        gather_part(s, far)
    fars = [far]
    for k in range(1, chips):
        fars.append(jump(far, k))
    for g in range(1, steps):
        near_part(g, far)
    fars = [after(x, near[-1][0]) for x in fars]
    pieces = []
    for g in range(steps):
        pieces.append(
            call(
                functools.partial(far_kernel, (chips, owned, rank, g)),
                [vmem] * (4 + chips),
                [vmem] * 2,
                [shape((rows, block))] * 2,
                [pltpu.VMEM((half * rank, 128), BF)],
                (4 * rows * block * rank * 2, 6 * rows * block, 4 * rank * 2 * rows),
            )(top, query, *near[g], *fars)
        )
    arrived = []
    for g in range(steps):
        arrived.append(swap(pieces[g][1]))
    theirs = pieces[-1][1]
    mixed, yn = call(
        mix_kernel,
        [vmem] * (2 + 2 * steps),
        [vmem] * 2,
        [shape((rows, width))] * 2,
        (),
        (4 * rows * width * wide, 2 * width * width, 0),
    )(tokens, *[piece[0] for piece in pieces], *arrived, w_out)
    for s in range(3, parts):
        share_part(s, yn)
    own_sides = list(gathered)
    for w in gathered:
        own_sides.append(swap(after(w, theirs)))

    def feed(x, dtype, weights):
        return call(
            functools.partial(feed_kernel, parts),
            [vmem] * (1 + len(weights)),
            vmem,
            shape((rows, width), dtype),
            (),
            (2 * rows * width * len(weights) * w_up.shape[1], len(weights) * own.size, rows * w_up.shape[1]),
        )(x, *weights)

    routes = list(zip(*[[k for k in range(1, chips) if not k & bit] for bit in share]))
    visitors = []
    for ks in routes:
        for which, route in enumerate((ks, ks[::-1])):
            visitors.append((which, route, cross(yn, route)))
    terms = [feed(yn, F32, own_sides)]
    mine_sides, their_sides = list(gathered), own_sides[parts:]
    if share:
        swapped = []
        for i, w in enumerate(shared):
            swapped.append(swap(after(w, theirs if i < 2 else terms[0])))
        mine_sides += shared
        their_sides = their_sides + swapped
    returned, last = [], yn
    for which, route, x in visitors:
        last = feed(after(x, terms[0]), BF, (mine_sides, their_sides)[which])
        returned.append(cross(last, route))
    if share:
        terms.append(feed(after(yn, last), F32, mine_sides[parts:] + their_sides[parts:]))
    result = mixed.astype(F32) + sum(terms)
    for x in returned:
        result = result + x.astype(F32)
    return result.astype(BF)[None]


def solution(mesh):
    in_specs = (P("dp", "seq", None), P(), P(), P(), P("dp", "seq"), P("dp", "seq"))
    out_specs = P("dp", "seq", None)
    return jax.shard_map(
        on_device, mesh=mesh, in_specs=in_specs, out_specs=out_specs, check_vma=False
    )
```

time: 132 us -> 96.9 us (0.73)
  waiting for transfers between devices: 60.4 us -> 30.6 us
  Pallas kernels: 40.6 us -> 31 us
  starting transfers between devices: 28.2 us -> 32.1 us
    ppermute x12 -> x6, waiting for transfers between devices: 54.5 us -> 0.19 us  [on_device(): lax.ppermute(x, 'seq', [(i, i ^ 2 * k) for i in range(n)])]
    ppermute x0 -> x8, waiting for transfers between devices: none -> 29.5 us  [on_device(): lax.ppermute(x, 'seq', [(i, i ^ 2 * ks[i % 2]) for i in range(n)])]
    pallas_call x7 -> x10, Pallas kernels: 39.9 us -> 30.3 us  [the longest x2 9.78 us: near_part(): call(functools.partial(near_kernel, g), [vmem] * (4 + len(halos)), [vmem]...]
    ppermute x0 -> x8, starting transfers between devices: none -> 8.54 us  [on_device(): lax.ppermute(x, 'seq', [(i, i ^ 2 * ks[i % 2]) for i in range(n)])]
    ppermute x12 -> x6, starting transfers between devices: 13.8 us -> 8.5 us  [on_device(): lax.ppermute(x, 'seq', [(i, i ^ 2 * k) for i in range(n)])]
    ppermute x11 -> x12, waiting for transfers between devices: 5.83 us -> 0.9 us  [on_device(): swap = lambda x: lax.ppermute(x, 'seq', [(i, i ^ 1) for i in range(n)])]
    ppermute x11 -> x12, starting transfers between devices: 4.88 us -> 5.47 us  [on_device(): swap = lambda x: lax.ppermute(x, 'seq', [(i, i ^ 1) for i in range(n)])]
  transfers between devices with their start and end apart: 27 -> 30, of which waited for: 13 -> 7; matrix products, arithmetic and copies ran while one was open for 1% -> 1% of each run, Pallas kernels for 29% -> 32%
where the time goes in v2:
time: 96.9 us; the launch traced here: 96.2 us
  starting transfers between devices  32.1 us (33%)
  Pallas kernels  31 us (32%)
  waiting for transfers between devices  30.6 us (32%)
  other arithmetic  2.28 us (2%)
    ppermute x8, waiting for transfers between devices, on_device(): lax.ppermute(x, 'seq', [(i, i ^ 2 * ks[i % 2]) for i in range(n)])  29.5 us
    pallas_call x2, Pallas kernels, near_part(): call(functools.partial(near_kernel, g), [vmem] * (4 + len(halos)), [vmem]...  9.78 us
    pallas_call x1, Pallas kernels, on_device(): call(functools.partial(project_kernel, (chips, owned, extra, rank)), [hbm...  9.02 us
    ppermute x3, starting transfers between devices, gather_part(): gathered.append(lax.ppermute(after(gathered[-1], *earlier), 'dp', follow))  8.89 us
    ppermute x8, starting transfers between devices, on_device(): lax.ppermute(x, 'seq', [(i, i ^ 2 * ks[i % 2]) for i in range(n)])  8.54 us
    ppermute x6, starting transfers between devices, on_device(): lax.ppermute(x, 'seq', [(i, i ^ 2 * k) for i in range(n)])  8.5 us
    pallas_call x4, Pallas kernels, feed(): call(functools.partial(feed_kernel, parts), [vmem] * (1 + len(weights)),...  5.85 us
    ppermute x12, starting transfers between devices, on_device(): swap = lambda x: lax.ppermute(x, 'seq', [(i, i ^ 1) for i in range(n)])  5.47 us
  transfers between devices with their start and end apart: 30, of which 7 were waited for; matrix products, arithmetic and copies ran while one was open for 1% of the time, Pallas kernels for 32%

profile of v2, /device:TPU:0, one launch (start us, length us, event | category | flops | bytes accessed | tf_op | source)
XLA Modules:
  0.0 96.2 jit_solution(3903998156841911344)
XLA Ops:
  1.2 1.1 %pad_maximum_fusion.rest_0_ = bf16[2,256,512]{2,1,0:T(8,128)(2,1)S(1)} fusion(bf16[1,256,512]{2,1,0:T(8,128)(2,1)} %bitcast.9, bf16[1,256,512]{2,1,0:T(8,128)(2,1)} %bitcast.10), kind=kLoop, calls=%fused_computation.2 | loop fusion | flops 262144 | bytes 1048576 | tf_op jit(solution)/shard_map/stack | solution.py:431
  2.3 2.6 %collective-permute-start.11 = (bf16[2,256,512]{2,1,0:T(8,128)(2,1)S(1)}, bf16[2,256,512]{2,1,0:T(8,128)(2,1)S(1)}, u32[]{:S(2)}, u32[]{:S(2)}) collective-permute-start(bf16[2,256,512]{2,1,0:T(8,128)(2,1)S(1)} %pad_maximum_fusion.rest_0_), channel_id=1, source_target_pairs={{0,8},{8,24},{24,16},{16,0},{1,9},{9,25},{25,17},{17,1},{2,10},{10... | collective-permute-start | bytes 1572872 | tf_op jit(solution)/shard_map/ppermute | solution.py:436
  4.9 9.0 %shard_map.64 = (bf16[512,512]{1,0:T(8,128)(2,1)S(1)}, bf16[512,512]{1,0:T(8,128)(2,1)S(1)}, bf16[512,512]{1,0:T(8,128)(2,1)S(1)}, bf16[1024,512]{1,0:T(8,128)(2...) custom-call(bf16[256,1024]{1,0:T(8,128)(2,1)} %bitcast.7, ...), custom_call_target="tpu_custom_call" | custom-call | flops 1610612736 | bytes 3145728 | tf_op jit(solution)/shard_map/pallas_call | solution.py:455
  13.9 2.8 %collective-permute-start.2 = (bf16[256,1024]{1,0:T(8,128)(2,1)S(1)}, bf16[256,1024]{1,0:T(8,128)(2,1)S(1)}, u32[]{:S(2)}, u32[]{:S(2)}) collective-permute-start(bf16[256,1024]{1,0:T(8,128)(2,1)S(1)} %collective-permute-done.1.rest_0_), channel_id=1, source_target_pairs={{0,1},{1,0},{2,3},{3,2},{4,5},{5,4},{6,7},{7,6},{8,9},{9,8},{10,11... | collective-permute-start | bytes 1572872 | tf_op jit(solution)/shard_map/ppermute | solution.py:423
  16.8 2.8 %collective-permute-start.12 = (bf16[2,256,512]{2,1,0:T(8,128)(2,1)S(1)}, bf16[2,256,512]{2,1,0:T(8,128)(2,1)S(1)}, u32[]{:S(2)}, u32[]{:S(2)}) collective-permute-start(bf16[2,256,512]{2,1,0:T(8,128)(2,1)S(1)} %collective-permute-done.11.rest_1_), channel_id=1, source_target_pairs={{0,8},{8,24},{24,16},{16,0},{1,9},{9,25},{25,17},{17,1},{2,10},{10... | collective-permute-start | bytes 1572872 | tf_op jit(solution)/shard_map/ppermute | solution.py:436
  19.6 2.2 %collective-permute-start.5 = (bf16[528,128]{1,0:T(8,128)(2,1)S(1)}, bf16[528,128]{1,0:T(8,128)(2,1)S(1)}, u32[]{:S(2)}, u32[]{:S(2)}) collective-permute-start(bf16[528,128]{1,0:T(8,128)(2,1)S(1)} %get-tuple-element.66), channel_id=1, source_target_pairs={{0,6},{1,7},{2,4},{3,5},{4,2},{5,3},{6,0},{7,1},{8,14},{9,15},{10,... | collective-permute-start | bytes 405512 | tf_op jit(solution)/shard_map/ppermute | solution.py:424
  21.8 2.8 %collective-permute-start.4 = (bf16[528,128]{1,0:T(8,128)(2,1)S(1)}, bf16[528,128]{1,0:T(8,128)(2,1)S(1)}, u32[]{:S(2)}, u32[]{:S(2)}) collective-permute-start(bf16[528,128]{1,0:T(8,128)(2,1)S(1)} %get-tuple-element.64), channel_id=1, source_target_pairs={{0,4},{1,5},{2,6},{3,7},{4,0},{5,1},{6,2},{7,3},{8,12},{9,13},{10,... | collective-permute-start | bytes 405512 | tf_op jit(solution)/shard_map/ppermute | solution.py:424
  24.6 2.0 %collective-permute-start.19 = (bf16[2,256,512]{2,1,0:T(8,128)(2,1)S(1)}, bf16[2,256,512]{2,1,0:T(8,128)(2,1)S(1)}, u32[]{:S(2)}, u32[]{:S(2)}) collective-permute-start(bf16[2,256,512]{2,1,0:T(8,128)(2,1)S(1)} %pad_maximum_fusion.rest_0_), channel_id=1, source_target_pairs={{0,4},{1,3},{2,6},{3,1},{4,0},{5,7},{6,2},{7,5},{8,12},{9,11},{10,... | collective-permute-start | bytes 1572872 | tf_op jit(solution)/shard_map/ppermute | solution.py:425
  26.7 6.1 %shard_map.65 = (f32[512,512]{1,0:T(8,128)S(1)}, f32[512,128]{1,0:T(8,128)S(1)}, bf16[512,512]{1,0:T(8,128)(2,1)S(1)}, bf16[512,512]{1,0:T(8,128)(2,1)S(1)}) custom-call(f32[8,128]{1,0:T(8,128)S(1)} %get-tuple-element.68.top_ref, bf16[512,512]{1,0:T(8,128)(2,1)S(1)} %get-tuple-element.52.q_ref, bf16[512,512]{1,0:T(8,128)(2,1)S(1)} %get-tuple-element.53.nk_ref, ...), custom_call_target="tpu_custom_call" | custom-call | flops 536870912 | bytes 1048576 | tf_op jit(solution)/shard_map/pallas_call | solution.py:491
  33.6 3.4 %collective-permute-start.13 = (bf16[2,256,512]{2,1,0:T(8,128)(2,1)S(1)}, bf16[2,256,512]{2,1,0:T(8,128)(2,1)S(1)}, u32[]{:S(2)}, u32[]{:S(2)}) collective-permute-start(bf16[2,256,512]{2,1,0:T(8,128)(2,1)S(1)} %collective-permute-done.12.rest_2_), channel_id=1, source_target_pairs={{0,8},{8,24},{24,16},{16,0},{1,9},{9,25},{25,17},{17,1},{2,10},{10... | collective-permute-start | bytes 1572872 | tf_op jit(solution)/shard_map/ppermute | solution.py:436
  37.0 1.4 %collective-permute-start.8 = (bf16[512,128]{1,0:T(8,128)(2,1)S(1)}, bf16[512,128]{1,0:T(8,128)(2,1)S(1)}, u32[]{:S(2)}, u32[]{:S(2)}) collective-permute-start(bf16[512,128]{1,0:T(8,128)(2,1)S(1)} %shard_map.66.rest_0_), channel_id=1, source_target_pairs={{0,6},{1,7},{2,4},{3,5},{4,2},{5,3},{6,0},{7,1},{8,14},{9,15},{10,... | collective-permute-start | bytes 393224 | tf_op jit(solution)/shard_map/ppermute | solution.py:424
  38.4 1.0 %collective-permute-start.7 = (bf16[512,128]{1,0:T(8,128)(2,1)S(1)}, bf16[512,128]{1,0:T(8,128)(2,1)S(1)}, u32[]{:S(2)}, u32[]{:S(2)}) collective-permute-start(bf16[512,128]{1,0:T(8,128)(2,1)S(1)} %shard_map.66.rest_0_), channel_id=1, source_target_pairs={{0,4},{1,5},{2,6},{3,7},{4,0},{5,1},{6,2},{7,3},{8,12},{9,13},{10,... | collective-permute-start | bytes 393224 | tf_op jit(solution)/shard_map/ppermute | solution.py:424
  39.4 1.1 %collective-permute-start.6 = (bf16[512,128]{1,0:T(8,128)(2,1)S(1)}, bf16[512,128]{1,0:T(8,128)(2,1)S(1)}, u32[]{:S(2)}, u32[]{:S(2)}) collective-permute-start(bf16[512,128]{1,0:T(8,128)(2,1)S(1)} %shard_map.66.rest_0_), channel_id=1, source_target_pairs={{0,2},{1,3},{2,0},{3,1},{4,6},{5,7},{6,4},{7,5},{8,10},{9,11},{10,... | collective-permute-start | bytes 393224 | tf_op jit(solution)/shard_map/ppermute | solution.py:424
  40.5 3.7 %shard_map.67 = (f32[512,512]{1,0:T(8,128)S(1)}, f32[512,128]{1,0:T(8,128)S(1)}) custom-call(f32[8,128]{1,0:T(8,128)S(1)} %get-tuple-element.68.top_ref, bf16[512,512]{1,0:T(8,128)(2,1)S(1)} %get-tuple-element.52.q_ref, bf16[512,512]{1,0:T(8,128)(2,1)S(1)} %get-tuple-element.53.nk_ref, bf16[512,512]{1,0:T(8,128)(2,1)S(1)} %get-tuple-element.54.nv_ref, ...), custom_call_target="tpu_custom_call" | custom-call | flops 536870912 | bytes 1048576 | tf_op jit(solution)/shard_map/pallas_call | solution.py:491
  44.5 2.2 %shard_map.69 = (bf16[256,256]{1,0:T(8,128)(2,1)S(1)}, bf16[256,256]{1,0:T(8,128)(2,1)S(1)}) custom-call(f32[8,128]{1,0:T(8,128)S(1)} %get-tuple-element.68.top_ref, bf16[512,512]{1,0:T(8,128)(2,1)S(1)} %get-tuple-element.52.q_ref, f32[512,512]{1,0:T(8,128)S(1)} %get-tuple-element.71.o_ref, f32[512,128]{1,0:T(8,128)S(1)} %get-tuple-element.77.m_ref, ...), custom_call_target="tpu_custom_call" | custom-call | flops 134217728 | bytes 393216 | tf_op jit(solution)/shard_map/pallas_call | solution.py:522
  47.3 2.4 %shard_map.68 = (bf16[256,256]{1,0:T(8,128)(2,1)S(1)}, bf16[256,256]{1,0:T(8,128)(2,1)S(1)}) custom-call(f32[8,128]{1,0:T(8,128)S(1)} %get-tuple-element.68.top_ref, bf16[512,512]{1,0:T(8,128)(2,1)S(1)} %get-tuple-element.52.q_ref, f32[512,512]{1,0:T(8,128)S(1)} %get-tuple-element.58.o_ref, f32[512,128]{1,0:T(8,128)S(1)} %get-tuple-element.59.m_ref, ...), custom_call_target="tpu_custom_call" | custom-call | flops 134217728 | bytes 393216 | tf_op jit(solution)/shard_map/pallas_call | solution.py:522
  51.7 1.0 %shard_map.70 = (bf16[256,1024]{1,0:T(8,128)(2,1)S(1)}, bf16[256,1024]{1,0:T(8,128)(2,1)S(1)}) custom-call(bf16[256,1024]{1,0:T(8,128)(2,1)S(1)} %bitcast.8, bf16[256,256]{1,0:T(8,128)(2,1)S(1)} %get-tuple-element.76.rest_0_, bf16[256,256]{1,0:T(8,128)(2,1)S(1)} %get-tuple-element.78.rest_1_, bf16[256,256]{1,0:T(8,128)(2,1)S(1)} %collective-permute-done.9.rest_2_, ...), custom_call_target="tpu_custom_call" | custom-call | flops 536870912 | bytes 2097152 | tf_op jit(solution)/shard_map/pallas_call | solution.py:535
  53.4 1.1 %collective-permute-start.25 = (bf16[2,256,512]{2,1,0:T(8,128)(2,1)S(1)}, bf16[2,256,512]{2,1,0:T(8,128)(2,1)S(1)}, u32[]{:S(2)}, u32[]{:S(2)}) collective-permute-start(bf16[2,256,512]{2,1,0:T(8,128)(2,1)S(1)} %collective-permute-done.13.rest_3_), channel_id=1, source_target_pairs={{0,4},{1,3},{2,6},{3,1},{4,0},{5,7},{6,2},{7,5},{8,12},{9,11},{10,... | collective-permute-start | bytes 1572872 | tf_op jit(solution)/shard_map/ppermute | solution.py:425
  54.5 0.9 collective-permute-start.23
  55.4 1.1 %collective-permute-start.27 = (bf16[256,1024]{1,0:T(8,128)(2,1)S(1)}, bf16[256,1024]{1,0:T(8,128)(2,1)S(1)}, u32[]{:S(2)}, u32[]{:S(2)}) collective-permute-start(bf16[256,1024]{1,0:T(8,128)(2,1)S(1)} %get-tuple-element.95.yn_ref), channel_id=1, source_target_pairs={{0,2},{1,5},{2,0},{3,7},{4,6},{5,1},{6,4},{7,3},{8,10},{9,13},{10,... | collective-permute-start | bytes 1572872 | tf_op jit(solution)/shard_map/ppermute | solution.py:425
  56.5 1.1 %collective-permute-start.18 = (bf16[256,1024]{1,0:T(8,128)(2,1)S(1)}, bf16[256,1024]{1,0:T(8,128)(2,1)S(1)}, u32[]{:S(2)}, u32[]{:S(2)}) collective-permute-start(bf16[256,1024]{1,0:T(8,128)(2,1)S(1)} %get-tuple-element.95.yn_ref), channel_id=1, source_target_pairs={{0,4},{1,3},{2,6},{3,1},{4,0},{5,7},{6,2},{7,5},{8,12},{9,11},{10,... | collective-permute-start | bytes 1572872 | tf_op jit(solution)/shard_map/ppermute | solution.py:425
  57.6 1.5 %shard_map.71 = f32[256,1024]{1,0:T(8,128)S(1)} custom-call(bf16[256,1024]{1,0:T(8,128)(2,1)S(1)} %get-tuple-element.95.yn_ref, bf16[2,256,512]{2,1,0:T(8,128)(2,1)S(1)} %pad_maximum_fusion.rest_0_, bf16[2,256,512]{2,1,0:T(8,128)(2,1)S(1)} %collective-permute-done.11.rest_1_, bf16[2,256,512]{2,1,0:T(8,128)(2,1)S(1)} %collective-permute-done.12.rest_2_, ...), custom_call_target="tpu_custom_call" | custom-call | flops 2147483648 | bytes 2097152 | tf_op jit(solution)/shard_map/pallas_call | solution.py:550
  59.1 9.0 %collective-permute-done.25.rest_3_.rest_7_ = bf16[2,256,512]{2,1,0:T(8,128)(2,1)S(1)} collective-permute-done((bf16[2,256,512]{2,1,0:T(8,128)(2,1)S(1)}, bf16[2,256,512]{2,1,0:T(8,128)(2,1)S(1)}, u32[]{:S(2)}, u32[]{:S(2)}) %collective-permute-start.25) | collective-permute-done | bytes 524320 | tf_op jit(solution)/shard_map/ppermute | solution.py:425
  68.1 5.7 %collective-permute-done.23.rest_2_.rest_6_ = bf16[2,256,512]{2,1,0:T(8,128)(2,1)S(1)} collective-permute-done((bf16[2,256,512]{2,1,0:T(8,128)(2,1)S(1)}, bf16[2,256,512]{2,1,0:T(8,128)(2,1)S(1)}, u32[]{:S(2)}, u32[]{:S(2)}) %collective-permute-start.23) | collective-permute-done | bytes 524320 | tf_op jit(solution)/shard_map/ppermute | solution.py:425
  74.3 5.1 %collective-permute-done.18.yn_ref = bf16[256,1024]{1,0:T(8,128)(2,1)S(1)} collective-permute-done((bf16[256,1024]{1,0:T(8,128)(2,1)S(1)}, bf16[256,1024]{1,0:T(8,128)(2,1)S(1)}, u32[]{:S(2)}, u32[]{:S(2)}) %collective-permute-start.18) | collective-permute-done | bytes 524320 | tf_op jit(solution)/shard_map/ppermute | solution.py:425
  79.4 1.5 %shard_map.74 = bf16[256,1024]{1,0:T(8,128)(2,1)S(1)} custom-call(bf16[256,1024]{1,0:T(8,128)(2,1)S(1)} %collective-permute-done.27.yn_ref, bf16[2,256,512]{2,1,0:T(8,128)(2,1)S(1)} %pad_maximum_fusion.rest_0_, bf16[2,256,512]{2,1,0:T(8,128)(2,1)S(1)} %collective-permute-done.11.rest_1_, bf16[2,256,512]{2,1,0:T(8,128)(2,1)S(1)} %collective-permute-done.12.rest_2_, ...), custom_call_target="tpu_custom_call" | custom-call | flops 2147483648 | bytes 2097152 | tf_op jit(solution)/shard_map/pallas_call | solution.py:550
  80.9 1.1 %collective-permute-start.28 = (bf16[256,1024]{1,0:T(8,128)(2,1)S(1)}, bf16[256,1024]{1,0:T(8,128)(2,1)S(1)}, u32[]{:S(2)}, u32[]{:S(2)}) collective-permute-start(bf16[256,1024]{1,0:T(8,128)(2,1)S(1)} %shard_map.74), channel_id=1, source_target_pairs={{0,2},{1,5},{2,0},{3,7},{4,6},{5,1},{6,4},{7,3},{8,10},{9,13},{10,... | collective-permute-start | bytes 1572872 | tf_op jit(solution)/shard_map/ppermute | solution.py:425
  82.1 1.5 %shard_map.72 = bf16[256,1024]{1,0:T(8,128)(2,1)S(1)} custom-call(bf16[256,1024]{1,0:T(8,128)(2,1)S(1)} %collective-permute-done.18.yn_ref, bf16[2,256,512]{2,1,0:T(8,128)(2,1)S(1)} %collective-permute-done.14.rest_4_.rest_0_, bf16[2,256,512]{2,1,0:T(8,128)(2,1)S(1)} %collective-permute-done.15.rest_5_.rest_1_, ...), custom_call_target="tpu_custom_call" | custom-call | flops 2147483648 | bytes 2097152 | tf_op jit(solution)/shard_map/pallas_call | solution.py:550
  83.6 1.1 %collective-permute-start.29 = (bf16[256,1024]{1,0:T(8,128)(2,1)S(1)}, bf16[256,1024]{1,0:T(8,128)(2,1)S(1)}, u32[]{:S(2)}, u32[]{:S(2)}) collective-permute-start(bf16[256,1024]{1,0:T(8,128)(2,1)S(1)} %shard_map.72), channel_id=1, source_target_pairs={{0,4},{1,3},{2,6},{3,1},{4,0},{5,7},{6,2},{7,5},{8,12},{9,11},{10,... | collective-permute-start | bytes 1572872 | tf_op jit(solution)/shard_map/ppermute | solution.py:425
  84.6 1.5 %shard_map.73 = f32[256,1024]{1,0:T(8,128)S(1)} custom-call(bf16[256,1024]{1,0:T(8,128)(2,1)S(1)} %get-tuple-element.95.yn_ref, bf16[2,256,512]{2,1,0:T(8,128)(2,1)S(1)} %collective-permute-done.19.rest_0_.rest_4_, bf16[2,256,512]{2,1,0:T(8,128)(2,1)S(1)} %collective-permute-done.21.rest_1_.rest_5_, ...), custom_call_target="tpu_custom_call" | custom-call | flops 2147483648 | bytes 2097152 | tf_op jit(solution)/shard_map/pallas_call | solution.py:550
  86.1 8.9 %collective-permute-done.28 = bf16[256,1024]{1,0:T(8,128)(2,1)S(1)} collective-permute-done((bf16[256,1024]{1,0:T(8,128)(2,1)S(1)}, bf16[256,1024]{1,0:T(8,128)(2,1)S(1)}, u32[]{:S(2)}, u32[]{:S(2)}) %collective-permute-start.28) | collective-permute-done | bytes 524320 | tf_op jit(solution)/shard_map/ppermute | solution.py:425
  95.0 1.2 %fusion = bf16[1,256,1024]{2,1,0:T(8,128)(2,1)} fusion(bf16[256,1024]{1,0:T(8,128)(2,1)S(1)} %collective-permute-done.29, bf16[256,1024]{1,0:T(8,128)(2,1)S(1)} %collective-permute-done.28, f32[256,1024]{1,0:T(8,128)S(1)} %shard_map.71, f32[256,1024]{1,0:T(8,128)S(1)} %shard_map.73, bf16[256,1024]{1,0:T(8,128)(2,1)S(1)} %get-tuple-element.81), kind=kLoop, calls=%fused_computation.1 | loop fusion | flops 2097152 | bytes 4194304 | tf_op jit(solution)/shard_map/broadcast_in_dim | solution.py:581
  (45 shorter events, 6.0 us)
Async XLA Ops:
  0.0 4.9 %collective-permute-start = (bf16[256,1024]{1,0:T(8,128)(2,1)}, bf16[256,1024]{1,0:T(8,128)(2,1)S(1)}, u32[]{:S(2)}, u32[]{:S(2)}) collective-permute-start(bf16[256,1024]{1,0:T(8,128)(2,1)} %bitcast.5), channel_id=1, source_target_pairs={{0,1},{1,0},{2,3},{3,2},{4,5},{5,4},{6,7},{7,6},{8,9},{9,8},{10,11... | collective-permute-start | bytes 1572872 | tf_op jit(solution)/shard_map/ppermute | solution.py:423
  0.5 13.4 %collective-permute-start.1 = (bf16[256,1024]{1,0:T(8,128)(2,1)}, bf16[256,1024]{1,0:T(8,128)(2,1)S(1)}, u32[]{:S(2)}, u32[]{:S(2)}) collective-permute-start(bf16[256,1024]{1,0:T(8,128)(2,1)} %bitcast.6), channel_id=1, source_target_pairs={{1,2},{3,4},{5,6},{2,1},{4,3},{6,5},{9,10},{11,12},{13,14},{10,9},... | collective-permute-start | bytes 1572872 | tf_op jit(solution)/shard_map/ppermute | solution.py:429
  2.3 14.5 %collective-permute-start.11 = (bf16[2,256,512]{2,1,0:T(8,128)(2,1)S(1)}, bf16[2,256,512]{2,1,0:T(8,128)(2,1)S(1)}, u32[]{:S(2)}, u32[]{:S(2)}) collective-permute-start(bf16[2,256,512]{2,1,0:T(8,128)(2,1)S(1)} %pad_maximum_fusion.rest_0_), channel_id=1, source_target_pairs={{0,8},{8,24},{24,16},{16,0},{1,9},{9,25},{25,17},{17,1},{2,10},{10... | collective-permute-start | bytes 1572872 | tf_op jit(solution)/shard_map/ppermute | solution.py:436
  13.9 10.7 %collective-permute-start.2 = (bf16[256,1024]{1,0:T(8,128)(2,1)S(1)}, bf16[256,1024]{1,0:T(8,128)(2,1)S(1)}, u32[]{:S(2)}, u32[]{:S(2)}) collective-permute-start(bf16[256,1024]{1,0:T(8,128)(2,1)S(1)} %collective-permute-done.1.rest_0_), channel_id=1, source_target_pairs={{0,1},{1,0},{2,3},{3,2},{4,5},{5,4},{6,7},{7,6},{8,9},{9,8},{10,11... | collective-permute-start | bytes 1572872 | tf_op jit(solution)/shard_map/ppermute | solution.py:423
  16.8 16.8 %collective-permute-start.12 = (bf16[2,256,512]{2,1,0:T(8,128)(2,1)S(1)}, bf16[2,256,512]{2,1,0:T(8,128)(2,1)S(1)}, u32[]{:S(2)}, u32[]{:S(2)}) collective-permute-start(bf16[2,256,512]{2,1,0:T(8,128)(2,1)S(1)} %collective-permute-done.11.rest_1_), channel_id=1, source_target_pairs={{0,8},{8,24},{24,16},{16,0},{1,9},{9,25},{25,17},{17,1},{2,10},{10... | collective-permute-start | bytes 1572872 | tf_op jit(solution)/shard_map/ppermute | solution.py:436
  19.6 13.2 %collective-permute-start.5 = (bf16[528,128]{1,0:T(8,128)(2,1)S(1)}, bf16[528,128]{1,0:T(8,128)(2,1)S(1)}, u32[]{:S(2)}, u32[]{:S(2)}) collective-permute-start(bf16[528,128]{1,0:T(8,128)(2,1)S(1)} %get-tuple-element.66), channel_id=1, source_target_pairs={{0,6},{1,7},{2,4},{3,5},{4,2},{5,3},{6,0},{7,1},{8,14},{9,15},{10,... | collective-permute-start | bytes 405512 | tf_op jit(solution)/shard_map/ppermute | solution.py:424
  21.8 11.0 %collective-permute-start.4 = (bf16[528,128]{1,0:T(8,128)(2,1)S(1)}, bf16[528,128]{1,0:T(8,128)(2,1)S(1)}, u32[]{:S(2)}, u32[]{:S(2)}) collective-permute-start(bf16[528,128]{1,0:T(8,128)(2,1)S(1)} %get-tuple-element.64), channel_id=1, source_target_pairs={{0,4},{1,5},{2,6},{3,7},{4,0},{5,1},{6,2},{7,3},{8,12},{9,13},{10,... | collective-permute-start | bytes 405512 | tf_op jit(solution)/shard_map/ppermute | solution.py:424
  24.6 8.2 %collective-permute-start.3 = (bf16[528,128]{1,0:T(8,128)(2,1)S(1)}, bf16[528,128]{1,0:T(8,128)(2,1)S(1)}, u32[]{:S(2)}, u32[]{:S(2)}) collective-permute-start(bf16[528,128]{1,0:T(8,128)(2,1)S(1)} %get-tuple-element.62), channel_id=1, source_target_pairs={{0,2},{1,3},{2,0},{3,1},{4,6},{5,7},{6,4},{7,5},{8,10},{9,11},{10,... | collective-permute-start | bytes 405512 | tf_op jit(solution)/shard_map/ppermute | solution.py:424
  24.6 25.1 %collective-permute-start.19 = (bf16[2,256,512]{2,1,0:T(8,128)(2,1)S(1)}, bf16[2,256,512]{2,1,0:T(8,128)(2,1)S(1)}, u32[]{:S(2)}, u32[]{:S(2)}) collective-permute-start(bf16[2,256,512]{2,1,0:T(8,128)(2,1)S(1)} %pad_maximum_fusion.rest_0_), channel_id=1, source_target_pairs={{0,4},{1,3},{2,6},{3,1},{4,0},{5,7},{6,2},{7,5},{8,12},{9,11},{10,... | collective-permute-start | bytes 1572872 | tf_op jit(solution)/shard_map/ppermute | solution.py:425
  26.7 25.0 %copy-start = (bf16[1024,1024]{1,0:T(8,128)(2,1)S(1)}, bf16[1024,1024]{1,0:T(8,128)(2,1)}, u32[]{:S(2)}) copy-start(bf16[1024,1024]{1,0:T(8,128)(2,1)} %rest_4_.1) | copy-start | bytes 6291460
  26.7 25.0 %copy-start.1 = (bf16[1,256,1024]{2,1,0:T(8,128)(2,1)S(1)}, bf16[1,256,1024]{2,1,0:T(8,128)(2,1)}, u32[]{:S(2)}) copy-start(bf16[1,256,1024]{2,1,0:T(8,128)(2,1)} %param.6) | copy-start | bytes 1572868
  33.6 16.3 %collective-permute-start.13 = (bf16[2,256,512]{2,1,0:T(8,128)(2,1)S(1)}, bf16[2,256,512]{2,1,0:T(8,128)(2,1)S(1)}, u32[]{:S(2)}, u32[]{:S(2)}) collective-permute-start(bf16[2,256,512]{2,1,0:T(8,128)(2,1)S(1)} %collective-permute-done.12.rest_2_), channel_id=1, source_target_pairs={{0,8},{8,24},{24,16},{16,0},{1,9},{9,25},{25,17},{17,1},{2,10},{10... | collective-permute-start | bytes 1572872 | tf_op jit(solution)/shard_map/ppermute | solution.py:436
  37.0 7.2 %collective-permute-start.8 = (bf16[512,128]{1,0:T(8,128)(2,1)S(1)}, bf16[512,128]{1,0:T(8,128)(2,1)S(1)}, u32[]{:S(2)}, u32[]{:S(2)}) collective-permute-start(bf16[512,128]{1,0:T(8,128)(2,1)S(1)} %shard_map.66.rest_0_), channel_id=1, source_target_pairs={{0,6},{1,7},{2,4},{3,5},{4,2},{5,3},{6,0},{7,1},{8,14},{9,15},{10,... | collective-permute-start | bytes 393224 | tf_op jit(solution)/shard_map/ppermute | solution.py:424
  38.4 6.1 %collective-permute-start.7 = (bf16[512,128]{1,0:T(8,128)(2,1)S(1)}, bf16[512,128]{1,0:T(8,128)(2,1)S(1)}, u32[]{:S(2)}, u32[]{:S(2)}) collective-permute-start(bf16[512,128]{1,0:T(8,128)(2,1)S(1)} %shard_map.66.rest_0_), channel_id=1, source_target_pairs={{0,4},{1,5},{2,6},{3,7},{4,0},{5,1},{6,2},{7,3},{8,12},{9,13},{10,... | collective-permute-start | bytes 393224 | tf_op jit(solution)/shard_map/ppermute | solution.py:424
  39.4 5.1 %collective-permute-start.6 = (bf16[512,128]{1,0:T(8,128)(2,1)S(1)}, bf16[512,128]{1,0:T(8,128)(2,1)S(1)}, u32[]{:S(2)}, u32[]{:S(2)}) collective-permute-start(bf16[512,128]{1,0:T(8,128)(2,1)S(1)} %shard_map.66.rest_0_), channel_id=1, source_target_pairs={{0,2},{1,3},{2,0},{3,1},{4,6},{5,7},{6,4},{7,5},{8,10},{9,11},{10,... | collective-permute-start | bytes 393224 | tf_op jit(solution)/shard_map/ppermute | solution.py:424
  44.2 9.2 %collective-permute-start.21 = (bf16[2,256,512]{2,1,0:T(8,128)(2,1)S(1)}, bf16[2,256,512]{2,1,0:T(8,128)(2,1)S(1)}, u32[]{:S(2)}, u32[]{:S(2)}) collective-permute-start(bf16[2,256,512]{2,1,0:T(8,128)(2,1)S(1)} %collective-permute-done.11.rest_1_), channel_id=1, source_target_pairs={{0,4},{1,3},{2,6},{3,1},{4,0},{5,7},{6,2},{7,5},{8,12},{9,11},{10,... | collective-permute-start | bytes 1572872 | tf_op jit(solution)/shard_map/ppermute | solution.py:425
  46.7 7.8 %collective-permute-start.14 = (bf16[2,256,512]{2,1,0:T(8,128)(2,1)S(1)}, bf16[2,256,512]{2,1,0:T(8,128)(2,1)S(1)}, u32[]{:S(2)}, u32[]{:S(2)}) collective-permute-start(bf16[2,256,512]{2,1,0:T(8,128)(2,1)S(1)} %pad_maximum_fusion.rest_0_), channel_id=1, source_target_pairs={{0,1},{1,0},{2,3},{3,2},{4,5},{5,4},{6,7},{7,6},{8,9},{9,8},{10,11... | collective-permute-start | bytes 1572872 | tf_op jit(solution)/shard_map/ppermute | solution.py:423
  46.8 8.6 %collective-permute-start.15 = (bf16[2,256,512]{2,1,0:T(8,128)(2,1)S(1)}, bf16[2,256,512]{2,1,0:T(8,128)(2,1)S(1)}, u32[]{:S(2)}, u32[]{:S(2)}) collective-permute-start(bf16[2,256,512]{2,1,0:T(8,128)(2,1)S(1)} %collective-permute-done.11.rest_1_), channel_id=1, source_target_pairs={{0,1},{1,0},{2,3},{3,2},{4,5},{5,4},{6,7},{7,6},{8,9},{9,8},{10,11... | collective-permute-start | bytes 1572872 | tf_op jit(solution)/shard_map/ppermute | solution.py:423
  49.8 1.4 %collective-permute-start.9 = (bf16[256,256]{1,0:T(8,128)(2,1)S(1)}, bf16[256,256]{1,0:T(8,128)(2,1)S(1)}, u32[]{:S(2)}, u32[]{:S(2)}) collective-permute-start(bf16[256,256]{1,0:T(8,128)(2,1)S(1)} %get-tuple-element.79), channel_id=1, source_target_pairs={{0,1},{1,0},{2,3},{3,2},{4,5},{5,4},{6,7},{7,6},{8,9},{9,8},{10,11... | collective-permute-start | bytes 393224 | tf_op jit(solution)/shard_map/ppermute | solution.py:423
  49.9 1.5 %collective-permute-start.10 = (bf16[256,256]{1,0:T(8,128)(2,1)S(1)}, bf16[256,256]{1,0:T(8,128)(2,1)S(1)}, u32[]{:S(2)}, u32[]{:S(2)}) collective-permute-start(bf16[256,256]{1,0:T(8,128)(2,1)S(1)} %get-tuple-element.80), channel_id=1, source_target_pairs={{0,1},{1,0},{2,3},{3,2},{4,5},{5,4},{6,7},{7,6},{8,9},{9,8},{10,11... | collective-permute-start | bytes 393224 | tf_op jit(solution)/shard_map/ppermute | solution.py:423
  51.2 5.4 %collective-permute-start.16 = (bf16[2,256,512]{2,1,0:T(8,128)(2,1)S(1)}, bf16[2,256,512]{2,1,0:T(8,128)(2,1)S(1)}, u32[]{:S(2)}, u32[]{:S(2)}) collective-permute-start(bf16[2,256,512]{2,1,0:T(8,128)(2,1)S(1)} %collective-permute-done.12.rest_2_), channel_id=1, source_target_pairs={{0,1},{1,0},{2,3},{3,2},{4,5},{5,4},{6,7},{7,6},{8,9},{9,8},{10,11... | collective-permute-start | bytes 1572872 | tf_op jit(solution)/shard_map/ppermute | solution.py:423
  51.4 5.2 %collective-permute-start.17 = (bf16[2,256,512]{2,1,0:T(8,128)(2,1)S(1)}, bf16[2,256,512]{2,1,0:T(8,128)(2,1)S(1)}, u32[]{:S(2)}, u32[]{:S(2)}) collective-permute-start(bf16[2,256,512]{2,1,0:T(8,128)(2,1)S(1)} %collective-permute-done.13.rest_3_), channel_id=1, source_target_pairs={{0,1},{1,0},{2,3},{3,2},{4,5},{5,4},{6,7},{7,6},{8,9},{9,8},{10,11... | collective-permute-start | bytes 1572872 | tf_op jit(solution)/shard_map/ppermute | solution.py:423
  53.4 14.7 %collective-permute-start.25 = (bf16[2,256,512]{2,1,0:T(8,128)(2,1)S(1)}, bf16[2,256,512]{2,1,0:T(8,128)(2,1)S(1)}, u32[]{:S(2)}, u32[]{:S(2)}) collective-permute-start(bf16[2,256,512]{2,1,0:T(8,128)(2,1)S(1)} %collective-permute-done.13.rest_3_), channel_id=1, source_target_pairs={{0,4},{1,3},{2,6},{3,1},{4,0},{5,7},{6,2},{7,5},{8,12},{9,11},{10,... | collective-permute-start | bytes 1572872 | tf_op jit(solution)/shard_map/ppermute | solution.py:425
  54.5 19.3 %collective-permute-start.23 = (bf16[2,256,512]{2,1,0:T(8,128)(2,1)S(1)}, bf16[2,256,512]{2,1,0:T(8,128)(2,1)S(1)}, u32[]{:S(2)}, u32[]{:S(2)}) collective-permute-start(bf16[2,256,512]{2,1,0:T(8,128)(2,1)S(1)} %collective-permute-done.12.rest_2_), channel_id=1, source_target_pairs={{0,4},{1,3},{2,6},{3,1},{4,0},{5,7},{6,2},{7,5},{8,12},{9,11},{10,... | collective-permute-start | bytes 1572872 | tf_op jit(solution)/shard_map/ppermute | solution.py:425
  55.4 18.4 %collective-permute-start.27 = (bf16[256,1024]{1,0:T(8,128)(2,1)S(1)}, bf16[256,1024]{1,0:T(8,128)(2,1)S(1)}, u32[]{:S(2)}, u32[]{:S(2)}) collective-permute-start(bf16[256,1024]{1,0:T(8,128)(2,1)S(1)} %get-tuple-element.95.yn_ref), channel_id=1, source_target_pairs={{0,2},{1,5},{2,0},{3,7},{4,6},{5,1},{6,4},{7,3},{8,10},{9,13},{10,... | collective-permute-start | bytes 1572872 | tf_op jit(solution)/shard_map/ppermute | solution.py:425
  56.5 25.5 %collective-permute-start.20 = (bf16[2,256,512]{2,1,0:T(8,128)(2,1)S(1)}, bf16[2,256,512]{2,1,0:T(8,128)(2,1)S(1)}, u32[]{:S(2)}, u32[]{:S(2)}) collective-permute-start(bf16[2,256,512]{2,1,0:T(8,128)(2,1)S(1)} %collective-permute-done.19.rest_0_.rest_4_), channel_id=1, source_target_pairs={{0,1},{1,0},{2,3},{3,2},{4,5},{5,4},{6,7},{7,6},{8,9},{9,8},{10,11... | collective-permute-start | bytes 1572872 | tf_op jit(solution)/shard_map/ppermute | solution.py:423
  56.5 22.9 %collective-permute-start.18 = (bf16[256,1024]{1,0:T(8,128)(2,1)S(1)}, bf16[256,1024]{1,0:T(8,128)(2,1)S(1)}, u32[]{:S(2)}, u32[]{:S(2)}) collective-permute-start(bf16[256,1024]{1,0:T(8,128)(2,1)S(1)} %get-tuple-element.95.yn_ref), channel_id=1, source_target_pairs={{0,4},{1,3},{2,6},{3,1},{4,0},{5,7},{6,2},{7,5},{8,12},{9,11},{10,... | collective-permute-start | bytes 1572872 | tf_op jit(solution)/shard_map/ppermute | solution.py:425
  68.1 14.0 %collective-permute-start.22 = (bf16[2,256,512]{2,1,0:T(8,128)(2,1)S(1)}, bf16[2,256,512]{2,1,0:T(8,128)(2,1)S(1)}, u32[]{:S(2)}, u32[]{:S(2)}) collective-permute-start(bf16[2,256,512]{2,1,0:T(8,128)(2,1)S(1)} %collective-permute-done.21.rest_1_.rest_5_), channel_id=1, source_target_pairs={{0,1},{1,0},{2,3},{3,2},{4,5},{5,4},{6,7},{7,6},{8,9},{9,8},{10,11... | collective-permute-start | bytes 1572872 | tf_op jit(solution)/shard_map/ppermute | solution.py:423
  73.8 8.2 %collective-permute-start.24 = (bf16[2,256,512]{2,1,0:T(8,128)(2,1)S(1)}, bf16[2,256,512]{2,1,0:T(8,128)(2,1)S(1)}, u32[]{:S(2)}, u32[]{:S(2)}) collective-permute-start(bf16[2,256,512]{2,1,0:T(8,128)(2,1)S(1)} %collective-permute-done.23.rest_2_.rest_6_), channel_id=1, source_target_pairs={{0,1},{1,0},{2,3},{3,2},{4,5},{5,4},{6,7},{7,6},{8,9},{9,8},{10,11... | collective-permute-start | bytes 1572872 | tf_op jit(solution)/shard_map/ppermute | solution.py:423
  73.8 8.2 %collective-permute-start.26 = (bf16[2,256,512]{2,1,0:T(8,128)(2,1)S(1)}, bf16[2,256,512]{2,1,0:T(8,128)(2,1)S(1)}, u32[]{:S(2)}, u32[]{:S(2)}) collective-permute-start(bf16[2,256,512]{2,1,0:T(8,128)(2,1)S(1)} %collective-permute-done.25.rest_3_.rest_7_), channel_id=1, source_target_pairs={{0,1},{1,0},{2,3},{3,2},{4,5},{5,4},{6,7},{7,6},{8,9},{9,8},{10,11... | collective-permute-start | bytes 1572872 | tf_op jit(solution)/shard_map/ppermute | solution.py:423
  80.9 14.1 %collective-permute-start.28 = (bf16[256,1024]{1,0:T(8,128)(2,1)S(1)}, bf16[256,1024]{1,0:T(8,128)(2,1)S(1)}, u32[]{:S(2)}, u32[]{:S(2)}) collective-permute-start(bf16[256,1024]{1,0:T(8,128)(2,1)S(1)} %shard_map.74), channel_id=1, source_target_pairs={{0,2},{1,5},{2,0},{3,7},{4,6},{5,1},{6,4},{7,3},{8,10},{9,13},{10,... | collective-permute-start | bytes 1572872 | tf_op jit(solution)/shard_map/ppermute | solution.py:425
  83.6 11.5 %collective-permute-start.29 = (bf16[256,1024]{1,0:T(8,128)(2,1)S(1)}, bf16[256,1024]{1,0:T(8,128)(2,1)S(1)}, u32[]{:S(2)}, u32[]{:S(2)}) collective-permute-start(bf16[256,1024]{1,0:T(8,128)(2,1)S(1)} %shard_map.72), channel_id=1, source_target_pairs={{0,4},{1,3},{2,6},{3,1},{4,0},{5,7},{6,2},{7,5},{8,12},{9,11},{10,... | collective-permute-start | bytes 1572872 | tf_op jit(solution)/shard_map/ppermute | solution.py:425

commit v3 on v2

--- a/solution.py
+++ b/solution.py
@@ -9,7 +9,6 @@
 
 
 HS = 64
-WBLK = 256
 EPS = 1e-05
 F32 = jnp.float32
 BF = jnp.bfloat16
@@ -17,6 +16,7 @@
 TT = (((0,), (1,)), ((), ()))
 VMEM_LIMIT = 24 * 1024 * 1024
 SMALL = 60.0
+CUTS = 2
 
 
 def dot(a, b):
@@ -235,49 +235,7 @@
     return jnp.max(top_ref[...]) * (HS * 1.02) < SMALL * SMALL
 
 
-def near_kernel(group, top_ref, q_ref, nk_ref, nv_ref, *rest):
-    if group == 0:
-        halo_ref, halop_ref, wk_ref, wv_ref, o_ref, m_ref, hk_ref, hv_ref, xh_ref = rest
-        half = halo_ref.shape[0]
-        xh_ref[:half] = layer_norm(halo_ref[...].astype(F32)).astype(BF)
-        xh_ref[half:] = layer_norm(halop_ref[...].astype(F32)).astype(BF)
-        x = xh_ref[...]
-        hk_ref[...], _ = head_norm(dot(x, wk_ref[...]).astype(BF))
-        hv_ref[...], _ = head_norm(dot(x, wv_ref[...]).astype(BF))
-    else:
-        hk_ref, hv_ref, o_ref, m_ref = rest
-    rows = hk_ref.shape[0] // 2
-    heads = o_ref.shape[1] // 128
-    me, n = lax.axis_index("seq"), lax.axis_size("seq")
-    other = lax.bitwise_xor(me, 1)
-    inside = [(i > 0) & (i < n - 1) for i in (me, other)]
-    place = lanes((rows, 128))
-
-    def attend(pair, shifted):
-        cut = pl.ds(pl.multiple_of(group * heads * HS + pair * 128, 128), 128)
-        kp = nk_ref[:, cut]
-        for side in range(2):
-            head = pair * 2 + side
-            vp = with_ones(nv_ref[:, cut], side)
-            for part in range(2):
-                these = slice(part * rows, (part + 1) * rows)
-                qm = one_head(q_ref[these, cut], side)
-                main = lax.dot_general(qm, kp, NT, preferred_element_type=F32)
-                halo = lax.dot_general(qm, hk_ref[these, cut], NT, preferred_element_type=F32)
-                halo = halo + jnp.where(inside[part], 0.0, -jnp.inf).astype(F32)
-                if shifted:
-                    peak = jnp.maximum(
-                        jnp.max(main, axis=1, keepdims=True), jnp.max(halo, axis=1, keepdims=True)
-                    )
-                    main, halo = main - peak, halo - peak
-                    m_ref[these] = jnp.where(place == head, peak, m_ref[these])
-                out = dot(jnp.exp(main).astype(BF), vp)
-                out = out + dot(jnp.exp(halo).astype(BF), with_ones(hv_ref[these, cut], side))
-                o_ref[these, pl.ds(pl.multiple_of(head * 128, 128), 128)] = out
-
-    small = small_scores(top_ref)
-    m_ref[...] = jnp.zeros_like(m_ref)
-
+def both_ways(small, heads, attend):
     @pl.when(small)
     def _():
         for pair in range(heads // 2):
@@ -292,11 +250,73 @@
         lax.fori_loop(0, heads // 2, one, 0)
 
 
+def pair_cut(pair):
+    return pl.ds(pl.multiple_of(pair * 128, 128), 128)
+
+
+def near_kernel(top_ref, q_ref, nk_ref, nv_ref, o_ref, m_ref):
+    rows = q_ref.shape[0] // 2
+    place = lanes((rows, 128))
+    m_ref[...] = jnp.zeros_like(m_ref)
+
+    def attend(pair, shifted):
+        cut = pair_cut(pair)
+        kp = nk_ref[:, cut]
+        for side in range(2):
+            vp = with_ones(nv_ref[:, cut], side)
+            for part in range(2):
+                these = slice(part * rows, (part + 1) * rows)
+                qm = one_head(q_ref[these, cut], side)
+                scores = lax.dot_general(qm, kp, NT, preferred_element_type=F32)
+                if shifted:
+                    peak = jnp.max(scores, axis=1, keepdims=True)
+                    scores = scores - peak
+                    m_ref[these] = jnp.where(place == pair * 2 + side, peak, m_ref[these])
+                o_ref[these, pair_cut(pair * 2 + side)] = dot(jnp.exp(scores).astype(BF), vp)
+
+    both_ways(small_scores(top_ref), nk_ref.shape[1] // HS, attend)
+
+
+def halo_kernel(top_ref, q_ref, before_ref, mb_ref, halo_ref, halop_ref, wk_ref, wv_ref, o_ref, m_ref, xh_ref, hk_ref, hv_ref):
+    rows = halo_ref.shape[0]
+    xh_ref[:rows] = layer_norm(halo_ref[...].astype(F32)).astype(BF)
+    xh_ref[rows:] = layer_norm(halop_ref[...].astype(F32)).astype(BF)
+    x = xh_ref[...]
+    hk_ref[...], _ = head_norm(dot(x, wk_ref[...]).astype(BF))
+    hv_ref[...], _ = head_norm(dot(x, wv_ref[...]).astype(BF))
+    me, n = lax.axis_index("seq"), lax.axis_size("seq")
+    other = lax.bitwise_xor(me, 1)
+    inside = [(i > 0) & (i < n - 1) for i in (me, other)]
+    place = lanes((rows, 128))
+    m_ref[...] = mb_ref[...]
+
+    def attend(pair, shifted):
+        cut = pair_cut(pair)
+        for side in range(2):
+            here = pair_cut(pair * 2 + side)
+            for part in range(2):
+                these = slice(part * rows, (part + 1) * rows)
+                qm = one_head(q_ref[these, cut], side)
+                scores = lax.dot_general(qm, hk_ref[these, cut], NT, preferred_element_type=F32)
+                scores = scores + jnp.where(inside[part], 0.0, -jnp.inf).astype(F32)
+                before = before_ref[these, here]
+                if shifted:
+                    head = place == pair * 2 + side
+                    peak = jnp.sum(jnp.where(head, mb_ref[these], 0.0), axis=1, keepdims=True)
+                    new = jnp.maximum(peak, jnp.max(scores, axis=1, keepdims=True))
+                    scores = scores - new
+                    before = before * jnp.exp(peak - new)
+                    m_ref[these] = jnp.where(head, new, m_ref[these])
+                o_ref[these, here] = before + dot(jnp.exp(scores).astype(BF), with_ones(hv_ref[these, cut], side))
+
+    both_ways(small_scores(top_ref), hk_ref.shape[1] // HS, attend)
+
+
 def far_kernel(sizes, top_ref, q_ref, o_ref, m_ref, *rest):
     chips, owned, rank, group = sizes
     fars, (mine_ref, theirs_ref, all_ref) = rest[:chips], rest[chips:]
     rows = mine_ref.shape[0]
-    heads = o_ref.shape[1] // 128
+    heads = mine_ref.shape[1] // HS
     _, chip = place_in_seq()
     for k in range(chips):
         source = lax.bitwise_xor(chip, k)
@@ -304,17 +324,18 @@
     place = lanes((rows, 128))
 
     def attend(pair, shifted):
-        cut = pl.ds(pl.multiple_of(group * heads * HS + pair * 128, 128), 128)
+        whole_pair = group * (heads // 2) + pair
+        cut = pair_cut(whole_pair)
         low_half = lanes((rows, 128)) < HS
         for part in range(2):
             these = slice(part * rows, (part + 1) * rows)
             sums = []
             for side in range(2):
                 qm = one_head(q_ref[these, cut], side)
-                head = pair * 2 + side
-                kv = all_ref[pl.ds(pl.multiple_of((group * heads + head) * rank, rank), rank), :]
+                head = whole_pair * 2 + side
+                kv = all_ref[pl.ds(pl.multiple_of(head * rank, rank), rank), :]
                 scores = lax.dot_general(qm, kv, NT, preferred_element_type=F32)
-                before = o_ref[these, pl.ds(pl.multiple_of(head * 128, 128), 128)]
+                before = o_ref[these, pair_cut(head)]
                 if shifted:
                     peak = jnp.sum(jnp.where(place == head, m_ref[these], 0.0), axis=1, keepdims=True)
                     new = jnp.maximum(peak, jnp.max(scores, axis=1, keepdims=True))
@@ -324,25 +345,13 @@
                 sums.append(before + pltpu.roll(out, 64, 1))
             total = pltpu.roll(jnp.where(low_half, sums[1], sums[0]), 64, 1)
             result = (jnp.where(low_half, sums[0], sums[1]) / total).astype(BF)
-            (mine_ref, theirs_ref)[part][:, pl.ds(pl.multiple_of(pair * 128, 128), 128)] = result
-
-    small = small_scores(top_ref)
-
-    @pl.when(small)
-    def _():
-        for pair in range(heads // 2):
-            attend(pair, False)
-
-    @pl.when(jnp.logical_not(small))
-    def _():
-        def one(pair, carry):
-            attend(pair, True)
-            return carry
-
-        lax.fori_loop(0, heads // 2, one, 0)
-
-
-def mix_kernel(tok_ref, *rest):
+            (mine_ref, theirs_ref)[part][:, pair_cut(pair)] = result
+
+    both_ways(small_scores(top_ref), heads, attend)
+
+
+def mix_kernel(cuts, tok_ref, *rest):
+    rest, cut_refs = rest[:-cuts], rest[-cuts:]
     pieces, (w_ref, mixed_ref, yn_ref) = rest[:-3], rest[-3:]
     wide = pieces[0].shape[1]
     half = len(pieces) // 2
@@ -354,7 +363,11 @@
         total = total + dot(piece[...], w_ref[pl.ds(start, wide), :])
     mixed = (tok_ref[...].astype(F32) + total).astype(BF)
     mixed_ref[...] = mixed
-    yn_ref[...] = layer_norm(mixed.astype(F32)).astype(BF)
+    yn = layer_norm(mixed.astype(F32)).astype(BF)
+    yn_ref[...] = yn
+    size = yn.shape[0] // cuts
+    for i, cut_ref in enumerate(cut_refs):
+        cut_ref[...] = yn[i * size : (i + 1) * size]
 
 
 def gelu(v):
@@ -365,9 +378,9 @@
     return [0] + list(range(1, size, 2)) + list(range(2, size, 2))[::-1]
 
 
-def feed_kernel(parts, yn_ref, *rest):
-    sides = len(rest[:-1]) // parts
-    out_ref = rest[-1]
+def feed_kernel(parts, added, yn_ref, *rest):
+    rest, more, out_ref = rest[: -1 - added], rest[-1 - added : -1], rest[-1]
+    sides = len(rest) // parts
     depth = rest[0].shape[1]
     dp = lax.axis_index("dp")
     ring = folded(parts)
@@ -385,6 +398,8 @@
             lax.dot_general(hidden[side], rest[side * parts + i][1], NT, preferred_element_type=F32)
             for side in range(sides)
         )
+        for ref in more:
+            total = total + ref[:, pl.ds(starts[i], depth)].astype(F32)
         out_ref[:, pl.ds(starts[i], depth)] = total.astype(out_ref.dtype)
 
 
@@ -443,7 +458,6 @@
         if share and s < parts:
             shared.append(cross(after(gathered[s], *earlier) if earlier else gathered[s], share))
 
-    share_part(0)
 
     half = heads // 2
     wide = half * HS
@@ -480,42 +494,45 @@
     for k in range(1, chips):
         pays.append(jump(out[k], k))
 
-    halo = after(halo, top)
-    halo_partner = swap(halo)
-    share_part(1, top)
     gather_part(2, top)
-    halos, near = [halo, halo_partner, w_key, w_value], []
-
-    def near_part(g, *earlier):
-        kept = [shape((2 * rows, wide))] * 2 if g == 0 else []
-        res = call(
-            functools.partial(near_kernel, g),
-            [vmem] * (4 + len(halos)),
-            [vmem] * (2 + len(kept)),
-            [shape((2 * rows, 2 * block), F32), shape((2 * rows, 128), F32)] + kept,
-            [pltpu.VMEM((2 * rows, width), BF)] if g == 0 else [],
-            (4 * rows * width * 2 * block, 4 * width * block, 4 * 3 * WBLK * 2 * rows),
-        )(after(top, *earlier) if earlier else top, query, near_keys, near_values, *halos)
-        near.append(res[:2])
-        return res[2:]
-
-    halos = near_part(0)
-    pays = [after(p, near[0][0]) for p in pays]
+    share_part(0, top)
+    near = call(
+        near_kernel,
+        [vmem] * 4,
+        [vmem] * 2,
+        [shape((2 * rows, 2 * wide), F32), shape((2 * rows, 128), F32)],
+        (),
+        (8 * rows * wide * 4 * rows, 8 * rows * wide, half * 2 * rows * 2 * rows),
+    )(top, query, near_keys, near_values)
+    pays = [after(p, near[0]) for p in pays]
     far = pl.pallas_call(
         functools.partial(combine_kernel, (chips, owned, extra)),
         out_shape=shape((owned, 128)),
         compiler_params=pltpu.CompilerParams(vmem_limit_bytes=VMEM_LIMIT),
         cost_estimate=pl.CostEstimate(flops=1000000, bytes_accessed=1000000, transcendentals=0),
     )(*pays)
-    share_part(2, far)
-    for s in range(3, parts):
-        gather_part(s, far)
+    share_part(1, far)
     fars = [far]
     for k in range(1, chips):
         fars.append(jump(far, k))
-    for g in range(1, steps):
-        near_part(g, far)
-    fars = [after(x, near[-1][0]) for x in fars]
+    halo = after(halo, far)
+    halo_partner = swap(halo)
+    near = call(
+        halo_kernel,
+        [vmem] * 8,
+        [vmem] * 2,
+        [shape((2 * rows, 2 * wide), F32), shape((2 * rows, 128), F32)],
+        [
+            pltpu.VMEM((2 * rows, width), BF),
+            pltpu.VMEM((2 * rows, wide), BF),
+            pltpu.VMEM((2 * rows, wide), BF),
+        ],
+        (4 * rows * width * 2 * wide, 4 * width * wide, half * rows * 2 * rows),
+    )(top, query, *near, halo, halo_partner, w_key, w_value)
+    share_part(2, near[0])
+    for s in range(3, parts):
+        gather_part(s, near[0])
+    fars = [after(x, near[0]) for x in fars]
     pieces = []
     for g in range(steps):
         pieces.append(
@@ -526,17 +543,17 @@
                 [shape((rows, block))] * 2,
                 [pltpu.VMEM((half * rank, 128), BF)],
                 (4 * rows * block * rank * 2, 6 * rows * block, 4 * rank * 2 * rows),
-            )(top, query, *near[g], *fars)
+            )(top, query, *near, *fars)
         )
     arrived = []
     for g in range(steps):
         arrived.append(swap(pieces[g][1]))
     theirs = pieces[-1][1]
-    mixed, yn = call(
-        mix_kernel,
+    mixed, yn, *yn_cuts = call(
+        functools.partial(mix_kernel, CUTS),
         [vmem] * (2 + 2 * steps),
-        [vmem] * 2,
-        [shape((rows, width))] * 2,
+        [vmem] * (2 + CUTS),
+        [shape((rows, width))] * 2 + [shape((rows // CUTS, width))] * CUTS,
         (),
         (4 * rows * width * wide, 2 * width * width, 0),
     )(tokens, *[piece[0] for piece in pieces], *arrived, w_out)
@@ -546,39 +563,42 @@
     for w in gathered:
         own_sides.append(swap(after(w, theirs)))
 
-    def feed(x, dtype, weights):
+    def feed(x, dtype, weights, *more):
         return call(
-            functools.partial(feed_kernel, parts),
-            [vmem] * (1 + len(weights)),
+            functools.partial(feed_kernel, parts, len(more)),
+            [vmem] * (1 + len(weights) + len(more)),
             vmem,
-            shape((rows, width), dtype),
+            shape(x.shape, dtype),
             (),
-            (2 * rows * width * len(weights) * w_up.shape[1], len(weights) * own.size, rows * w_up.shape[1]),
-        )(x, *weights)
+            (2 * x.size * len(weights) * w_up.shape[1], len(weights) * own.size, rows * w_up.shape[1]),
+        )(x, *weights, *more)
 
     routes = list(zip(*[[k for k in range(1, chips) if not k & bit] for bit in share]))
     visitors = []
-    for ks in routes:
-        for which, route in enumerate((ks, ks[::-1])):
-            visitors.append((which, route, cross(yn, route)))
-    terms = [feed(yn, F32, own_sides)]
+    for cut in yn_cuts:
+        for ks in routes:
+            for which, route in enumerate((ks, ks[::-1])):
+                visitors.append((which, route, cross(cut, route)))
+    total = feed(yn, F32, own_sides, mixed)
     mine_sides, their_sides = list(gathered), own_sides[parts:]
     if share:
         swapped = []
         for i, w in enumerate(shared):
-            swapped.append(swap(after(w, theirs if i < 2 else terms[0])))
+            swapped.append(swap(after(w, theirs if i < 2 else total)))
         mine_sides += shared
         their_sides = their_sides + swapped
-    returned, last = [], yn
+    returned, last = [], total
     for which, route, x in visitors:
-        last = feed(after(x, terms[0]), BF, (mine_sides, their_sides)[which])
-        returned.append(cross(last, route))
+        last = feed(after(x, last), BF, (mine_sides, their_sides)[which])
+        returned.append(cross(last, route).astype(F32))
     if share:
-        terms.append(feed(after(yn, last), F32, mine_sides[parts:] + their_sides[parts:]))
-    result = mixed.astype(F32) + sum(terms)
-    for x in returned:
-        result = result + x.astype(F32)
-    return result.astype(BF)[None]
+        total = feed(after(yn, last), F32, mine_sides[parts:] + their_sides[parts:], total)
+    if returned:
+        each = len(returned) // CUTS
+        total = total + jnp.concatenate(
+            [sum(returned[i * each : (i + 1) * each]) for i in range(CUTS)], axis=0
+        )
+    return total.astype(BF)[None]
 
 
 def solution(mesh):

time: 96.9 us -> 116 us (1.20)
  waiting for transfers between devices: 30.6 us -> 45.9 us
  Pallas kernels: 31 us -> 34.5 us
    ppermute x6, waiting for transfers between devices: 0.19 us -> 9.79 us  [on_device(): lax.ppermute(x, 'seq', [(i, i ^ 2 * k) for i in range(n)])]
    ppermute x3, waiting for transfers between devices: 0.01 us -> 6.58 us  [gather_part(): gathered.append(lax.ppermute(after(gathered[-1], *earlier), 'dp', follow))]
    ppermute x8 -> x12, starting transfers between devices: 8.54 us -> 12.7 us  [on_device(): lax.ppermute(x, 'seq', [(i, i ^ 2 * ks[i % 2]) for i in range(n)])]
    pallas_call x7 -> x9, Pallas kernels: 16.6 us -> 20.1 us  [the longest x6 7.67 us: feed(): call(functools.partial(feed_kernel, parts, len(more)), [vmem] * (1 + len(...]
    ppermute x12, starting transfers between devices: 5.47 us -> 2.76 us  [on_device(): swap = lambda x: lax.ppermute(x, 'seq', [(i, i ^ 1) for i in range(n)])]
    ppermute x3, starting transfers between devices: 8.89 us -> 7.09 us  [gather_part(): gathered.append(lax.ppermute(after(gathered[-1], *earlier), 'dp', follow))]
    ppermute x8 -> x12, waiting for transfers between devices: 29.5 us -> 29 us  [on_device(): lax.ppermute(x, 'seq', [(i, i ^ 2 * ks[i % 2]) for i in range(n)])]
  transfers between devices with their start and end apart: 30 -> 34, of which waited for: 7 -> 14; matrix products, arithmetic and copies ran while one was open for 1% -> 1% of each run, Pallas kernels for 32% -> 29%
where the time goes in v3:
time: 116 us; the launch traced here: 115 us
  waiting for transfers between devices  45.9 us (40%)
  Pallas kernels  34.5 us (30%)
  starting transfers between devices  32.5 us (28%)
  other arithmetic  2.14 us (2%)
    ppermute x12, waiting for transfers between devices, on_device(): lax.ppermute(x, 'seq', [(i, i ^ 2 * ks[i % 2]) for i in range(n)])  29 us
    ppermute x12, starting transfers between devices, on_device(): lax.ppermute(x, 'seq', [(i, i ^ 2 * ks[i % 2]) for i in range(n)])  12.7 us
    ppermute x6, waiting for transfers between devices, on_device(): lax.ppermute(x, 'seq', [(i, i ^ 2 * k) for i in range(n)])  9.79 us
    ppermute x6, starting transfers between devices, on_device(): lax.ppermute(x, 'seq', [(i, i ^ 2 * k) for i in range(n)])  9.28 us
    pallas_call x1, Pallas kernels, on_device(): call(functools.partial(project_kernel, (chips, owned, extra, rank)), [hbm...  9.02 us
    pallas_call x6, Pallas kernels, feed(): call(functools.partial(feed_kernel, parts, len(more)), [vmem] * (1 + len(...  7.67 us
    ppermute x3, starting transfers between devices, gather_part(): gathered.append(lax.ppermute(after(gathered[-1], *earlier), 'dp', follow))  7.09 us
    ppermute x3, waiting for transfers between devices, gather_part(): gathered.append(lax.ppermute(after(gathered[-1], *earlier), 'dp', follow))  6.58 us
  transfers between devices with their start and end apart: 34, of which 14 were waited for; matrix products, arithmetic and copies ran while one was open for 1% of the time, Pallas kernels for 29%

profile of v3, /device:TPU:0, one launch (start us, length us, event | category | flops | bytes accessed | tf_op | source)
XLA Modules:
  0.0 115.4 jit_solution(7826153287286974690)
XLA Ops:
  2.3 2.6 %collective-permute-start.15 = (bf16[2,256,512]{2,1,0:T(8,128)(2,1)S(1)}, bf16[2,256,512]{2,1,0:T(8,128)(2,1)S(1)}, u32[]{:S(2)}, u32[]{:S(2)}) collective-permute-start(bf16[2,256,512]{2,1,0:T(8,128)(2,1)S(1)} %pad_maximum_fusion.rest_0_), channel_id=1, source_target_pairs={{0,8},{8,24},{24,16},{16,0},{1,9},{9,25},{25,17},{17,1},{2,10},{10... | collective-permute-start | bytes 1572872 | tf_op jit(solution)/shard_map/ppermute | solution.py:451
  4.9 9.0 %shard_map.64 = (bf16[512,512]{1,0:T(8,128)(2,1)S(1)}, bf16[512,512]{1,0:T(8,128)(2,1)S(1)}, bf16[512,512]{1,0:T(8,128)(2,1)S(1)}, bf16[1024,512]{1,0:T(8,128)(2...) custom-call(bf16[256,1024]{1,0:T(8,128)(2,1)} %bitcast.7, ...), custom_call_target="tpu_custom_call" | custom-call | flops 1610612736 | bytes 3145728 | tf_op jit(solution)/shard_map/pallas_call | solution.py:469
  13.9 4.4 %collective-permute-start.4 = (bf16[528,128]{1,0:T(8,128)(2,1)S(1)}, bf16[528,128]{1,0:T(8,128)(2,1)S(1)}, u32[]{:S(2)}, u32[]{:S(2)}) collective-permute-start(bf16[528,128]{1,0:T(8,128)(2,1)S(1)} %get-tuple-element.66), channel_id=1, source_target_pairs={{0,6},{1,7},{2,4},{3,5},{4,2},{5,3},{6,0},{7,1},{8,14},{9,15},{10,... | collective-permute-start | bytes 405512 | tf_op jit(solution)/shard_map/ppermute | solution.py:439
  19.7 5.6 %shard_map.65 = (f32[512,1024]{1,0:T(8,128)S(1)}, f32[512,128]{1,0:T(8,128)S(1)}) custom-call(f32[8,128]{1,0:T(8,128)S(1)} %get-tuple-element.54.top_ref, bf16[512,512]{1,0:T(8,128)(2,1)S(1)} %get-tuple-element.55.q_ref, bf16[512,512]{1,0:T(8,128)(2,1)S(1)} %get-tuple-element.56.nk_ref, bf16[512,512]{1,0:T(8,128)(2,1)S(1)} %get-tuple-element.57.nv_ref), custom_call_target="tpu_custom_call" | custom-call | flops 1073741824 | bytes 1048576 | tf_op jit(solution)/shard_map/pallas_call | solution.py:499
  26.7 2.8 %collective-permute-start.16 = (bf16[2,256,512]{2,1,0:T(8,128)(2,1)S(1)}, bf16[2,256,512]{2,1,0:T(8,128)(2,1)S(1)}, u32[]{:S(2)}, u32[]{:S(2)}) collective-permute-start(bf16[2,256,512]{2,1,0:T(8,128)(2,1)S(1)} %collective-permute-done.15.rest_1_), channel_id=1, source_target_pairs={{0,8},{8,24},{24,16},{16,0},{1,9},{9,25},{25,17},{17,1},{2,10},{10... | collective-permute-start | bytes 1572872 | tf_op jit(solution)/shard_map/ppermute | solution.py:451
  29.5 5.8 %shard_map.67 = (f32[512,1024]{1,0:T(8,128)S(1)}, f32[512,128]{1,0:T(8,128)S(1)}) custom-call(f32[8,128]{1,0:T(8,128)S(1)} %get-tuple-element.54.top_ref, bf16[512,512]{1,0:T(8,128)(2,1)S(1)} %get-tuple-element.55.q_ref, f32[512,1024]{1,0:T(8,128)S(1)} %get-tuple-element.58.before_ref, f32[512,128]{1,0:T(8,128)S(1)} %get-tuple-element.59.mb_ref, ...), custom_call_target="tpu_custom_call" | custom-call | flops 1073741824 | bytes 2097152 | tf_op jit(solution)/shard_map/pallas_call | solution.py:520
  35.3 6.6 %collective-permute-done.16.rest_2_ = bf16[2,256,512]{2,1,0:T(8,128)(2,1)S(1)} collective-permute-done((bf16[2,256,512]{2,1,0:T(8,128)(2,1)S(1)}, bf16[2,256,512]{2,1,0:T(8,128)(2,1)S(1)}, u32[]{:S(2)}, u32[]{:S(2)}) %collective-permute-start.16) | collective-permute-done | bytes 524320 | tf_op jit(solution)/shard_map/ppermute | solution.py:451
  41.9 1.7 %collective-permute-start.17 = (bf16[2,256,512]{2,1,0:T(8,128)(2,1)S(1)}, bf16[2,256,512]{2,1,0:T(8,128)(2,1)S(1)}, u32[]{:S(2)}, u32[]{:S(2)}) collective-permute-start(bf16[2,256,512]{2,1,0:T(8,128)(2,1)S(1)} %collective-permute-done.16.rest_2_), channel_id=1, source_target_pairs={{0,8},{8,24},{24,16},{16,0},{1,9},{9,25},{25,17},{17,1},{2,10},{10... | collective-permute-start | bytes 1572872 | tf_op jit(solution)/shard_map/ppermute | solution.py:451
  43.6 1.6 %collective-permute-start.22 = (bf16[2,256,512]{2,1,0:T(8,128)(2,1)S(1)}, bf16[2,256,512]{2,1,0:T(8,128)(2,1)S(1)}, u32[]{:S(2)}, u32[]{:S(2)}) collective-permute-start(bf16[2,256,512]{2,1,0:T(8,128)(2,1)S(1)} %pad_maximum_fusion.rest_0_), channel_id=1, source_target_pairs={{0,4},{1,3},{2,6},{3,1},{4,0},{5,7},{6,2},{7,5},{8,12},{9,11},{10,... | collective-permute-start | bytes 1572872 | tf_op jit(solution)/shard_map/ppermute | solution.py:440
  45.2 1.3 %collective-permute-start.8 = (bf16[512,128]{1,0:T(8,128)(2,1)S(1)}, bf16[512,128]{1,0:T(8,128)(2,1)S(1)}, u32[]{:S(2)}, u32[]{:S(2)}) collective-permute-start(bf16[512,128]{1,0:T(8,128)(2,1)S(1)} %shard_map.66.rest_0_), channel_id=1, source_target_pairs={{0,6},{1,7},{2,4},{3,5},{4,2},{5,3},{6,0},{7,1},{8,14},{9,15},{10,... | collective-permute-start | bytes 393224 | tf_op jit(solution)/shard_map/ppermute | solution.py:439
  47.2 1.4 %collective-permute-start.6 = (bf16[512,128]{1,0:T(8,128)(2,1)S(1)}, bf16[512,128]{1,0:T(8,128)(2,1)S(1)}, u32[]{:S(2)}, u32[]{:S(2)}) collective-permute-start(bf16[512,128]{1,0:T(8,128)(2,1)S(1)} %shard_map.66.rest_0_), channel_id=1, source_target_pairs={{0,2},{1,3},{2,0},{3,1},{4,6},{5,7},{6,4},{7,5},{8,10},{9,11},{10,... | collective-permute-start | bytes 393224 | tf_op jit(solution)/shard_map/ppermute | solution.py:439
  48.7 3.8 %collective-permute-done.8.rest_3_ = bf16[512,128]{1,0:T(8,128)(2,1)S(1)} collective-permute-done((bf16[512,128]{1,0:T(8,128)(2,1)S(1)}, bf16[512,128]{1,0:T(8,128)(2,1)S(1)}, u32[]{:S(2)}, u32[]{:S(2)}) %collective-permute-start.8) | collective-permute-done | bytes 131104 | tf_op jit(solution)/shard_map/ppermute | solution.py:439
  52.9 5.5 %collective-permute-done.7.rest_2_ = bf16[512,128]{1,0:T(8,128)(2,1)S(1)} collective-permute-done((bf16[512,128]{1,0:T(8,128)(2,1)S(1)}, bf16[512,128]{1,0:T(8,128)(2,1)S(1)}, u32[]{:S(2)}, u32[]{:S(2)}) %collective-permute-start.7) | collective-permute-done | bytes 131104 | tf_op jit(solution)/shard_map/ppermute | solution.py:439
  58.4 2.2 %shard_map.69 = (bf16[256,256]{1,0:T(8,128)(2,1)S(1)}, bf16[256,256]{1,0:T(8,128)(2,1)S(1)}) custom-call(f32[8,128]{1,0:T(8,128)S(1)} %get-tuple-element.54.top_ref, bf16[512,512]{1,0:T(8,128)(2,1)S(1)} %get-tuple-element.55.q_ref, f32[512,1024]{1,0:T(8,128)S(1)} %get-tuple-element.71.o_ref, f32[512,128]{1,0:T(8,128)S(1)} %get-tuple-element.72.m_ref, ...), custom_call_target="tpu_custom_call" | custom-call | flops 134217728 | bytes 393216 | tf_op jit(solution)/shard_map/pallas_call | solution.py:539
  60.7 2.4 %shard_map.68 = (bf16[256,256]{1,0:T(8,128)(2,1)S(1)}, bf16[256,256]{1,0:T(8,128)(2,1)S(1)}) custom-call(f32[8,128]{1,0:T(8,128)S(1)} %get-tuple-element.54.top_ref, bf16[512,512]{1,0:T(8,128)(2,1)S(1)} %get-tuple-element.55.q_ref, f32[512,1024]{1,0:T(8,128)S(1)} %get-tuple-element.71.o_ref, f32[512,128]{1,0:T(8,128)S(1)} %get-tuple-element.72.m_ref, ...), custom_call_target="tpu_custom_call" | custom-call | flops 134217728 | bytes 393216 | tf_op jit(solution)/shard_map/pallas_call | solution.py:539
  66.3 1.1 collective-permute-start.24
  68.9 1.2 %collective-permute-start.14 = (bf16[128,1024]{1,0:T(8,128)(2,1)S(1)}, bf16[128,1024]{1,0:T(8,128)(2,1)S(1)}, u32[]{:S(2)}, u32[]{:S(2)}) collective-permute-start(bf16[128,1024]{1,0:T(8,128)(2,1)S(1)} %get-tuple-element.83), channel_id=1, source_target_pairs={{0,2},{1,5},{2,0},{3,7},{4,6},{5,1},{6,4},{7,3},{8,10},{9,13},{10,... | collective-permute-start | bytes 786440 | tf_op jit(solution)/shard_map/ppermute | solution.py:440
  70.1 1.5 %shard_map.71.rest_8_ = f32[256,1024]{1,0:T(8,128)S(1)} custom-call(bf16[256,1024]{1,0:T(8,128)(2,1)S(1)} %get-tuple-element.102.yn_ref, bf16[2,256,512]{2,1,0:T(8,128)(2,1)S(1)} %pad_maximum_fusion.rest_0_, bf16[2,256,512]{2,1,0:T(8,128)(2,1)S(1)} %collective-permute-done.15.rest_1_, bf16[2,256,512]{2,1,0:T(8,128)(2,1)S(1)} %collective-permute-done.16.rest_2_, ...), custom_call_target="tpu_custom_call" | custom-call | flops 2147483648 | bytes 2097152 | tf_op jit(solution)/shard_map/pallas_call | solution.py:567
  71.6 6.7 %collective-permute-done.24.rest_6_.rest_2_ = bf16[2,256,512]{2,1,0:T(8,128)(2,1)S(1)} collective-permute-done((bf16[2,256,512]{2,1,0:T(8,128)(2,1)S(1)}, bf16[2,256,512]{2,1,0:T(8,128)(2,1)S(1)}, u32[]{:S(2)}, u32[]{:S(2)}) %collective-permute-start.24) | collective-permute-done | bytes 524320 | tf_op jit(solution)/shard_map/ppermute | solution.py:440
  78.3 5.6 %collective-permute-done.25.rest_7_.rest_3_ = bf16[2,256,512]{2,1,0:T(8,128)(2,1)S(1)} collective-permute-done((bf16[2,256,512]{2,1,0:T(8,128)(2,1)S(1)}, bf16[2,256,512]{2,1,0:T(8,128)(2,1)S(1)}, u32[]{:S(2)}, u32[]{:S(2)}) %collective-permute-start.25) | collective-permute-done | bytes 524320 | tf_op jit(solution)/shard_map/ppermute | solution.py:440
  84.0 1.1 collective-permute-start.13
  85.0 5.3 %collective-permute-done.13.yn_ref = bf16[128,1024]{1,0:T(8,128)(2,1)S(1)} collective-permute-done((bf16[128,1024]{1,0:T(8,128)(2,1)S(1)}, bf16[128,1024]{1,0:T(8,128)(2,1)S(1)}, u32[]{:S(2)}, u32[]{:S(2)}) %collective-permute-start.13) | collective-permute-done | bytes 262176 | tf_op jit(solution)/shard_map/ppermute | solution.py:440
  90.3 1.2 %collective-permute-start.12 = (bf16[128,1024]{1,0:T(8,128)(2,1)S(1)}, bf16[128,1024]{1,0:T(8,128)(2,1)S(1)}, u32[]{:S(2)}, u32[]{:S(2)}) collective-permute-start(bf16[128,1024]{1,0:T(8,128)(2,1)S(1)} %get-tuple-element.82), channel_id=1, source_target_pairs={{0,2},{1,5},{2,0},{3,7},{4,6},{5,1},{6,4},{7,3},{8,10},{9,13},{10,... | collective-permute-start | bytes 786440 | tf_op jit(solution)/shard_map/ppermute | solution.py:440
  92.5 1.2 %shard_map.72 = bf16[128,1024]{1,0:T(8,128)(2,1)S(1)} custom-call(bf16[128,1024]{1,0:T(8,128)(2,1)S(1)} %collective-permute-done.14.yn_ref, bf16[2,256,512]{2,1,0:T(8,128)(2,1)S(1)} %pad_maximum_fusion.rest_0_, bf16[2,256,512]{2,1,0:T(8,128)(2,1)S(1)} %collective-permute-done.15.rest_1_, bf16[2,256,512]{2,1,0:T(8,128)(2,1)S(1)} %collective-permute-done.16.rest_2_, ...), custom_call_target="tpu_custom_call" | custom-call | flops 1073741824 | bytes 2097152 | tf_op jit(solution)/shard_map/pallas_call | solution.py:567
  93.7 1.2 %shard_map.73 = bf16[128,1024]{1,0:T(8,128)(2,1)S(1)} custom-call(bf16[128,1024]{1,0:T(8,128)(2,1)S(1)} %collective-permute-done.13.yn_ref, bf16[2,256,512]{2,1,0:T(8,128)(2,1)S(1)} %collective-permute-done.18.rest_4_.rest_0_, bf16[2,256,512]{2,1,0:T(8,128)(2,1)S(1)} %collective-permute-done.19.rest_5_.rest_1_, ...), custom_call_target="tpu_custom_call" | custom-call | flops 1073741824 | bytes 2097152 | tf_op jit(solution)/shard_map/pallas_call | solution.py:567
  94.9 4.1 %collective-permute-done.12.yn_ref = bf16[128,1024]{1,0:T(8,128)(2,1)S(1)} collective-permute-done((bf16[128,1024]{1,0:T(8,128)(2,1)S(1)}, bf16[128,1024]{1,0:T(8,128)(2,1)S(1)}, u32[]{:S(2)}, u32[]{:S(2)}) %collective-permute-start.12) | collective-permute-done | bytes 262176 | tf_op jit(solution)/shard_map/ppermute | solution.py:440
  99.0 1.2 %shard_map.74 = bf16[128,1024]{1,0:T(8,128)(2,1)S(1)} custom-call(bf16[128,1024]{1,0:T(8,128)(2,1)S(1)} %collective-permute-done.12.yn_ref, bf16[2,256,512]{2,1,0:T(8,128)(2,1)S(1)} %pad_maximum_fusion.rest_0_, bf16[2,256,512]{2,1,0:T(8,128)(2,1)S(1)} %collective-permute-done.15.rest_1_, bf16[2,256,512]{2,1,0:T(8,128)(2,1)S(1)} %collective-permute-done.16.rest_2_, ...), custom_call_target="tpu_custom_call" | custom-call | flops 1073741824 | bytes 2097152 | tf_op jit(solution)/shard_map/pallas_call | solution.py:567
  100.2 1.2 %shard_map.75 = bf16[128,1024]{1,0:T(8,128)(2,1)S(1)} custom-call(bf16[128,1024]{1,0:T(8,128)(2,1)S(1)} %collective-permute-done.11.yn_ref, bf16[2,256,512]{2,1,0:T(8,128)(2,1)S(1)} %collective-permute-done.18.rest_4_.rest_0_, bf16[2,256,512]{2,1,0:T(8,128)(2,1)S(1)} %collective-permute-done.19.rest_5_.rest_1_, ...), custom_call_target="tpu_custom_call" | custom-call | flops 1073741824 | bytes 2097152 | tf_op jit(solution)/shard_map/pallas_call | solution.py:567
  102.4 1.2 %collective-permute-start.32 = (bf16[128,1024]{1,0:T(8,128)(2,1)S(1)}, bf16[128,1024]{1,0:T(8,128)(2,1)S(1)}, u32[]{:S(2)}, u32[]{:S(2)}) collective-permute-start(bf16[128,1024]{1,0:T(8,128)(2,1)S(1)} %shard_map.74), channel_id=1, source_target_pairs={{0,2},{1,5},{2,0},{3,7},{4,6},{5,1},{6,4},{7,3},{8,10},{9,13},{10,... | collective-permute-start | bytes 786440 | tf_op jit(solution)/shard_map/ppermute | solution.py:440
  105.5 1.5 %shard_map.76 = f32[256,1024]{1,0:T(8,128)S(1)} custom-call(bf16[256,1024]{1,0:T(8,128)(2,1)S(1)} %get-tuple-element.102.yn_ref, bf16[2,256,512]{2,1,0:T(8,128)(2,1)S(1)} %collective-permute-done.22.rest_4_.rest_0_, bf16[2,256,512]{2,1,0:T(8,128)(2,1)S(1)} %collective-permute-done.23.rest_5_.rest_1_, ...), custom_call_target="tpu_custom_call" | custom-call | flops 2147483648 | bytes 2097152 | tf_op jit(solution)/shard_map/pallas_call | solution.py:567
  107.0 3.6 %collective-permute-done.33 = bf16[128,1024]{1,0:T(8,128)(2,1)S(1)} collective-permute-done((bf16[128,1024]{1,0:T(8,128)(2,1)S(1)}, bf16[128,1024]{1,0:T(8,128)(2,1)S(1)}, u32[]{:S(2)}, u32[]{:S(2)}) %collective-permute-start.33) | collective-permute-done | bytes 262176 | tf_op jit(solution)/shard_map/ppermute | solution.py:440
  111.0 2.7 %collective-permute-done.30 = bf16[128,1024]{1,0:T(8,128)(2,1)S(1)} collective-permute-done((bf16[128,1024]{1,0:T(8,128)(2,1)S(1)}, bf16[128,1024]{1,0:T(8,128)(2,1)S(1)}, u32[]{:S(2)}, u32[]{:S(2)}) %collective-permute-start.30) | collective-permute-done | bytes 262176 | tf_op jit(solution)/shard_map/ppermute | solution.py:440
  (57 shorter events, 16.6 us)
Async XLA Ops:
  0.0 4.9 %collective-permute-start = (bf16[256,1024]{1,0:T(8,128)(2,1)}, bf16[256,1024]{1,0:T(8,128)(2,1)S(1)}, u32[]{:S(2)}, u32[]{:S(2)}) collective-permute-start(bf16[256,1024]{1,0:T(8,128)(2,1)} %bitcast.5), channel_id=1, source_target_pairs={{0,1},{1,0},{2,3},{3,2},{4,5},{5,4},{6,7},{7,6},{8,9},{9,8},{10,11... | collective-permute-start | bytes 1572872 | tf_op jit(solution)/shard_map/ppermute | solution.py:438
  0.5 26.1 %collective-permute-start.1 = (bf16[256,1024]{1,0:T(8,128)(2,1)}, bf16[256,1024]{1,0:T(8,128)(2,1)S(1)}, u32[]{:S(2)}, u32[]{:S(2)}) collective-permute-start(bf16[256,1024]{1,0:T(8,128)(2,1)} %bitcast.6), channel_id=1, source_target_pairs={{1,2},{3,4},{5,6},{2,1},{4,3},{6,5},{9,10},{11,12},{13,14},{10,9},... | collective-permute-start | bytes 1572872 | tf_op jit(solution)/shard_map/ppermute | solution.py:444
  2.3 24.4 %collective-permute-start.15 = (bf16[2,256,512]{2,1,0:T(8,128)(2,1)S(1)}, bf16[2,256,512]{2,1,0:T(8,128)(2,1)S(1)}, u32[]{:S(2)}, u32[]{:S(2)}) collective-permute-start(bf16[2,256,512]{2,1,0:T(8,128)(2,1)S(1)} %pad_maximum_fusion.rest_0_), channel_id=1, source_target_pairs={{0,8},{8,24},{24,16},{16,0},{1,9},{9,25},{25,17},{17,1},{2,10},{10... | collective-permute-start | bytes 1572872 | tf_op jit(solution)/shard_map/ppermute | solution.py:451
  13.9 11.4 %collective-permute-start.4 = (bf16[528,128]{1,0:T(8,128)(2,1)S(1)}, bf16[528,128]{1,0:T(8,128)(2,1)S(1)}, u32[]{:S(2)}, u32[]{:S(2)}) collective-permute-start(bf16[528,128]{1,0:T(8,128)(2,1)S(1)} %get-tuple-element.66), channel_id=1, source_target_pairs={{0,6},{1,7},{2,4},{3,5},{4,2},{5,3},{6,0},{7,1},{8,14},{9,15},{10,... | collective-permute-start | bytes 405512 | tf_op jit(solution)/shard_map/ppermute | solution.py:439
  18.3 7.3 %collective-permute-start.3 = (bf16[528,128]{1,0:T(8,128)(2,1)S(1)}, bf16[528,128]{1,0:T(8,128)(2,1)S(1)}, u32[]{:S(2)}, u32[]{:S(2)}) collective-permute-start(bf16[528,128]{1,0:T(8,128)(2,1)S(1)} %get-tuple-element.64), channel_id=1, source_target_pairs={{0,4},{1,5},{2,6},{3,7},{4,0},{5,1},{6,2},{7,3},{8,12},{9,13},{10,... | collective-permute-start | bytes 405512 | tf_op jit(solution)/shard_map/ppermute | solution.py:439
  18.8 7.1 %collective-permute-start.2 = (bf16[528,128]{1,0:T(8,128)(2,1)S(1)}, bf16[528,128]{1,0:T(8,128)(2,1)S(1)}, u32[]{:S(2)}, u32[]{:S(2)}) collective-permute-start(bf16[528,128]{1,0:T(8,128)(2,1)S(1)} %get-tuple-element.62), channel_id=1, source_target_pairs={{0,2},{1,3},{2,0},{3,1},{4,6},{5,7},{6,4},{7,5},{8,10},{9,11},{10,... | collective-permute-start | bytes 405512 | tf_op jit(solution)/shard_map/ppermute | solution.py:439
  26.6 2.9 %collective-permute-start.5 = (bf16[256,1024]{1,0:T(8,128)(2,1)S(1)}, bf16[256,1024]{1,0:T(8,128)(2,1)S(1)}, u32[]{:S(2)}, u32[]{:S(2)}) collective-permute-start(bf16[256,1024]{1,0:T(8,128)(2,1)S(1)} %collective-permute-done.1.halo_ref), channel_id=1, source_target_pairs={{0,1},{1,0},{2,3},{3,2},{4,5},{5,4},{6,7},{7,6},{8,9},{9,8},{10,11... | collective-permute-start | bytes 1572872 | tf_op jit(solution)/shard_map/ppermute | solution.py:438
  26.7 15.2 %collective-permute-start.16 = (bf16[2,256,512]{2,1,0:T(8,128)(2,1)S(1)}, bf16[2,256,512]{2,1,0:T(8,128)(2,1)S(1)}, u32[]{:S(2)}, u32[]{:S(2)}) collective-permute-start(bf16[2,256,512]{2,1,0:T(8,128)(2,1)S(1)} %collective-permute-done.15.rest_1_), channel_id=1, source_target_pairs={{0,8},{8,24},{24,16},{16,0},{1,9},{9,25},{25,17},{17,1},{2,10},{10... | collective-permute-start | bytes 1572872 | tf_op jit(solution)/shard_map/ppermute | solution.py:451
  41.9 21.8 %collective-permute-start.17 = (bf16[2,256,512]{2,1,0:T(8,128)(2,1)S(1)}, bf16[2,256,512]{2,1,0:T(8,128)(2,1)S(1)}, u32[]{:S(2)}, u32[]{:S(2)}) collective-permute-start(bf16[2,256,512]{2,1,0:T(8,128)(2,1)S(1)} %collective-permute-done.16.rest_2_), channel_id=1, source_target_pairs={{0,8},{8,24},{24,16},{16,0},{1,9},{9,25},{25,17},{17,1},{2,10},{10... | collective-permute-start | bytes 1572872 | tf_op jit(solution)/shard_map/ppermute | solution.py:451
  43.6 20.2 %collective-permute-start.22 = (bf16[2,256,512]{2,1,0:T(8,128)(2,1)S(1)}, bf16[2,256,512]{2,1,0:T(8,128)(2,1)S(1)}, u32[]{:S(2)}, u32[]{:S(2)}) collective-permute-start(bf16[2,256,512]{2,1,0:T(8,128)(2,1)S(1)} %pad_maximum_fusion.rest_0_), channel_id=1, source_target_pairs={{0,4},{1,3},{2,6},{3,1},{4,0},{5,7},{6,2},{7,5},{8,12},{9,11},{10,... | collective-permute-start | bytes 1572872 | tf_op jit(solution)/shard_map/ppermute | solution.py:440
  45.2 7.3 %collective-permute-start.8 = (bf16[512,128]{1,0:T(8,128)(2,1)S(1)}, bf16[512,128]{1,0:T(8,128)(2,1)S(1)}, u32[]{:S(2)}, u32[]{:S(2)}) collective-permute-start(bf16[512,128]{1,0:T(8,128)(2,1)S(1)} %shard_map.66.rest_0_), channel_id=1, source_target_pairs={{0,6},{1,7},{2,4},{3,5},{4,2},{5,3},{6,0},{7,1},{8,14},{9,15},{10,... | collective-permute-start | bytes 393224 | tf_op jit(solution)/shard_map/ppermute | solution.py:439
  46.5 11.9 %collective-permute-start.7 = (bf16[512,128]{1,0:T(8,128)(2,1)S(1)}, bf16[512,128]{1,0:T(8,128)(2,1)S(1)}, u32[]{:S(2)}, u32[]{:S(2)}) collective-permute-start(bf16[512,128]{1,0:T(8,128)(2,1)S(1)} %shard_map.66.rest_0_), channel_id=1, source_target_pairs={{0,4},{1,5},{2,6},{3,7},{4,0},{5,1},{6,2},{7,3},{8,12},{9,13},{10,... | collective-permute-start | bytes 393224 | tf_op jit(solution)/shard_map/ppermute | solution.py:439
  47.2 11.2 %collective-permute-start.6 = (bf16[512,128]{1,0:T(8,128)(2,1)S(1)}, bf16[512,128]{1,0:T(8,128)(2,1)S(1)}, u32[]{:S(2)}, u32[]{:S(2)}) collective-permute-start(bf16[512,128]{1,0:T(8,128)(2,1)S(1)} %shard_map.66.rest_0_), channel_id=1, source_target_pairs={{0,2},{1,3},{2,0},{3,1},{4,6},{5,7},{6,4},{7,5},{8,10},{9,11},{10,... | collective-permute-start | bytes 393224 | tf_op jit(solution)/shard_map/ppermute | solution.py:439
  52.4 13.8 %collective-permute-start.23 = (bf16[2,256,512]{2,1,0:T(8,128)(2,1)S(1)}, bf16[2,256,512]{2,1,0:T(8,128)(2,1)S(1)}, u32[]{:S(2)}, u32[]{:S(2)}) collective-permute-start(bf16[2,256,512]{2,1,0:T(8,128)(2,1)S(1)} %collective-permute-done.15.rest_1_), channel_id=1, source_target_pairs={{0,4},{1,3},{2,6},{3,1},{4,0},{5,7},{6,2},{7,5},{8,12},{9,11},{10,... | collective-permute-start | bytes 1572872 | tf_op jit(solution)/shard_map/ppermute | solution.py:440
  60.6 6.8 %collective-permute-start.18 = (bf16[2,256,512]{2,1,0:T(8,128)(2,1)S(1)}, bf16[2,256,512]{2,1,0:T(8,128)(2,1)S(1)}, u32[]{:S(2)}, u32[]{:S(2)}) collective-permute-start(bf16[2,256,512]{2,1,0:T(8,128)(2,1)S(1)} %pad_maximum_fusion.rest_0_), channel_id=1, source_target_pairs={{0,1},{1,0},{2,3},{3,2},{4,5},{5,4},{6,7},{7,6},{8,9},{9,8},{10,11... | collective-permute-start | bytes 1572872 | tf_op jit(solution)/shard_map/ppermute | solution.py:438
  63.8 4.6 %collective-permute-start.19 = (bf16[2,256,512]{2,1,0:T(8,128)(2,1)S(1)}, bf16[2,256,512]{2,1,0:T(8,128)(2,1)S(1)}, u32[]{:S(2)}, u32[]{:S(2)}) collective-permute-start(bf16[2,256,512]{2,1,0:T(8,128)(2,1)S(1)} %collective-permute-done.15.rest_1_), channel_id=1, source_target_pairs={{0,1},{1,0},{2,3},{3,2},{4,5},{5,4},{6,7},{7,6},{8,9},{9,8},{10,11... | collective-permute-start | bytes 1572872 | tf_op jit(solution)/shard_map/ppermute | solution.py:438
  64.7 3.7 %collective-permute-start.20 = (bf16[2,256,512]{2,1,0:T(8,128)(2,1)S(1)}, bf16[2,256,512]{2,1,0:T(8,128)(2,1)S(1)}, u32[]{:S(2)}, u32[]{:S(2)}) collective-permute-start(bf16[2,256,512]{2,1,0:T(8,128)(2,1)S(1)} %collective-permute-done.16.rest_2_), channel_id=1, source_target_pairs={{0,1},{1,0},{2,3},{3,2},{4,5},{5,4},{6,7},{7,6},{8,9},{9,8},{10,11... | collective-permute-start | bytes 1572872 | tf_op jit(solution)/shard_map/ppermute | solution.py:438
  65.1 3.8 %collective-permute-start.21 = (bf16[2,256,512]{2,1,0:T(8,128)(2,1)S(1)}, bf16[2,256,512]{2,1,0:T(8,128)(2,1)S(1)}, u32[]{:S(2)}, u32[]{:S(2)}) collective-permute-start(bf16[2,256,512]{2,1,0:T(8,128)(2,1)S(1)} %collective-permute-done.17.rest_3_), channel_id=1, source_target_pairs={{0,1},{1,0},{2,3},{3,2},{4,5},{5,4},{6,7},{7,6},{8,9},{9,8},{10,11... | collective-permute-start | bytes 1572872 | tf_op jit(solution)/shard_map/ppermute | solution.py:438
  66.3 12.1 %collective-permute-start.24 = (bf16[2,256,512]{2,1,0:T(8,128)(2,1)S(1)}, bf16[2,256,512]{2,1,0:T(8,128)(2,1)S(1)}, u32[]{:S(2)}, u32[]{:S(2)}) collective-permute-start(bf16[2,256,512]{2,1,0:T(8,128)(2,1)S(1)} %collective-permute-done.16.rest_2_), channel_id=1, source_target_pairs={{0,4},{1,3},{2,6},{3,1},{4,0},{5,7},{6,2},{7,5},{8,12},{9,11},{10,... | collective-permute-start | bytes 1572872 | tf_op jit(solution)/shard_map/ppermute | solution.py:440
  67.4 16.5 %collective-permute-start.25 = (bf16[2,256,512]{2,1,0:T(8,128)(2,1)S(1)}, bf16[2,256,512]{2,1,0:T(8,128)(2,1)S(1)}, u32[]{:S(2)}, u32[]{:S(2)}) collective-permute-start(bf16[2,256,512]{2,1,0:T(8,128)(2,1)S(1)} %collective-permute-done.17.rest_3_), channel_id=1, source_target_pairs={{0,4},{1,3},{2,6},{3,1},{4,0},{5,7},{6,2},{7,5},{8,12},{9,11},{10,... | collective-permute-start | bytes 1572872 | tf_op jit(solution)/shard_map/ppermute | solution.py:440
  68.4 23.2 %collective-permute-start.26 = (bf16[2,256,512]{2,1,0:T(8,128)(2,1)S(1)}, bf16[2,256,512]{2,1,0:T(8,128)(2,1)S(1)}, u32[]{:S(2)}, u32[]{:S(2)}) collective-permute-start(bf16[2,256,512]{2,1,0:T(8,128)(2,1)S(1)} %collective-permute-done.22.rest_4_.rest_0_), channel_id=1, source_target_pairs={{0,1},{1,0},{2,3},{3,2},{4,5},{5,4},{6,7},{7,6},{8,9},{9,8},{10,11... | collective-permute-start | bytes 1572872 | tf_op jit(solution)/shard_map/ppermute | solution.py:438
  68.4 25.3 %collective-permute-start.27 = (bf16[2,256,512]{2,1,0:T(8,128)(2,1)S(1)}, bf16[2,256,512]{2,1,0:T(8,128)(2,1)S(1)}, u32[]{:S(2)}, u32[]{:S(2)}) collective-permute-start(bf16[2,256,512]{2,1,0:T(8,128)(2,1)S(1)} %collective-permute-done.23.rest_5_.rest_1_), channel_id=1, source_target_pairs={{0,1},{1,0},{2,3},{3,2},{4,5},{5,4},{6,7},{7,6},{8,9},{9,8},{10,11... | collective-permute-start | bytes 1572872 | tf_op jit(solution)/shard_map/ppermute | solution.py:438
  68.9 15.1 %collective-permute-start.14 = (bf16[128,1024]{1,0:T(8,128)(2,1)S(1)}, bf16[128,1024]{1,0:T(8,128)(2,1)S(1)}, u32[]{:S(2)}, u32[]{:S(2)}) collective-permute-start(bf16[128,1024]{1,0:T(8,128)(2,1)S(1)} %get-tuple-element.83), channel_id=1, source_target_pairs={{0,2},{1,5},{2,0},{3,7},{4,6},{5,1},{6,4},{7,3},{8,10},{9,13},{10,... | collective-permute-start | bytes 786440 | tf_op jit(solution)/shard_map/ppermute | solution.py:440
  78.3 15.4 %collective-permute-start.28 = (bf16[2,256,512]{2,1,0:T(8,128)(2,1)S(1)}, bf16[2,256,512]{2,1,0:T(8,128)(2,1)S(1)}, u32[]{:S(2)}, u32[]{:S(2)}) collective-permute-start(bf16[2,256,512]{2,1,0:T(8,128)(2,1)S(1)} %collective-permute-done.24.rest_6_.rest_2_), channel_id=1, source_target_pairs={{0,1},{1,0},{2,3},{3,2},{4,5},{5,4},{6,7},{7,6},{8,9},{9,8},{10,11... | collective-permute-start | bytes 1572872 | tf_op jit(solution)/shard_map/ppermute | solution.py:438
  84.0 9.7 %collective-permute-start.29 = (bf16[2,256,512]{2,1,0:T(8,128)(2,1)S(1)}, bf16[2,256,512]{2,1,0:T(8,128)(2,1)S(1)}, u32[]{:S(2)}, u32[]{:S(2)}) collective-permute-start(bf16[2,256,512]{2,1,0:T(8,128)(2,1)S(1)} %collective-permute-done.25.rest_7_.rest_3_), channel_id=1, source_target_pairs={{0,1},{1,0},{2,3},{3,2},{4,5},{5,4},{6,7},{7,6},{8,9},{9,8},{10,11... | collective-permute-start | bytes 1572872 | tf_op jit(solution)/shard_map/ppermute | solution.py:438
  84.0 6.4 %collective-permute-start.13 = (bf16[128,1024]{1,0:T(8,128)(2,1)S(1)}, bf16[128,1024]{1,0:T(8,128)(2,1)S(1)}, u32[]{:S(2)}, u32[]{:S(2)}) collective-permute-start(bf16[128,1024]{1,0:T(8,128)(2,1)S(1)} %get-tuple-element.83), channel_id=1, source_target_pairs={{0,4},{1,3},{2,6},{3,1},{4,0},{5,7},{6,2},{7,5},{8,12},{9,11},{10,... | collective-permute-start | bytes 786440 | tf_op jit(solution)/shard_map/ppermute | solution.py:440
  90.3 8.7 %collective-permute-start.12 = (bf16[128,1024]{1,0:T(8,128)(2,1)S(1)}, bf16[128,1024]{1,0:T(8,128)(2,1)S(1)}, u32[]{:S(2)}, u32[]{:S(2)}) collective-permute-start(bf16[128,1024]{1,0:T(8,128)(2,1)S(1)} %get-tuple-element.82), channel_id=1, source_target_pairs={{0,2},{1,5},{2,0},{3,7},{4,6},{5,1},{6,4},{7,3},{8,10},{9,13},{10,... | collective-permute-start | bytes 786440 | tf_op jit(solution)/shard_map/ppermute | solution.py:440
  91.5 8.6 %collective-permute-start.11 = (bf16[128,1024]{1,0:T(8,128)(2,1)S(1)}, bf16[128,1024]{1,0:T(8,128)(2,1)S(1)}, u32[]{:S(2)}, u32[]{:S(2)}) collective-permute-start(bf16[128,1024]{1,0:T(8,128)(2,1)S(1)} %get-tuple-element.82), channel_id=1, source_target_pairs={{0,4},{1,3},{2,6},{3,1},{4,0},{5,7},{6,2},{7,5},{8,12},{9,11},{10,... | collective-permute-start | bytes 786440 | tf_op jit(solution)/shard_map/ppermute | solution.py:440
  101.4 9.2 %collective-permute-start.33 = (bf16[128,1024]{1,0:T(8,128)(2,1)S(1)}, bf16[128,1024]{1,0:T(8,128)(2,1)S(1)}, u32[]{:S(2)}, u32[]{:S(2)}) collective-permute-start(bf16[128,1024]{1,0:T(8,128)(2,1)S(1)} %shard_map.75), channel_id=1, source_target_pairs={{0,4},{1,3},{2,6},{3,1},{4,0},{5,7},{6,2},{7,5},{8,12},{9,11},{10,... | collective-permute-start | bytes 786440 | tf_op jit(solution)/shard_map/ppermute | solution.py:440
  102.4 8.5 %collective-permute-start.32 = (bf16[128,1024]{1,0:T(8,128)(2,1)S(1)}, bf16[128,1024]{1,0:T(8,128)(2,1)S(1)}, u32[]{:S(2)}, u32[]{:S(2)}) collective-permute-start(bf16[128,1024]{1,0:T(8,128)(2,1)S(1)} %shard_map.74), channel_id=1, source_target_pairs={{0,2},{1,5},{2,0},{3,7},{4,6},{5,1},{6,4},{7,3},{8,10},{9,13},{10,... | collective-permute-start | bytes 786440 | tf_op jit(solution)/shard_map/ppermute | solution.py:440
  103.6 10.1 %collective-permute-start.30 = (bf16[128,1024]{1,0:T(8,128)(2,1)S(1)}, bf16[128,1024]{1,0:T(8,128)(2,1)S(1)}, u32[]{:S(2)}, u32[]{:S(2)}) collective-permute-start(bf16[128,1024]{1,0:T(8,128)(2,1)S(1)} %shard_map.72), channel_id=1, source_target_pairs={{0,2},{1,5},{2,0},{3,7},{4,6},{5,1},{6,4},{7,3},{8,10},{9,13},{10,... | collective-permute-start | bytes 786440 | tf_op jit(solution)/shard_map/ppermute | solution.py:440
  104.4 9.9 %collective-permute-start.31 = (bf16[128,1024]{1,0:T(8,128)(2,1)S(1)}, bf16[128,1024]{1,0:T(8,128)(2,1)S(1)}, u32[]{:S(2)}, u32[]{:S(2)}) collective-permute-start(bf16[128,1024]{1,0:T(8,128)(2,1)S(1)} %shard_map.73), channel_id=1, source_target_pairs={{0,4},{1,3},{2,6},{3,1},{4,0},{5,7},{6,2},{7,5},{8,12},{9,11},{10,... | collective-permute-start | bytes 786440 | tf_op jit(solution)/shard_map/ppermute | solution.py:440
  (4 other events, 12.2 us)

commit v4 on v3

--- a/solution.py
+++ b/solution.py
@@ -17,6 +17,7 @@
 VMEM_LIMIT = 24 * 1024 * 1024
 SMALL = 60.0
 CUTS = 2
+BOTH = [(side, part) for side in range(2) for part in range(2)]
 
 
 def dot(a, b):
@@ -144,53 +145,41 @@
     top_ref[...] = jnp.broadcast_to(jnp.max(head_sum(query)), top_ref.shape)
     stat_rows = owned // 128
 
-    def pair_sums(pair, shifted):
-        cut = pl.ds(pl.multiple_of(pair * 128, 128), 128)
-        kp, vp = kk_ref[:, cut], vv_ref[:, cut]
+    def score(pair, side):
+        wp = wp_ref[pair * 2 + side]
+        none = jnp.zeros_like(wp)
+        wide_wp = jnp.concatenate([wp, none] if side == 0 else [none, wp], axis=0)
+        return lax.dot_general(wide_wp, kk_ref[:, pair_cut(pair)], TT, preferred_element_type=F32)
+
+    def finish(pair, side, logits, shifted):
+        kp, vp = kk_ref[:, pair_cut(pair)], vv_ref[:, pair_cut(pair)]
         turned = pltpu.roll(vp.astype(F32), 64, 1).astype(BF)
         low_half = lanes(kp.shape) < HS
-        for side in range(2):
-            mixed = jnp.where(low_half, kp, turned) if side == 0 else jnp.where(low_half, turned, kp)
-            wp = wp_ref[pair * 2 + side]
-            none = jnp.zeros_like(wp)
-            wide_wp = jnp.concatenate([wp, none] if side == 0 else [none, wp], axis=0)
-            logits = lax.dot_general(wide_wp, kp, TT, preferred_element_type=F32)
+        mixed = jnp.where(low_half, kp, turned) if side == 0 else jnp.where(low_half, turned, kp)
+        if shifted:
+            peak = jnp.max(logits, axis=1, keepdims=True)
+            logits = logits - peak
+        weight = jnp.exp(logits).astype(BF)
+        total = jnp.sum(weight.astype(F32), axis=1, keepdims=True)
+        sums = dot(weight, mixed).astype(BF)
+        for part in range(rank // 128):
+            column = (pair * 2 + side) * rank + part * 128
+            owner, offset = column // owned, column % owned
+            here = slice(part * 128, (part + 1) * 128)
+            pay_ref[owner, pl.ds(pl.multiple_of(offset, 128), 128), :] = sums[here]
+            entries = [(3, to_row(total[here]))]
             if shifted:
-                peak = jnp.max(logits, axis=1, keepdims=True)
-                logits = logits - peak
-            weight = jnp.exp(logits).astype(BF)
-            total = jnp.sum(weight.astype(F32), axis=1, keepdims=True)
-            sums = dot(weight, mixed).astype(BF)
-            for part in range(rank // 128):
-                column = (pair * 2 + side) * rank + part * 128
-                owner, offset = column // owned, column % owned
-                here = slice(part * 128, (part + 1) * 128)
-                pay_ref[owner, pl.ds(pl.multiple_of(offset, 128), 128), :] = sums[here]
-                entries = [(3, to_row(total[here]))]
-                if shifted:
-                    one = to_row(peak[here])
-                    first = one.astype(BF).astype(F32)
-                    second = (one - first).astype(BF).astype(F32)
-                    entries += [(0, first), (1, second), (2, one - first - second)]
-                for i, row in entries:
-                    stat_ref[owner, pl.ds(i * stat_rows + offset // 128, 1), :] = row
+                one = to_row(peak[here])
+                first = one.astype(BF).astype(F32)
+                second = (one - first).astype(BF).astype(F32)
+                entries += [(0, first), (1, second), (2, one - first - second)]
+            for i, row in entries:
+                stat_ref[owner, pl.ds(i * stat_rows + offset // 128, 1), :] = row
 
     column_norm = jnp.max(jnp.sum(jnp.square(wp_ref[...].astype(F32)), axis=1))
     near_zero = jnp.max(key_top) * HS * column_norm < SMALL * SMALL
 
-    @pl.when(near_zero)
-    def _():
-        for pair in range(heads // 2):
-            pair_sums(pair, False)
-
-    @pl.when(jnp.logical_not(near_zero))
-    def _():
-        def one(pair, carry):
-            pair_sums(pair, True)
-            return carry
-
-        lax.fori_loop(0, heads // 2, one, 0)
-
+    one_ahead(near_zero, heads // 2, [(0,), (1,)], score, finish)
     pay_ref[:, owned:, :] = stat_ref[...].astype(BF)
     copies = [
         pltpu.make_async_copy(pay_ref.at[lax.bitwise_xor(chip, k)], pays[k], out_sem.at[k]) for k in range(chips)
@@ -235,19 +224,23 @@
     return jnp.max(top_ref[...]) * (HS * 1.02) < SMALL * SMALL
 
 
-def both_ways(small, heads, attend):
+def one_ahead(small, pairs, kinds, score, finish):
     @pl.when(small)
     def _():
-        for pair in range(heads // 2):
-            attend(pair, False)
+        units = [(pair, *kind) for pair in range(pairs) for kind in kinds]
+        ahead = score(*units[0])
+        for i, unit in enumerate(units):
+            scores, ahead = ahead, score(*units[i + 1]) if i + 1 < len(units) else None
+            finish(*unit, scores, False)
 
     @pl.when(jnp.logical_not(small))
     def _():
         def one(pair, carry):
-            attend(pair, True)
+            for kind in kinds:
+                finish(pair, *kind, score(pair, *kind), True)
             return carry
 
-        lax.fori_loop(0, heads // 2, one, 0)
+        lax.fori_loop(0, pairs, one, 0)
 
 
 def pair_cut(pair):
@@ -259,22 +252,23 @@
     place = lanes((rows, 128))
     m_ref[...] = jnp.zeros_like(m_ref)
 
-    def attend(pair, shifted):
-        cut = pair_cut(pair)
-        kp = nk_ref[:, cut]
-        for side in range(2):
-            vp = with_ones(nv_ref[:, cut], side)
-            for part in range(2):
-                these = slice(part * rows, (part + 1) * rows)
-                qm = one_head(q_ref[these, cut], side)
-                scores = lax.dot_general(qm, kp, NT, preferred_element_type=F32)
-                if shifted:
-                    peak = jnp.max(scores, axis=1, keepdims=True)
-                    scores = scores - peak
-                    m_ref[these] = jnp.where(place == pair * 2 + side, peak, m_ref[these])
-                o_ref[these, pair_cut(pair * 2 + side)] = dot(jnp.exp(scores).astype(BF), vp)
-
-    both_ways(small_scores(top_ref), nk_ref.shape[1] // HS, attend)
+    def rows_of(part):
+        return slice(part * rows, (part + 1) * rows)
+
+    def score(pair, side, part):
+        qm = one_head(q_ref[rows_of(part), pair_cut(pair)], side)
+        return lax.dot_general(qm, nk_ref[:, pair_cut(pair)], NT, preferred_element_type=F32)
+
+    def finish(pair, side, part, scores, shifted):
+        these = rows_of(part)
+        if shifted:
+            peak = jnp.max(scores, axis=1, keepdims=True)
+            scores = scores - peak
+            m_ref[these] = jnp.where(place == pair * 2 + side, peak, m_ref[these])
+        vp = with_ones(nv_ref[:, pair_cut(pair)], side)
+        o_ref[these, pair_cut(pair * 2 + side)] = dot(jnp.exp(scores).astype(BF), vp)
+
+    one_ahead(small_scores(top_ref), nk_ref.shape[1] // 128, BOTH, score, finish)
 
 
 def halo_kernel(top_ref, q_ref, before_ref, mb_ref, halo_ref, halop_ref, wk_ref, wv_ref, o_ref, m_ref, xh_ref, hk_ref, hv_ref):
@@ -290,26 +284,29 @@
     place = lanes((rows, 128))
     m_ref[...] = mb_ref[...]
 
-    def attend(pair, shifted):
-        cut = pair_cut(pair)
-        for side in range(2):
-            here = pair_cut(pair * 2 + side)
-            for part in range(2):
-                these = slice(part * rows, (part + 1) * rows)
-                qm = one_head(q_ref[these, cut], side)
-                scores = lax.dot_general(qm, hk_ref[these, cut], NT, preferred_element_type=F32)
-                scores = scores + jnp.where(inside[part], 0.0, -jnp.inf).astype(F32)
-                before = before_ref[these, here]
-                if shifted:
-                    head = place == pair * 2 + side
-                    peak = jnp.sum(jnp.where(head, mb_ref[these], 0.0), axis=1, keepdims=True)
-                    new = jnp.maximum(peak, jnp.max(scores, axis=1, keepdims=True))
-                    scores = scores - new
-                    before = before * jnp.exp(peak - new)
-                    m_ref[these] = jnp.where(head, new, m_ref[these])
-                o_ref[these, here] = before + dot(jnp.exp(scores).astype(BF), with_ones(hv_ref[these, cut], side))
-
-    both_ways(small_scores(top_ref), hk_ref.shape[1] // HS, attend)
+    def rows_of(part):
+        return slice(part * rows, (part + 1) * rows)
+
+    def score(pair, side, part):
+        these, cut = rows_of(part), pair_cut(pair)
+        qm = one_head(q_ref[these, cut], side)
+        scores = lax.dot_general(qm, hk_ref[these, cut], NT, preferred_element_type=F32)
+        return scores + jnp.where(inside[part], 0.0, -jnp.inf).astype(F32)
+
+    def finish(pair, side, part, scores, shifted):
+        these, here = rows_of(part), pair_cut(pair * 2 + side)
+        before = before_ref[these, here]
+        if shifted:
+            head = place == pair * 2 + side
+            peak = jnp.sum(jnp.where(head, mb_ref[these], 0.0), axis=1, keepdims=True)
+            new = jnp.maximum(peak, jnp.max(scores, axis=1, keepdims=True))
+            scores = scores - new
+            before = before * jnp.exp(peak - new)
+            m_ref[these] = jnp.where(head, new, m_ref[these])
+        values = with_ones(hv_ref[these, pair_cut(pair)], side)
+        o_ref[these, here] = before + dot(jnp.exp(scores).astype(BF), values)
+
+    one_ahead(small_scores(top_ref), hk_ref.shape[1] // 128, BOTH, score, finish)
 
 
 def far_kernel(sizes, top_ref, q_ref, o_ref, m_ref, *rest):
@@ -323,31 +320,43 @@
         all_ref[pl.ds(pl.multiple_of(source * owned, owned), owned), :] = fars[k][...]
     place = lanes((rows, 128))
 
-    def attend(pair, shifted):
-        whole_pair = group * (heads // 2) + pair
-        cut = pair_cut(whole_pair)
+    def rows_of(part):
+        return slice(part * rows, (part + 1) * rows)
+
+    def pair_of(pair):
+        return group * (heads // 2) + pair
+
+    def summary(pair, side):
+        head = pair_of(pair) * 2 + side
+        return all_ref[pl.ds(pl.multiple_of(head * rank, rank), rank), :]
+
+    def score(pair, part):
+        query = q_ref[rows_of(part), pair_cut(pair_of(pair))]
+        return [
+            lax.dot_general(one_head(query, side), summary(pair, side), NT, preferred_element_type=F32)
+            for side in range(2)
+        ]
+
+    def finish(pair, part, scores, shifted):
+        these = rows_of(part)
         low_half = lanes((rows, 128)) < HS
-        for part in range(2):
-            these = slice(part * rows, (part + 1) * rows)
-            sums = []
-            for side in range(2):
-                qm = one_head(q_ref[these, cut], side)
-                head = whole_pair * 2 + side
-                kv = all_ref[pl.ds(pl.multiple_of(head * rank, rank), rank), :]
-                scores = lax.dot_general(qm, kv, NT, preferred_element_type=F32)
-                before = o_ref[these, pair_cut(head)]
-                if shifted:
-                    peak = jnp.sum(jnp.where(place == head, m_ref[these], 0.0), axis=1, keepdims=True)
-                    new = jnp.maximum(peak, jnp.max(scores, axis=1, keepdims=True))
-                    scores = scores - new
-                    before = before * jnp.exp(peak - new)
-                out = dot(jnp.exp(scores).astype(BF), with_ones(kv, 1 - side))
-                sums.append(before + pltpu.roll(out, 64, 1))
-            total = pltpu.roll(jnp.where(low_half, sums[1], sums[0]), 64, 1)
-            result = (jnp.where(low_half, sums[0], sums[1]) / total).astype(BF)
-            (mine_ref, theirs_ref)[part][:, pair_cut(pair)] = result
-
-    both_ways(small_scores(top_ref), heads, attend)
+        sums = []
+        for side in range(2):
+            head = pair_of(pair) * 2 + side
+            weight = scores[side]
+            before = o_ref[these, pair_cut(head)]
+            if shifted:
+                peak = jnp.sum(jnp.where(place == head, m_ref[these], 0.0), axis=1, keepdims=True)
+                new = jnp.maximum(peak, jnp.max(weight, axis=1, keepdims=True))
+                weight = weight - new
+                before = before * jnp.exp(peak - new)
+            out = dot(jnp.exp(weight).astype(BF), with_ones(summary(pair, side), 1 - side))
+            sums.append(before + pltpu.roll(out, 64, 1))
+        total = pltpu.roll(jnp.where(low_half, sums[1], sums[0]), 64, 1)
+        result = (jnp.where(low_half, sums[0], sums[1]) / total).astype(BF)
+        (mine_ref, theirs_ref)[part][:, pair_cut(pair)] = result
+
+    one_ahead(small_scores(top_ref), heads // 2, [(0,), (1,)], score, finish)
 
 
 def mix_kernel(cuts, tok_ref, *rest):
@@ -505,6 +514,8 @@
         (8 * rows * wide * 4 * rows, 8 * rows * wide, half * 2 * rows * 2 * rows),
     )(top, query, near_keys, near_values)
     pays = [after(p, near[0]) for p in pays]
+    halo = after(halo, near[0])
+    halo_partner = swap(halo)
     far = pl.pallas_call(
         functools.partial(combine_kernel, (chips, owned, extra)),
         out_shape=shape((owned, 128)),
@@ -515,8 +526,6 @@
     fars = [far]
     for k in range(1, chips):
         fars.append(jump(far, k))
-    halo = after(halo, far)
-    halo_partner = swap(halo)
     near = call(
         halo_kernel,
         [vmem] * 8,

time: 116 us -> 116 us (level)
    ppermute x6, starting transfers between devices: 9.28 us -> 7.19 us  [on_device(): lax.ppermute(x, 'seq', [(i, i ^ 2 * k) for i in range(n)])]
    ppermute x12, starting transfers between devices: 2.76 us -> 4.78 us  [on_device(): swap = lambda x: lax.ppermute(x, 'seq', [(i, i ^ 1) for i in range(n)])]
  transfers between devices with their start and end apart: 34 -> 34, of which waited for: 14 -> 16; matrix products, arithmetic and copies ran while one was open for 1% -> 1% of each run, Pallas kernels for 29% -> 29%
where the time goes in v4:
time: 116 us
  waiting for transfers between devices  46.3 us (40%)
  Pallas kernels  34.5 us (30%)
  starting transfers between devices  32.7 us (28%)
  other arithmetic  2.14 us (2%)
    ppermute x12, waiting for transfers between devices, on_device(): lax.ppermute(x, 'seq', [(i, i ^ 2 * ks[i % 2]) for i in range(n)])  29.4 us
    ppermute x12, starting transfers between devices, on_device(): lax.ppermute(x, 'seq', [(i, i ^ 2 * ks[i % 2]) for i in range(n)])  13.1 us
    ppermute x6, waiting for transfers between devices, on_device(): lax.ppermute(x, 'seq', [(i, i ^ 2 * k) for i in range(n)])  10.1 us
    pallas_call x1, Pallas kernels, on_device(): call(functools.partial(project_kernel, (chips, owned, extra, rank)), [hbm...  9.08 us
    pallas_call x6, Pallas kernels, feed(): call(functools.partial(feed_kernel, parts, len(more)), [vmem] * (1 + len(...  7.68 us
    ppermute x6, starting transfers between devices, on_device(): lax.ppermute(x, 'seq', [(i, i ^ 2 * k) for i in range(n)])  7.19 us
    ppermute x3, starting transfers between devices, gather_part(): gathered.append(lax.ppermute(after(gathered[-1], *earlier), 'dp', follow))  6.89 us
    ppermute x3, waiting for transfers between devices, gather_part(): gathered.append(lax.ppermute(after(gathered[-1], *earlier), 'dp', follow))  6.2 us
  transfers between devices with their start and end apart: 34, of which 16 were waited for; matrix products, arithmetic and copies ran while one was open for 1% of the time, Pallas kernels for 29%

profile of v4, /device:TPU:0, one launch (start us, length us, event | category | flops | bytes accessed | tf_op | source)
XLA Modules:
  0.0 115.9 jit_solution(4515084562236261928)
XLA Ops:
  2.3 2.6 %collective-permute-start.15 = (bf16[2,256,512]{2,1,0:T(8,128)(2,1)S(1)}, bf16[2,256,512]{2,1,0:T(8,128)(2,1)S(1)}, u32[]{:S(2)}, u32[]{:S(2)}) collective-permute-start(bf16[2,256,512]{2,1,0:T(8,128)(2,1)S(1)} %pad_maximum_fusion.rest_0_), channel_id=1, source_target_pairs={{0,8},{8,24},{24,16},{16,0},{1,9},{9,25},{25,17},{17,1},{2,10},{10... | collective-permute-start | bytes 1572872 | tf_op jit(solution)/shard_map/ppermute | solution.py:460
  4.9 9.1 %shard_map.64 = (bf16[512,512]{1,0:T(8,128)(2,1)S(1)}, bf16[512,512]{1,0:T(8,128)(2,1)S(1)}, bf16[512,512]{1,0:T(8,128)(2,1)S(1)}, bf16[1024,512]{1,0:T(8,128)(2...) custom-call(bf16[256,1024]{1,0:T(8,128)(2,1)} %bitcast.7, ...), custom_call_target="tpu_custom_call" | custom-call | flops 1610612736 | bytes 3145728 | tf_op jit(solution)/shard_map/pallas_call | solution.py:478
  14.0 5.6 %shard_map.65 = (f32[512,1024]{1,0:T(8,128)S(1)}, f32[512,128]{1,0:T(8,128)S(1)}) custom-call(f32[8,128]{1,0:T(8,128)S(1)} %get-tuple-element.54.top_ref, bf16[512,512]{1,0:T(8,128)(2,1)S(1)} %get-tuple-element.55.q_ref, bf16[512,512]{1,0:T(8,128)(2,1)S(1)} %get-tuple-element.56.nk_ref, bf16[512,512]{1,0:T(8,128)(2,1)S(1)} %get-tuple-element.57.nv_ref), custom_call_target="tpu_custom_call" | custom-call | flops 1073741824 | bytes 1048576 | tf_op jit(solution)/shard_map/pallas_call | solution.py:508
  19.6 2.6 %collective-permute-start.2 = (bf16[256,1024]{1,0:T(8,128)(2,1)S(1)}, bf16[256,1024]{1,0:T(8,128)(2,1)S(1)}, u32[]{:S(2)}, u32[]{:S(2)}) collective-permute-start(bf16[256,1024]{1,0:T(8,128)(2,1)S(1)} %collective-permute-done.1.halo_ref), channel_id=1, source_target_pairs={{0,1},{1,0},{2,3},{3,2},{4,5},{5,4},{6,7},{7,6},{8,9},{9,8},{10,11... | collective-permute-start | bytes 1572872 | tf_op jit(solution)/shard_map/ppermute | solution.py:447
  22.2 2.6 %collective-permute-start.16 = (bf16[2,256,512]{2,1,0:T(8,128)(2,1)S(1)}, bf16[2,256,512]{2,1,0:T(8,128)(2,1)S(1)}, u32[]{:S(2)}, u32[]{:S(2)}) collective-permute-start(bf16[2,256,512]{2,1,0:T(8,128)(2,1)S(1)} %collective-permute-done.15.rest_1_), channel_id=1, source_target_pairs={{0,8},{8,24},{24,16},{16,0},{1,9},{9,25},{25,17},{17,1},{2,10},{10... | collective-permute-start | bytes 1572872 | tf_op jit(solution)/shard_map/ppermute | solution.py:460
  24.8 6.0 %shard_map.66 = (f32[512,1024]{1,0:T(8,128)S(1)}, f32[512,128]{1,0:T(8,128)S(1)}) custom-call(f32[8,128]{1,0:T(8,128)S(1)} %get-tuple-element.54.top_ref, bf16[512,512]{1,0:T(8,128)(2,1)S(1)} %get-tuple-element.55.q_ref, f32[512,1024]{1,0:T(8,128)S(1)} %get-tuple-element.58.before_ref, f32[512,128]{1,0:T(8,128)S(1)} %get-tuple-element.59.mb_ref, ...), custom_call_target="tpu_custom_call" | custom-call | flops 1073741824 | bytes 2097152 | tf_op jit(solution)/shard_map/pallas_call | solution.py:529
  30.8 6.2 %collective-permute-done.16.rest_2_ = bf16[2,256,512]{2,1,0:T(8,128)(2,1)S(1)} collective-permute-done((bf16[2,256,512]{2,1,0:T(8,128)(2,1)S(1)}, bf16[2,256,512]{2,1,0:T(8,128)(2,1)S(1)}, u32[]{:S(2)}, u32[]{:S(2)}) %collective-permute-start.16) | collective-permute-done | bytes 524320 | tf_op jit(solution)/shard_map/ppermute | solution.py:460
  37.0 1.7 %collective-permute-start.17 = (bf16[2,256,512]{2,1,0:T(8,128)(2,1)S(1)}, bf16[2,256,512]{2,1,0:T(8,128)(2,1)S(1)}, u32[]{:S(2)}, u32[]{:S(2)}) collective-permute-start(bf16[2,256,512]{2,1,0:T(8,128)(2,1)S(1)} %collective-permute-done.16.rest_2_), channel_id=1, source_target_pairs={{0,8},{8,24},{24,16},{16,0},{1,9},{9,25},{25,17},{17,1},{2,10},{10... | collective-permute-start | bytes 1572872 | tf_op jit(solution)/shard_map/ppermute | solution.py:460
  38.7 2.2 %collective-permute-start.5 = (bf16[528,128]{1,0:T(8,128)(2,1)S(1)}, bf16[528,128]{1,0:T(8,128)(2,1)S(1)}, u32[]{:S(2)}, u32[]{:S(2)}) collective-permute-start(bf16[528,128]{1,0:T(8,128)(2,1)S(1)} %get-tuple-element.71), channel_id=1, source_target_pairs={{0,6},{1,7},{2,4},{3,5},{4,2},{5,3},{6,0},{7,1},{8,14},{9,15},{10,... | collective-permute-start | bytes 405512 | tf_op jit(solution)/shard_map/ppermute | solution.py:448
  42.3 2.0 %collective-permute-start.22 = (bf16[2,256,512]{2,1,0:T(8,128)(2,1)S(1)}, bf16[2,256,512]{2,1,0:T(8,128)(2,1)S(1)}, u32[]{:S(2)}, u32[]{:S(2)}) collective-permute-start(bf16[2,256,512]{2,1,0:T(8,128)(2,1)S(1)} %pad_maximum_fusion.rest_0_), channel_id=1, source_target_pairs={{0,4},{1,3},{2,6},{3,1},{4,0},{5,7},{6,2},{7,5},{8,12},{9,11},{10,... | collective-permute-start | bytes 1572872 | tf_op jit(solution)/shard_map/ppermute | solution.py:449
  45.5 1.4 %collective-permute-done.4.refs_2_ = bf16[528,128]{1,0:T(8,128)(2,1)S(1)} collective-permute-done((bf16[528,128]{1,0:T(8,128)(2,1)S(1)}, bf16[528,128]{1,0:T(8,128)(2,1)S(1)}, u32[]{:S(2)}, u32[]{:S(2)}) %collective-permute-start.4) | collective-permute-done | bytes 135200 | tf_op jit(solution)/shard_map/ppermute | solution.py:448
  46.9 2.7 %collective-permute-done.3.refs_1_ = bf16[528,128]{1,0:T(8,128)(2,1)S(1)} collective-permute-done((bf16[528,128]{1,0:T(8,128)(2,1)S(1)}, bf16[528,128]{1,0:T(8,128)(2,1)S(1)}, u32[]{:S(2)}, u32[]{:S(2)}) %collective-permute-start.3) | collective-permute-done | bytes 135200 | tf_op jit(solution)/shard_map/ppermute | solution.py:448
  51.0 1.5 %collective-permute-start.7 = (bf16[512,128]{1,0:T(8,128)(2,1)S(1)}, bf16[512,128]{1,0:T(8,128)(2,1)S(1)}, u32[]{:S(2)}, u32[]{:S(2)}) collective-permute-start(bf16[512,128]{1,0:T(8,128)(2,1)S(1)} %shard_map.67.rest_0_), channel_id=1, source_target_pairs={{0,4},{1,5},{2,6},{3,7},{4,0},{5,1},{6,2},{7,3},{8,12},{9,13},{10,... | collective-permute-start | bytes 393224 | tf_op jit(solution)/shard_map/ppermute | solution.py:448
  52.5 1.4 %collective-permute-start.6 = (bf16[512,128]{1,0:T(8,128)(2,1)S(1)}, bf16[512,128]{1,0:T(8,128)(2,1)S(1)}, u32[]{:S(2)}, u32[]{:S(2)}) collective-permute-start(bf16[512,128]{1,0:T(8,128)(2,1)S(1)} %shard_map.67.rest_0_), channel_id=1, source_target_pairs={{0,2},{1,3},{2,0},{3,1},{4,6},{5,7},{6,4},{7,5},{8,10},{9,11},{10,... | collective-permute-start | bytes 393224 | tf_op jit(solution)/shard_map/ppermute | solution.py:448
  53.9 3.4 %collective-permute-done.8.rest_3_ = bf16[512,128]{1,0:T(8,128)(2,1)S(1)} collective-permute-done((bf16[512,128]{1,0:T(8,128)(2,1)S(1)}, bf16[512,128]{1,0:T(8,128)(2,1)S(1)}, u32[]{:S(2)}, u32[]{:S(2)}) %collective-permute-start.8) | collective-permute-done | bytes 131104 | tf_op jit(solution)/shard_map/ppermute | solution.py:448
  58.9 2.1 %shard_map.69 = (bf16[256,256]{1,0:T(8,128)(2,1)S(1)}, bf16[256,256]{1,0:T(8,128)(2,1)S(1)}) custom-call(f32[8,128]{1,0:T(8,128)S(1)} %get-tuple-element.54.top_ref, bf16[512,512]{1,0:T(8,128)(2,1)S(1)} %get-tuple-element.55.q_ref, f32[512,1024]{1,0:T(8,128)S(1)} %get-tuple-element.63.o_ref, f32[512,128]{1,0:T(8,128)S(1)} %get-tuple-element.64.m_ref, ...), custom_call_target="tpu_custom_call" | custom-call | flops 134217728 | bytes 393216 | tf_op jit(solution)/shard_map/pallas_call | solution.py:548
  61.3 2.3 %shard_map.68 = (bf16[256,256]{1,0:T(8,128)(2,1)S(1)}, bf16[256,256]{1,0:T(8,128)(2,1)S(1)}) custom-call(f32[8,128]{1,0:T(8,128)S(1)} %get-tuple-element.54.top_ref, bf16[512,512]{1,0:T(8,128)(2,1)S(1)} %get-tuple-element.55.q_ref, f32[512,1024]{1,0:T(8,128)S(1)} %get-tuple-element.63.o_ref, f32[512,128]{1,0:T(8,128)S(1)} %get-tuple-element.64.m_ref, ...), custom_call_target="tpu_custom_call" | custom-call | flops 134217728 | bytes 393216 | tf_op jit(solution)/shard_map/pallas_call | solution.py:548
  68.7 1.4 %collective-permute-start.14 = (bf16[128,1024]{1,0:T(8,128)(2,1)S(1)}, bf16[128,1024]{1,0:T(8,128)(2,1)S(1)}, u32[]{:S(2)}, u32[]{:S(2)}) collective-permute-start(bf16[128,1024]{1,0:T(8,128)(2,1)S(1)} %get-tuple-element.83), channel_id=1, source_target_pairs={{0,2},{1,5},{2,0},{3,7},{4,6},{5,1},{6,4},{7,3},{8,10},{9,13},{10,... | collective-permute-start | bytes 786440 | tf_op jit(solution)/shard_map/ppermute | solution.py:449
  70.2 1.5 %shard_map.71.rest_8_ = f32[256,1024]{1,0:T(8,128)S(1)} custom-call(bf16[256,1024]{1,0:T(8,128)(2,1)S(1)} %get-tuple-element.102.yn_ref, bf16[2,256,512]{2,1,0:T(8,128)(2,1)S(1)} %pad_maximum_fusion.rest_0_, bf16[2,256,512]{2,1,0:T(8,128)(2,1)S(1)} %collective-permute-done.15.rest_1_, bf16[2,256,512]{2,1,0:T(8,128)(2,1)S(1)} %collective-permute-done.16.rest_2_, ...), custom_call_target="tpu_custom_call" | custom-call | flops 2147483648 | bytes 2097152 | tf_op jit(solution)/shard_map/pallas_call | solution.py:576
  71.7 7.0 %collective-permute-done.24.rest_6_.rest_2_ = bf16[2,256,512]{2,1,0:T(8,128)(2,1)S(1)} collective-permute-done((bf16[2,256,512]{2,1,0:T(8,128)(2,1)S(1)}, bf16[2,256,512]{2,1,0:T(8,128)(2,1)S(1)}, u32[]{:S(2)}, u32[]{:S(2)}) %collective-permute-start.24) | collective-permute-done | bytes 524320 | tf_op jit(solution)/shard_map/ppermute | solution.py:449
  78.7 5.6 %collective-permute-done.25.rest_7_.rest_3_ = bf16[2,256,512]{2,1,0:T(8,128)(2,1)S(1)} collective-permute-done((bf16[2,256,512]{2,1,0:T(8,128)(2,1)S(1)}, bf16[2,256,512]{2,1,0:T(8,128)(2,1)S(1)}, u32[]{:S(2)}, u32[]{:S(2)}) %collective-permute-start.25) | collective-permute-done | bytes 524320 | tf_op jit(solution)/shard_map/ppermute | solution.py:449
  85.3 5.4 %collective-permute-done.13.yn_ref = bf16[128,1024]{1,0:T(8,128)(2,1)S(1)} collective-permute-done((bf16[128,1024]{1,0:T(8,128)(2,1)S(1)}, bf16[128,1024]{1,0:T(8,128)(2,1)S(1)}, u32[]{:S(2)}, u32[]{:S(2)}) %collective-permute-start.13) | collective-permute-done | bytes 262176 | tf_op jit(solution)/shard_map/ppermute | solution.py:449
  90.7 1.4 %collective-permute-start.12 = (bf16[128,1024]{1,0:T(8,128)(2,1)S(1)}, bf16[128,1024]{1,0:T(8,128)(2,1)S(1)}, u32[]{:S(2)}, u32[]{:S(2)}) collective-permute-start(bf16[128,1024]{1,0:T(8,128)(2,1)S(1)} %get-tuple-element.82), channel_id=1, source_target_pairs={{0,2},{1,5},{2,0},{3,7},{4,6},{5,1},{6,4},{7,3},{8,10},{9,13},{10,... | collective-permute-start | bytes 786440 | tf_op jit(solution)/shard_map/ppermute | solution.py:449
  93.0 1.2 %shard_map.72 = bf16[128,1024]{1,0:T(8,128)(2,1)S(1)} custom-call(bf16[128,1024]{1,0:T(8,128)(2,1)S(1)} %collective-permute-done.14.yn_ref, bf16[2,256,512]{2,1,0:T(8,128)(2,1)S(1)} %pad_maximum_fusion.rest_0_, bf16[2,256,512]{2,1,0:T(8,128)(2,1)S(1)} %collective-permute-done.15.rest_1_, bf16[2,256,512]{2,1,0:T(8,128)(2,1)S(1)} %collective-permute-done.16.rest_2_, ...), custom_call_target="tpu_custom_call" | custom-call | flops 1073741824 | bytes 2097152 | tf_op jit(solution)/shard_map/pallas_call | solution.py:576
  94.2 1.2 %shard_map.73 = bf16[128,1024]{1,0:T(8,128)(2,1)S(1)} custom-call(bf16[128,1024]{1,0:T(8,128)(2,1)S(1)} %collective-permute-done.13.yn_ref, bf16[2,256,512]{2,1,0:T(8,128)(2,1)S(1)} %collective-permute-done.18.rest_4_.rest_0_, bf16[2,256,512]{2,1,0:T(8,128)(2,1)S(1)} %collective-permute-done.19.rest_5_.rest_1_, ...), custom_call_target="tpu_custom_call" | custom-call | flops 1073741824 | bytes 2097152 | tf_op jit(solution)/shard_map/pallas_call | solution.py:576
  95.4 3.8 %collective-permute-done.12.yn_ref = bf16[128,1024]{1,0:T(8,128)(2,1)S(1)} collective-permute-done((bf16[128,1024]{1,0:T(8,128)(2,1)S(1)}, bf16[128,1024]{1,0:T(8,128)(2,1)S(1)}, u32[]{:S(2)}, u32[]{:S(2)}) %collective-permute-start.12) | collective-permute-done | bytes 262176 | tf_op jit(solution)/shard_map/ppermute | solution.py:449
  99.3 1.2 %shard_map.74 = bf16[128,1024]{1,0:T(8,128)(2,1)S(1)} custom-call(bf16[128,1024]{1,0:T(8,128)(2,1)S(1)} %collective-permute-done.12.yn_ref, bf16[2,256,512]{2,1,0:T(8,128)(2,1)S(1)} %pad_maximum_fusion.rest_0_, bf16[2,256,512]{2,1,0:T(8,128)(2,1)S(1)} %collective-permute-done.15.rest_1_, bf16[2,256,512]{2,1,0:T(8,128)(2,1)S(1)} %collective-permute-done.16.rest_2_, ...), custom_call_target="tpu_custom_call" | custom-call | flops 1073741824 | bytes 2097152 | tf_op jit(solution)/shard_map/pallas_call | solution.py:576
  100.5 1.2 %shard_map.75 = bf16[128,1024]{1,0:T(8,128)(2,1)S(1)} custom-call(bf16[128,1024]{1,0:T(8,128)(2,1)S(1)} %collective-permute-done.11.yn_ref, bf16[2,256,512]{2,1,0:T(8,128)(2,1)S(1)} %collective-permute-done.18.rest_4_.rest_0_, bf16[2,256,512]{2,1,0:T(8,128)(2,1)S(1)} %collective-permute-done.19.rest_5_.rest_1_, ...), custom_call_target="tpu_custom_call" | custom-call | flops 1073741824 | bytes 2097152 | tf_op jit(solution)/shard_map/pallas_call | solution.py:576
  102.8 1.4 %collective-permute-start.32 = (bf16[128,1024]{1,0:T(8,128)(2,1)S(1)}, bf16[128,1024]{1,0:T(8,128)(2,1)S(1)}, u32[]{:S(2)}, u32[]{:S(2)}) collective-permute-start(bf16[128,1024]{1,0:T(8,128)(2,1)S(1)} %shard_map.74), channel_id=1, source_target_pairs={{0,2},{1,5},{2,0},{3,7},{4,6},{5,1},{6,4},{7,3},{8,10},{9,13},{10,... | collective-permute-start | bytes 786440 | tf_op jit(solution)/shard_map/ppermute | solution.py:449
  105.8 1.5 %shard_map.76 = f32[256,1024]{1,0:T(8,128)S(1)} custom-call(bf16[256,1024]{1,0:T(8,128)(2,1)S(1)} %get-tuple-element.102.yn_ref, bf16[2,256,512]{2,1,0:T(8,128)(2,1)S(1)} %collective-permute-done.22.rest_4_.rest_0_, bf16[2,256,512]{2,1,0:T(8,128)(2,1)S(1)} %collective-permute-done.23.rest_5_.rest_1_, ...), custom_call_target="tpu_custom_call" | custom-call | flops 2147483648 | bytes 2097152 | tf_op jit(solution)/shard_map/pallas_call | solution.py:576
  107.3 3.6 %collective-permute-done.33 = bf16[128,1024]{1,0:T(8,128)(2,1)S(1)} collective-permute-done((bf16[128,1024]{1,0:T(8,128)(2,1)S(1)}, bf16[128,1024]{1,0:T(8,128)(2,1)S(1)}, u32[]{:S(2)}, u32[]{:S(2)}) %collective-permute-start.33) | collective-permute-done | bytes 262176 | tf_op jit(solution)/shard_map/ppermute | solution.py:449
  111.1 2.7 %collective-permute-done.30 = bf16[128,1024]{1,0:T(8,128)(2,1)S(1)} collective-permute-done((bf16[128,1024]{1,0:T(8,128)(2,1)S(1)}, bf16[128,1024]{1,0:T(8,128)(2,1)S(1)}, u32[]{:S(2)}, u32[]{:S(2)}) %collective-permute-start.30) | collective-permute-done | bytes 262176 | tf_op jit(solution)/shard_map/ppermute | solution.py:449
  (57 shorter events, 20.0 us)
Async XLA Ops:
  0.0 4.9 %collective-permute-start = (bf16[256,1024]{1,0:T(8,128)(2,1)}, bf16[256,1024]{1,0:T(8,128)(2,1)S(1)}, u32[]{:S(2)}, u32[]{:S(2)}) collective-permute-start(bf16[256,1024]{1,0:T(8,128)(2,1)} %bitcast.5), channel_id=1, source_target_pairs={{0,1},{1,0},{2,3},{3,2},{4,5},{5,4},{6,7},{7,6},{8,9},{9,8},{10,11... | collective-permute-start | bytes 1572872 | tf_op jit(solution)/shard_map/ppermute | solution.py:447
  0.5 19.1 %collective-permute-start.1 = (bf16[256,1024]{1,0:T(8,128)(2,1)}, bf16[256,1024]{1,0:T(8,128)(2,1)S(1)}, u32[]{:S(2)}, u32[]{:S(2)}) collective-permute-start(bf16[256,1024]{1,0:T(8,128)(2,1)} %bitcast.6), channel_id=1, source_target_pairs={{1,2},{3,4},{5,6},{2,1},{4,3},{6,5},{9,10},{11,12},{13,14},{10,9},... | collective-permute-start | bytes 1572872 | tf_op jit(solution)/shard_map/ppermute | solution.py:453
  2.3 19.9 %collective-permute-start.15 = (bf16[2,256,512]{2,1,0:T(8,128)(2,1)S(1)}, bf16[2,256,512]{2,1,0:T(8,128)(2,1)S(1)}, u32[]{:S(2)}, u32[]{:S(2)}) collective-permute-start(bf16[2,256,512]{2,1,0:T(8,128)(2,1)S(1)} %pad_maximum_fusion.rest_0_), channel_id=1, source_target_pairs={{0,8},{8,24},{24,16},{16,0},{1,9},{9,25},{25,17},{17,1},{2,10},{10... | collective-permute-start | bytes 1572872 | tf_op jit(solution)/shard_map/ppermute | solution.py:460
  19.6 5.2 %collective-permute-start.2 = (bf16[256,1024]{1,0:T(8,128)(2,1)S(1)}, bf16[256,1024]{1,0:T(8,128)(2,1)S(1)}, u32[]{:S(2)}, u32[]{:S(2)}) collective-permute-start(bf16[256,1024]{1,0:T(8,128)(2,1)S(1)} %collective-permute-done.1.halo_ref), channel_id=1, source_target_pairs={{0,1},{1,0},{2,3},{3,2},{4,5},{5,4},{6,7},{7,6},{8,9},{9,8},{10,11... | collective-permute-start | bytes 1572872 | tf_op jit(solution)/shard_map/ppermute | solution.py:447
  22.2 14.8 %collective-permute-start.16 = (bf16[2,256,512]{2,1,0:T(8,128)(2,1)S(1)}, bf16[2,256,512]{2,1,0:T(8,128)(2,1)S(1)}, u32[]{:S(2)}, u32[]{:S(2)}) collective-permute-start(bf16[2,256,512]{2,1,0:T(8,128)(2,1)S(1)} %collective-permute-done.15.rest_1_), channel_id=1, source_target_pairs={{0,8},{8,24},{24,16},{16,0},{1,9},{9,25},{25,17},{17,1},{2,10},{10... | collective-permute-start | bytes 1572872 | tf_op jit(solution)/shard_map/ppermute | solution.py:460
  37.0 27.0 %collective-permute-start.17 = (bf16[2,256,512]{2,1,0:T(8,128)(2,1)S(1)}, bf16[2,256,512]{2,1,0:T(8,128)(2,1)S(1)}, u32[]{:S(2)}, u32[]{:S(2)}) collective-permute-start(bf16[2,256,512]{2,1,0:T(8,128)(2,1)S(1)} %collective-permute-done.16.rest_2_), channel_id=1, source_target_pairs={{0,8},{8,24},{24,16},{16,0},{1,9},{9,25},{25,17},{17,1},{2,10},{10... | collective-permute-start | bytes 1572872 | tf_op jit(solution)/shard_map/ppermute | solution.py:460
  38.7 6.8 %collective-permute-start.5 = (bf16[528,128]{1,0:T(8,128)(2,1)S(1)}, bf16[528,128]{1,0:T(8,128)(2,1)S(1)}, u32[]{:S(2)}, u32[]{:S(2)}) collective-permute-start(bf16[528,128]{1,0:T(8,128)(2,1)S(1)} %get-tuple-element.71), channel_id=1, source_target_pairs={{0,6},{1,7},{2,4},{3,5},{4,2},{5,3},{6,0},{7,1},{8,14},{9,15},{10,... | collective-permute-start | bytes 405512 | tf_op jit(solution)/shard_map/ppermute | solution.py:448
  40.9 6.0 %collective-permute-start.4 = (bf16[528,128]{1,0:T(8,128)(2,1)S(1)}, bf16[528,128]{1,0:T(8,128)(2,1)S(1)}, u32[]{:S(2)}, u32[]{:S(2)}) collective-permute-start(bf16[528,128]{1,0:T(8,128)(2,1)S(1)} %get-tuple-element.69), channel_id=1, source_target_pairs={{0,4},{1,5},{2,6},{3,7},{4,0},{5,1},{6,2},{7,3},{8,12},{9,13},{10,... | collective-permute-start | bytes 405512 | tf_op jit(solution)/shard_map/ppermute | solution.py:448
  41.6 8.0 %collective-permute-start.3 = (bf16[528,128]{1,0:T(8,128)(2,1)S(1)}, bf16[528,128]{1,0:T(8,128)(2,1)S(1)}, u32[]{:S(2)}, u32[]{:S(2)}) collective-permute-start(bf16[528,128]{1,0:T(8,128)(2,1)S(1)} %get-tuple-element.67), channel_id=1, source_target_pairs={{0,2},{1,3},{2,0},{3,1},{4,6},{5,7},{6,4},{7,5},{8,10},{9,11},{10,... | collective-permute-start | bytes 405512 | tf_op jit(solution)/shard_map/ppermute | solution.py:448
  42.3 21.9 %collective-permute-start.22 = (bf16[2,256,512]{2,1,0:T(8,128)(2,1)S(1)}, bf16[2,256,512]{2,1,0:T(8,128)(2,1)S(1)}, u32[]{:S(2)}, u32[]{:S(2)}) collective-permute-start(bf16[2,256,512]{2,1,0:T(8,128)(2,1)S(1)} %pad_maximum_fusion.rest_0_), channel_id=1, source_target_pairs={{0,4},{1,3},{2,6},{3,1},{4,0},{5,7},{6,2},{7,5},{8,12},{9,11},{10,... | collective-permute-start | bytes 1572872 | tf_op jit(solution)/shard_map/ppermute | solution.py:449
  50.4 7.0 %collective-permute-start.8 = (bf16[512,128]{1,0:T(8,128)(2,1)S(1)}, bf16[512,128]{1,0:T(8,128)(2,1)S(1)}, u32[]{:S(2)}, u32[]{:S(2)}) collective-permute-start(bf16[512,128]{1,0:T(8,128)(2,1)S(1)} %shard_map.67.rest_0_), channel_id=1, source_target_pairs={{0,6},{1,7},{2,4},{3,5},{4,2},{5,3},{6,0},{7,1},{8,14},{9,15},{10,... | collective-permute-start | bytes 393224 | tf_op jit(solution)/shard_map/ppermute | solution.py:448
  51.0 7.1 %collective-permute-start.7 = (bf16[512,128]{1,0:T(8,128)(2,1)S(1)}, bf16[512,128]{1,0:T(8,128)(2,1)S(1)}, u32[]{:S(2)}, u32[]{:S(2)}) collective-permute-start(bf16[512,128]{1,0:T(8,128)(2,1)S(1)} %shard_map.67.rest_0_), channel_id=1, source_target_pairs={{0,4},{1,5},{2,6},{3,7},{4,0},{5,1},{6,2},{7,3},{8,12},{9,13},{10,... | collective-permute-start | bytes 393224 | tf_op jit(solution)/shard_map/ppermute | solution.py:448
  52.5 6.4 %collective-permute-start.6 = (bf16[512,128]{1,0:T(8,128)(2,1)S(1)}, bf16[512,128]{1,0:T(8,128)(2,1)S(1)}, u32[]{:S(2)}, u32[]{:S(2)}) collective-permute-start(bf16[512,128]{1,0:T(8,128)(2,1)S(1)} %shard_map.67.rest_0_), channel_id=1, source_target_pairs={{0,2},{1,3},{2,0},{3,1},{4,6},{5,7},{6,4},{7,5},{8,10},{9,11},{10,... | collective-permute-start | bytes 393224 | tf_op jit(solution)/shard_map/ppermute | solution.py:448
  57.4 9.3 %collective-permute-start.23 = (bf16[2,256,512]{2,1,0:T(8,128)(2,1)S(1)}, bf16[2,256,512]{2,1,0:T(8,128)(2,1)S(1)}, u32[]{:S(2)}, u32[]{:S(2)}) collective-permute-start(bf16[2,256,512]{2,1,0:T(8,128)(2,1)S(1)} %collective-permute-done.15.rest_1_), channel_id=1, source_target_pairs={{0,4},{1,3},{2,6},{3,1},{4,0},{5,7},{6,2},{7,5},{8,12},{9,11},{10,... | collective-permute-start | bytes 1572872 | tf_op jit(solution)/shard_map/ppermute | solution.py:449
  61.0 6.7 %collective-permute-start.18 = (bf16[2,256,512]{2,1,0:T(8,128)(2,1)S(1)}, bf16[2,256,512]{2,1,0:T(8,128)(2,1)S(1)}, u32[]{:S(2)}, u32[]{:S(2)}) collective-permute-start(bf16[2,256,512]{2,1,0:T(8,128)(2,1)S(1)} %pad_maximum_fusion.rest_0_), channel_id=1, source_target_pairs={{0,1},{1,0},{2,3},{3,2},{4,5},{5,4},{6,7},{7,6},{8,9},{9,8},{10,11... | collective-permute-start | bytes 1572872 | tf_op jit(solution)/shard_map/ppermute | solution.py:447
  64.3 4.5 %collective-permute-start.19 = (bf16[2,256,512]{2,1,0:T(8,128)(2,1)S(1)}, bf16[2,256,512]{2,1,0:T(8,128)(2,1)S(1)}, u32[]{:S(2)}, u32[]{:S(2)}) collective-permute-start(bf16[2,256,512]{2,1,0:T(8,128)(2,1)S(1)} %collective-permute-done.15.rest_1_), channel_id=1, source_target_pairs={{0,1},{1,0},{2,3},{3,2},{4,5},{5,4},{6,7},{7,6},{8,9},{9,8},{10,11... | collective-permute-start | bytes 1572872 | tf_op jit(solution)/shard_map/ppermute | solution.py:447
  65.1 3.6 %collective-permute-start.20 = (bf16[2,256,512]{2,1,0:T(8,128)(2,1)S(1)}, bf16[2,256,512]{2,1,0:T(8,128)(2,1)S(1)}, u32[]{:S(2)}, u32[]{:S(2)}) collective-permute-start(bf16[2,256,512]{2,1,0:T(8,128)(2,1)S(1)} %collective-permute-done.16.rest_2_), channel_id=1, source_target_pairs={{0,1},{1,0},{2,3},{3,2},{4,5},{5,4},{6,7},{7,6},{8,9},{9,8},{10,11... | collective-permute-start | bytes 1572872 | tf_op jit(solution)/shard_map/ppermute | solution.py:447
  65.4 4.8 %collective-permute-start.21 = (bf16[2,256,512]{2,1,0:T(8,128)(2,1)S(1)}, bf16[2,256,512]{2,1,0:T(8,128)(2,1)S(1)}, u32[]{:S(2)}, u32[]{:S(2)}) collective-permute-start(bf16[2,256,512]{2,1,0:T(8,128)(2,1)S(1)} %collective-permute-done.17.rest_3_), channel_id=1, source_target_pairs={{0,1},{1,0},{2,3},{3,2},{4,5},{5,4},{6,7},{7,6},{8,9},{9,8},{10,11... | collective-permute-start | bytes 1572872 | tf_op jit(solution)/shard_map/ppermute | solution.py:447
  66.6 12.1 %collective-permute-start.24 = (bf16[2,256,512]{2,1,0:T(8,128)(2,1)S(1)}, bf16[2,256,512]{2,1,0:T(8,128)(2,1)S(1)}, u32[]{:S(2)}, u32[]{:S(2)}) collective-permute-start(bf16[2,256,512]{2,1,0:T(8,128)(2,1)S(1)} %collective-permute-done.16.rest_2_), channel_id=1, source_target_pairs={{0,4},{1,3},{2,6},{3,1},{4,0},{5,7},{6,2},{7,5},{8,12},{9,11},{10,... | collective-permute-start | bytes 1572872 | tf_op jit(solution)/shard_map/ppermute | solution.py:449
  67.7 16.6 %collective-permute-start.25 = (bf16[2,256,512]{2,1,0:T(8,128)(2,1)S(1)}, bf16[2,256,512]{2,1,0:T(8,128)(2,1)S(1)}, u32[]{:S(2)}, u32[]{:S(2)}) collective-permute-start(bf16[2,256,512]{2,1,0:T(8,128)(2,1)S(1)} %collective-permute-done.17.rest_3_), channel_id=1, source_target_pairs={{0,4},{1,3},{2,6},{3,1},{4,0},{5,7},{6,2},{7,5},{8,12},{9,11},{10,... | collective-permute-start | bytes 1572872 | tf_op jit(solution)/shard_map/ppermute | solution.py:449
  68.7 23.3 %collective-permute-start.26 = (bf16[2,256,512]{2,1,0:T(8,128)(2,1)S(1)}, bf16[2,256,512]{2,1,0:T(8,128)(2,1)S(1)}, u32[]{:S(2)}, u32[]{:S(2)}) collective-permute-start(bf16[2,256,512]{2,1,0:T(8,128)(2,1)S(1)} %collective-permute-done.22.rest_4_.rest_0_), channel_id=1, source_target_pairs={{0,1},{1,0},{2,3},{3,2},{4,5},{5,4},{6,7},{7,6},{8,9},{9,8},{10,11... | collective-permute-start | bytes 1572872 | tf_op jit(solution)/shard_map/ppermute | solution.py:447
  68.7 15.6 %collective-permute-start.14 = (bf16[128,1024]{1,0:T(8,128)(2,1)S(1)}, bf16[128,1024]{1,0:T(8,128)(2,1)S(1)}, u32[]{:S(2)}, u32[]{:S(2)}) collective-permute-start(bf16[128,1024]{1,0:T(8,128)(2,1)S(1)} %get-tuple-element.83), channel_id=1, source_target_pairs={{0,2},{1,5},{2,0},{3,7},{4,6},{5,1},{6,4},{7,3},{8,10},{9,13},{10,... | collective-permute-start | bytes 786440 | tf_op jit(solution)/shard_map/ppermute | solution.py:449
  70.2 24.0 %collective-permute-start.27 = (bf16[2,256,512]{2,1,0:T(8,128)(2,1)S(1)}, bf16[2,256,512]{2,1,0:T(8,128)(2,1)S(1)}, u32[]{:S(2)}, u32[]{:S(2)}) collective-permute-start(bf16[2,256,512]{2,1,0:T(8,128)(2,1)S(1)} %collective-permute-done.23.rest_5_.rest_1_), channel_id=1, source_target_pairs={{0,1},{1,0},{2,3},{3,2},{4,5},{5,4},{6,7},{7,6},{8,9},{9,8},{10,11... | collective-permute-start | bytes 1572872 | tf_op jit(solution)/shard_map/ppermute | solution.py:447
  78.7 15.5 %collective-permute-start.28 = (bf16[2,256,512]{2,1,0:T(8,128)(2,1)S(1)}, bf16[2,256,512]{2,1,0:T(8,128)(2,1)S(1)}, u32[]{:S(2)}, u32[]{:S(2)}) collective-permute-start(bf16[2,256,512]{2,1,0:T(8,128)(2,1)S(1)} %collective-permute-done.24.rest_6_.rest_2_), channel_id=1, source_target_pairs={{0,1},{1,0},{2,3},{3,2},{4,5},{5,4},{6,7},{7,6},{8,9},{9,8},{10,11... | collective-permute-start | bytes 1572872 | tf_op jit(solution)/shard_map/ppermute | solution.py:447
  84.3 9.9 %collective-permute-start.29 = (bf16[2,256,512]{2,1,0:T(8,128)(2,1)S(1)}, bf16[2,256,512]{2,1,0:T(8,128)(2,1)S(1)}, u32[]{:S(2)}, u32[]{:S(2)}) collective-permute-start(bf16[2,256,512]{2,1,0:T(8,128)(2,1)S(1)} %collective-permute-done.25.rest_7_.rest_3_), channel_id=1, source_target_pairs={{0,1},{1,0},{2,3},{3,2},{4,5},{5,4},{6,7},{7,6},{8,9},{9,8},{10,11... | collective-permute-start | bytes 1572872 | tf_op jit(solution)/shard_map/ppermute | solution.py:447
  84.3 6.4 %collective-permute-start.13 = (bf16[128,1024]{1,0:T(8,128)(2,1)S(1)}, bf16[128,1024]{1,0:T(8,128)(2,1)S(1)}, u32[]{:S(2)}, u32[]{:S(2)}) collective-permute-start(bf16[128,1024]{1,0:T(8,128)(2,1)S(1)} %get-tuple-element.83), channel_id=1, source_target_pairs={{0,4},{1,3},{2,6},{3,1},{4,0},{5,7},{6,2},{7,5},{8,12},{9,11},{10,... | collective-permute-start | bytes 786440 | tf_op jit(solution)/shard_map/ppermute | solution.py:449
  90.7 8.6 %collective-permute-start.12 = (bf16[128,1024]{1,0:T(8,128)(2,1)S(1)}, bf16[128,1024]{1,0:T(8,128)(2,1)S(1)}, u32[]{:S(2)}, u32[]{:S(2)}) collective-permute-start(bf16[128,1024]{1,0:T(8,128)(2,1)S(1)} %get-tuple-element.82), channel_id=1, source_target_pairs={{0,2},{1,5},{2,0},{3,7},{4,6},{5,1},{6,4},{7,3},{8,10},{9,13},{10,... | collective-permute-start | bytes 786440 | tf_op jit(solution)/shard_map/ppermute | solution.py:449
  92.1 8.4 %collective-permute-start.11 = (bf16[128,1024]{1,0:T(8,128)(2,1)S(1)}, bf16[128,1024]{1,0:T(8,128)(2,1)S(1)}, u32[]{:S(2)}, u32[]{:S(2)}) collective-permute-start(bf16[128,1024]{1,0:T(8,128)(2,1)S(1)} %get-tuple-element.82), channel_id=1, source_target_pairs={{0,4},{1,3},{2,6},{3,1},{4,0},{5,7},{6,2},{7,5},{8,12},{9,11},{10,... | collective-permute-start | bytes 786440 | tf_op jit(solution)/shard_map/ppermute | solution.py:449
  101.7 9.2 %collective-permute-start.33 = (bf16[128,1024]{1,0:T(8,128)(2,1)S(1)}, bf16[128,1024]{1,0:T(8,128)(2,1)S(1)}, u32[]{:S(2)}, u32[]{:S(2)}) collective-permute-start(bf16[128,1024]{1,0:T(8,128)(2,1)S(1)} %shard_map.75), channel_id=1, source_target_pairs={{0,4},{1,3},{2,6},{3,1},{4,0},{5,7},{6,2},{7,5},{8,12},{9,11},{10,... | collective-permute-start | bytes 786440 | tf_op jit(solution)/shard_map/ppermute | solution.py:449
  102.8 8.3 %collective-permute-start.32 = (bf16[128,1024]{1,0:T(8,128)(2,1)S(1)}, bf16[128,1024]{1,0:T(8,128)(2,1)S(1)}, u32[]{:S(2)}, u32[]{:S(2)}) collective-permute-start(bf16[128,1024]{1,0:T(8,128)(2,1)S(1)} %shard_map.74), channel_id=1, source_target_pairs={{0,2},{1,5},{2,0},{3,7},{4,6},{5,1},{6,4},{7,3},{8,10},{9,13},{10,... | collective-permute-start | bytes 786440 | tf_op jit(solution)/shard_map/ppermute | solution.py:449
  104.1 9.7 %collective-permute-start.30 = (bf16[128,1024]{1,0:T(8,128)(2,1)S(1)}, bf16[128,1024]{1,0:T(8,128)(2,1)S(1)}, u32[]{:S(2)}, u32[]{:S(2)}) collective-permute-start(bf16[128,1024]{1,0:T(8,128)(2,1)S(1)} %shard_map.72), channel_id=1, source_target_pairs={{0,2},{1,5},{2,0},{3,7},{4,6},{5,1},{6,4},{7,3},{8,10},{9,13},{10,... | collective-permute-start | bytes 786440 | tf_op jit(solution)/shard_map/ppermute | solution.py:449
  104.8 10.1 %collective-permute-start.31 = (bf16[128,1024]{1,0:T(8,128)(2,1)S(1)}, bf16[128,1024]{1,0:T(8,128)(2,1)S(1)}, u32[]{:S(2)}, u32[]{:S(2)}) collective-permute-start(bf16[128,1024]{1,0:T(8,128)(2,1)S(1)} %shard_map.73), channel_id=1, source_target_pairs={{0,4},{1,3},{2,6},{3,1},{4,0},{5,7},{6,2},{7,5},{8,12},{9,11},{10,... | collective-permute-start | bytes 786440 | tf_op jit(solution)/shard_map/ppermute | solution.py:449
  (4 other events, 12.0 us)
